TPU v7x, 32 devices: a whole 2x2x4 slice. The times are simulated.
32 devices in a mesh: rep: 4 (over y, core), fsdp: 4 (over z), seq: 2 (over x).
Axes of the slice: x: 2, y: 2, z: 4, core: 2. Of those that a mesh axis runs over, the one named last changes fastest.
Arguments:
- tokens: bfloat16 [12288, 768], P(('rep', 'fsdp', 'seq')), may hold values from -6 to 6
- piece_starts: int32 [16, 2], P(('rep', 'fsdp')), may hold values from 0 to 512, as said below
- routes: int32 [12288, 2], P(('rep', 'fsdp', 'seq')), may hold values from 0 to 3, all different within a row; in each aligned block of 384 rows (0 to 383, 384 to 767, ...) at most 288 rows name the same one
- buckets: int32 [1535], replicated, may hold values from 0 to 31
- attn_q: bfloat16 [768, 768], P(('fsdp', 'seq')), may hold values from -0.21875 to 0.21875
- attn_k: bfloat16 [768, 768], P(('fsdp', 'seq')), may hold values from -0.21875 to 0.21875
- attn_v: bfloat16 [768, 768], P(('fsdp', 'seq')), may hold values from -0.21875 to 0.21875
- attn_o: bfloat16 [768, 768], P(('fsdp', 'seq')), may hold values from -0.875 to 0.875
- expert_in: bfloat16 [4, 768, 3072], P(None, ('fsdp', 'seq')), may hold values from -0.21875 to 0.21875
- expert_out: bfloat16 [4, 3072, 768], P(None, ('fsdp', 'seq')), may hold values from -0.109375 to 0.109375
- gain_attn: float32 [768], replicated, may hold values from 0.5 to 1.5
- gain_ffn: float32 [768], replicated, may hold values from 0.5 to 1.5
- rel_table: float32 [32, 12], replicated, may hold values from -4 to 4
- router: float32 [768, 4], replicated, may hold values from -0.15 to 0.15
- cotangent: bfloat16 [12288, 768], P(('rep', 'fsdp', 'seq')), may hold values from -6 to 6
Outputs:
- out_rows: bfloat16 [12288, 768], P(('rep', 'fsdp', 'seq'))
- tokens_grad: bfloat16 [12288, 768], P(('rep', 'fsdp', 'seq'))
- attn_q_grad: float32 [768, 768], P(('fsdp', 'seq'))
- attn_k_grad: float32 [768, 768], P(('fsdp', 'seq'))
- attn_v_grad: float32 [768, 768], P(('fsdp', 'seq'))
- attn_o_grad: float32 [768, 768], P(('fsdp', 'seq'))
- expert_in_grad: float32 [4, 768, 3072], P(None, ('fsdp', 'seq'))
- expert_out_grad: float32 [4, 3072, 768], P(None, ('fsdp', 'seq'))
- gain_attn_grad: float32 [768], replicated
- gain_ffn_grad: float32 [768], replicated
- rel_table_grad: float32 [32, 12], replicated
- router_grad: float32 [768, 4], replicated
Inputs may be any that keep to these rules, and one draw needn't show every extreme that they name: `routes`: A token's two experts differ. In the rows of one device (aligned blocks of 384 tokens) no expert is named more than 288 times, a bound that some block reaches. `piece_starts`: each sequence has two picture pieces of 256 positions inside it; the first ends at or before position 256 and the second starts at or after it.
All inputs are finite; a program needn't handle non-finite values.
Results may differ from a plain program's by a relative error of at most 0.018.
Values may be sent and summed in bfloat16 or wider, within the bound.
A program may use at most 256 MiB of HBM per device.

v0:
```python
import jax
import jax.numpy as jnp
from jax import lax
from jax.sharding import PartitionSpec as P

PIECE = 256
CAP = 288


epsilon = 1e-06
masked_out = -1e30
highest = lax.Precision.HIGHEST


def mat_mul(a_mat, b_mat):
    return jnp.dot(a_mat, b_mat, precision=highest)


def norm_rows(values, gain_vec):
    return values * lax.rsqrt(jnp.mean(values * values, -1, keepdims=True) + epsilon) * gain_vec


def piece_labels(positions, starts):
    inside = (positions[:, None] >= starts[None, :]) & (
        positions[:, None] < starts[None, :] + PIECE
    )
    return jnp.where(jnp.any(inside, 1), jnp.sum(jnp.where(inside, starts[None, :], 0), 1), -1)


def gate_values(logits, route_ids):
    soft_probs = jax.nn.softmax(logits, -1)
    chosen = jnp.take_along_axis(soft_probs, route_ids, 1)
    return chosen / jnp.sum(chosen, 1, keepdims=True)


def slot_index(route_ids, n_experts, capacity):
    flat_routes = route_ids.reshape(-1)
    expert_hot = (flat_routes[:, None] == jnp.arange(n_experts)[None, :]).astype(jnp.int32)
    before = jnp.cumsum(expert_hot, 0) - expert_hot
    return flat_routes * capacity + jnp.sum(before * expert_hot, 1)


def per_device(
    tokens,
    piece_starts,
    routes,
    buckets,
    attn_q,
    attn_k,
    attn_v,
    attn_o,
    expert_in,
    expert_out,
    gain_attn,
    gain_ffn,
    rel_table,
    router,
    cotangent,
):
    n_rows = tokens.shape[0]
    model_width = tokens.shape[1]
    n_heads = rel_table.shape[1]
    n_buckets = rel_table.shape[0]
    head_dim = model_width // n_heads
    n_experts = expert_in.shape[0]
    capacity = CAP
    length = n_rows * lax.axis_size("seq")
    starts = piece_starts[0]
    x_rows = tokens.astype(jnp.float32)
    w_query, w_key, w_value, w_output = (
        lax.all_gather(attn_q, ("fsdp", "seq"), axis=0, tiled=True),
        lax.all_gather(attn_k, ("fsdp", "seq"), axis=0, tiled=True),
        lax.all_gather(attn_v, ("fsdp", "seq"), axis=0, tiled=True),
        lax.all_gather(attn_o, ("fsdp", "seq"), axis=0, tiled=True),
    )
    h_one = norm_rows(x_rows, gain_attn).astype(jnp.bfloat16)
    q_rows = jnp.dot(h_one, w_query, preferred_element_type=jnp.float32).astype(jnp.bfloat16)
    k_rows = jnp.dot(h_one, w_key, preferred_element_type=jnp.float32).astype(jnp.bfloat16)
    v_rows = jnp.dot(h_one, w_value, preferred_element_type=jnp.float32).astype(jnp.bfloat16)
    k_all, v_all = (
        lax.all_gather(k_rows, "seq", axis=0, tiled=True),
        lax.all_gather(v_rows, "seq", axis=0, tiled=True),
    )
    keys_h = k_all.reshape(length, n_heads, head_dim)
    values_h = v_all.reshape(length, n_heads, head_dim)
    bucket_range = jnp.arange(n_buckets, dtype=jnp.int32)
    pos_k = jnp.arange(length, dtype=jnp.int32)
    labels_k = piece_labels(pos_k, starts)
    pos_q = lax.axis_index("seq") * n_rows + jnp.arange(n_rows, dtype=jnp.int32)
    n_blocks = n_rows // n_rows
    q_blocks = q_rows.reshape(n_blocks, n_rows, n_heads, head_dim)
    pos_blocks = pos_q.reshape(n_blocks, n_rows)

    def block_scores(q_blk, pos_blk):
        offset = pos_k[None, :] - pos_blk[:, None] + (length - 1)
        bucket_ids = buckets[offset]
        bucket_match = (bucket_ids[None, :, :] == bucket_range[:, None, None]).astype(jnp.float32)
        bias_blk = jnp.einsum("nqk,nh->hqk", bucket_match, rel_table, precision=highest)
        raw_scores = (
            jnp.einsum("qhd,khd->hqk", q_blk, keys_h, preferred_element_type=jnp.float32) * 0.125
            + bias_blk
        )
        labels_q = piece_labels(pos_blk, starts)
        allowed = (pos_k[None, :] <= pos_blk[:, None]) | (
            labels_q[:, None] == labels_k[None, :]
        ) & (labels_q[:, None] >= 0)
        return (jnp.where(allowed[None], raw_scores, masked_out), bucket_match)

    def forward_block(pieces):
        scores, bucket_match = block_scores(pieces[0], pieces[1])
        row_top = jnp.max(scores, -1, keepdims=True)
        exp_scores = jnp.exp(scores - row_top)
        row_total = jnp.sum(exp_scores, -1, keepdims=True)
        soft_probs = exp_scores / row_total
        att_blk = jnp.einsum(
            "hqk,khd->qhd",
            soft_probs.astype(jnp.bfloat16),
            values_h,
            preferred_element_type=jnp.float32,
        )
        return (att_blk.astype(jnp.bfloat16), row_top[..., 0] + jnp.log(row_total[..., 0]))

    att_blocks, lse_blocks = lax.map(forward_block, (q_blocks, pos_blocks))
    att_rows = att_blocks.reshape(n_rows, model_width)
    x_mid = x_rows + jnp.dot(att_rows, w_output, preferred_element_type=jnp.float32)
    h_two = norm_rows(x_mid, gain_ffn).astype(jnp.bfloat16)
    h_float = h_two.astype(jnp.float32)
    logits = mat_mul(h_float, router)
    gate_vals = gate_values(logits, routes)
    slot_flat = slot_index(routes, n_experts, capacity)
    dispatch = (
        jnp.zeros((n_experts * capacity, model_width), jnp.bfloat16)
        .at[slot_flat]
        .set(jnp.repeat(h_two, 2, axis=0))
    )
    dispatch = dispatch.reshape(n_experts, capacity, model_width)
    w_in, w_out = (
        lax.all_gather(expert_in, ("fsdp", "seq"), axis=1, tiled=True),
        lax.all_gather(expert_out, ("fsdp", "seq"), axis=1, tiled=True),
    )
    up_vals = jnp.einsum("ecd,edf->ecf", dispatch, w_in, preferred_element_type=jnp.float32)
    act_low = jax.nn.gelu(up_vals, approximate=True).astype(jnp.bfloat16)
    y_flat = jnp.einsum("ecf,efd->ecd", act_low, w_out, preferred_element_type=jnp.float32).astype(
        jnp.bfloat16
    )
    y_flat = y_flat.reshape(n_experts * capacity, model_width)
    picked = y_flat[slot_flat].reshape(n_rows, 2, model_width).astype(jnp.float32)
    out_rows = (x_mid + jnp.sum(gate_vals[:, :, None] * picked, 1)).astype(jnp.bfloat16)
    grad_out = cotangent.astype(jnp.float32)
    w_query_b, w_key_b, w_value_b, w_output_b = (
        lax.all_gather(attn_q, ("fsdp", "seq"), axis=0, tiled=True),
        lax.all_gather(attn_k, ("fsdp", "seq"), axis=0, tiled=True),
        lax.all_gather(attn_v, ("fsdp", "seq"), axis=0, tiled=True),
        lax.all_gather(attn_o, ("fsdp", "seq"), axis=0, tiled=True),
    )
    w_in_b, w_out_b = (
        lax.all_gather(expert_in, ("fsdp", "seq"), axis=1, tiled=True),
        lax.all_gather(expert_out, ("fsdp", "seq"), axis=1, tiled=True),
    )
    grad_gates = jnp.sum(grad_out[:, None, :] * picked, -1)
    grad_y = (
        jnp.zeros((n_experts * capacity, model_width), jnp.float32)
        .at[slot_flat]
        .set((gate_vals[:, :, None] * grad_out[:, None, :]).reshape(2 * n_rows, model_width))
    )
    grad_y = grad_y.astype(jnp.bfloat16).reshape(n_experts, capacity, model_width)
    grad_act = jnp.einsum("ecd,efd->ecf", grad_y, w_out_b, preferred_element_type=jnp.float32)
    gelu_out, gelu_pull = jax.vjp(lambda inputs: jax.nn.gelu(inputs, approximate=True), up_vals)
    grad_up = gelu_pull(grad_act)[0].astype(jnp.bfloat16)
    grad_w_out = jnp.einsum("ecf,ecd->efd", act_low, grad_y, preferred_element_type=jnp.float32)
    grad_w_in = jnp.einsum("ecd,ecf->edf", dispatch, grad_up, preferred_element_type=jnp.float32)
    grad_disp = jnp.einsum("ecf,edf->ecd", grad_up, w_in_b, preferred_element_type=jnp.float32)
    grad_disp = grad_disp.reshape(n_experts * capacity, model_width)
    gate_out, gate_pull = jax.vjp(lambda inputs: gate_values(inputs, routes), logits)
    grad_logits = gate_pull(grad_gates)[0]
    grad_router = mat_mul(h_float.T, grad_logits)
    grad_h_two = jnp.sum(grad_disp[slot_flat].reshape(n_rows, 2, model_width), 1) + mat_mul(
        grad_logits, router.T
    )
    norm_two, norm_pull_two = jax.vjp(norm_rows, x_mid, gain_ffn)
    grad_mid, grad_gain_ffn = norm_pull_two(grad_h_two)
    grad_mid = grad_mid + grad_out
    grad_branch = grad_mid.astype(jnp.bfloat16)
    grad_w_output = jnp.dot(att_rows.T, grad_branch, preferred_element_type=jnp.float32)
    grad_att = jnp.dot(grad_branch, w_output_b.T, preferred_element_type=jnp.float32).astype(
        jnp.bfloat16
    )
    grad_att_blocks = grad_att.reshape(n_blocks, n_rows, n_heads, head_dim)

    def backward_block(sums, pieces):
        grad_keys, grad_values, grad_bias = sums
        q_blk, pos_blk, lse_blk, grad_blk = pieces
        scores, bucket_match = block_scores(q_blk, pos_blk)
        soft_probs = jnp.exp(scores - lse_blk[:, :, None])
        grad_probs = jnp.einsum(
            "qhd,khd->hqk", grad_blk, values_h, preferred_element_type=jnp.float32
        )
        grad_scores = soft_probs * (
            grad_probs - jnp.sum(soft_probs * grad_probs, -1, keepdims=True)
        )
        grad_scores = grad_scores.astype(jnp.bfloat16)
        grad_q = (
            jnp.einsum("hqk,khd->qhd", grad_scores, keys_h, preferred_element_type=jnp.float32)
            * 0.125
        )
        grad_keys = (
            grad_keys
            + jnp.einsum("hqk,qhd->khd", grad_scores, q_blk, preferred_element_type=jnp.float32)
            * 0.125
        )
        grad_values = grad_values + jnp.einsum(
            "hqk,qhd->khd",
            soft_probs.astype(jnp.bfloat16),
            grad_blk,
            preferred_element_type=jnp.float32,
        )
        grad_bias = grad_bias + jnp.einsum(
            "hqk,nqk->nh",
            grad_scores,
            bucket_match.astype(jnp.bfloat16),
            preferred_element_type=jnp.float32,
        )
        return ((grad_keys, grad_values, grad_bias), grad_q)

    zero_keys = jnp.zeros((length, n_heads, head_dim), jnp.float32)
    start_sums = (zero_keys, zero_keys, jnp.zeros((n_buckets, n_heads), jnp.float32))
    end_sums, grad_q_blocks = lax.scan(
        backward_block, start_sums, (q_blocks, pos_blocks, lse_blocks, grad_att_blocks)
    )
    grad_keys, grad_values, grad_table = end_sums
    grad_k_rows, grad_v_rows = (
        lax.psum_scatter(
            grad_keys.reshape(length, model_width).astype(jnp.bfloat16),
            "seq",
            scatter_dimension=0,
            tiled=True,
        ).astype(jnp.float32),
        lax.psum_scatter(
            grad_values.reshape(length, model_width).astype(jnp.bfloat16),
            "seq",
            scatter_dimension=0,
            tiled=True,
        ).astype(jnp.float32),
    )
    grad_q_low = grad_q_blocks.reshape(n_rows, model_width).astype(jnp.bfloat16)
    grad_k_low = grad_k_rows.astype(jnp.bfloat16)
    grad_v_low = grad_v_rows.astype(jnp.bfloat16)
    grad_w_query = jnp.dot(h_one.T, grad_q_low, preferred_element_type=jnp.float32)
    grad_w_key = jnp.dot(h_one.T, grad_k_low, preferred_element_type=jnp.float32)
    grad_w_value = jnp.dot(h_one.T, grad_v_low, preferred_element_type=jnp.float32)
    grad_h_one = jnp.dot(grad_q_low, w_query_b.T, preferred_element_type=jnp.float32)
    grad_h_one = grad_h_one + jnp.dot(grad_k_low, w_key_b.T, preferred_element_type=jnp.float32)
    grad_h_one = grad_h_one + jnp.dot(grad_v_low, w_value_b.T, preferred_element_type=jnp.float32)
    norm_one, norm_pull_one = jax.vjp(norm_rows, x_rows, gain_attn)
    grad_x_part, grad_gain_attn = norm_pull_one(grad_h_one)
    grad_tokens = (grad_mid + grad_x_part).astype(jnp.bfloat16)
    sum_gain_attn, sum_gain_ffn, sum_table, sum_router = lax.psum(
        (grad_gain_attn, grad_gain_ffn, grad_table, grad_router), ("rep", "fsdp", "seq")
    )
    own_q, own_k, own_v, own_o, own_in, own_out = (
        lax.psum_scatter(grad_w_query, ("fsdp", "seq"), scatter_dimension=0, tiled=True),
        lax.psum_scatter(grad_w_key, ("fsdp", "seq"), scatter_dimension=0, tiled=True),
        lax.psum_scatter(grad_w_value, ("fsdp", "seq"), scatter_dimension=0, tiled=True),
        lax.psum_scatter(grad_w_output, ("fsdp", "seq"), scatter_dimension=0, tiled=True),
        lax.psum_scatter(grad_w_in, ("fsdp", "seq"), scatter_dimension=1, tiled=True),
        lax.psum_scatter(grad_w_out, ("fsdp", "seq"), scatter_dimension=1, tiled=True),
    )
    piece_q, piece_k, piece_v, piece_o, piece_in, piece_out = (
        lax.psum_scatter(
            own_q.reshape(-1).astype(jnp.bfloat16), "rep", scatter_dimension=0, tiled=True
        ).astype(jnp.float32),
        lax.psum_scatter(
            own_k.reshape(-1).astype(jnp.bfloat16), "rep", scatter_dimension=0, tiled=True
        ).astype(jnp.float32),
        lax.psum_scatter(
            own_v.reshape(-1).astype(jnp.bfloat16), "rep", scatter_dimension=0, tiled=True
        ).astype(jnp.float32),
        lax.psum_scatter(
            own_o.reshape(-1).astype(jnp.bfloat16), "rep", scatter_dimension=0, tiled=True
        ).astype(jnp.float32),
        lax.psum_scatter(
            own_in.reshape(-1).astype(jnp.bfloat16), "rep", scatter_dimension=0, tiled=True
        ).astype(jnp.float32),
        lax.psum_scatter(
            own_out.reshape(-1).astype(jnp.bfloat16), "rep", scatter_dimension=0, tiled=True
        ).astype(jnp.float32),
    )
    flat_q, flat_k, flat_v, flat_o, flat_in, flat_out = (
        lax.all_gather(piece_q.astype(jnp.bfloat16), "rep", axis=0, tiled=True).astype(
            piece_q.dtype
        ),
        lax.all_gather(piece_k.astype(jnp.bfloat16), "rep", axis=0, tiled=True).astype(
            piece_k.dtype
        ),
        lax.all_gather(piece_v.astype(jnp.bfloat16), "rep", axis=0, tiled=True).astype(
            piece_v.dtype
        ),
        lax.all_gather(piece_o.astype(jnp.bfloat16), "rep", axis=0, tiled=True).astype(
            piece_o.dtype
        ),
        lax.all_gather(piece_in.astype(jnp.bfloat16), "rep", axis=0, tiled=True).astype(
            piece_in.dtype
        ),
        lax.all_gather(piece_out.astype(jnp.bfloat16), "rep", axis=0, tiled=True).astype(
            piece_out.dtype
        ),
    )
    sum_q = flat_q.reshape(attn_q.shape)
    sum_k = flat_k.reshape(attn_k.shape)
    sum_v = flat_v.reshape(attn_v.shape)
    sum_o = flat_o.reshape(attn_o.shape)
    sum_in = flat_in.reshape(expert_in.shape)
    sum_out = flat_out.reshape(expert_out.shape)
    return (
        out_rows,
        grad_tokens,
        sum_q,
        sum_k,
        sum_v,
        sum_o,
        sum_in,
        sum_out,
        sum_gain_attn,
        sum_gain_ffn,
        sum_table,
        sum_router,
    )


def solution(mesh):
    in_specs = (
        P(("rep", "fsdp", "seq"), None),
        P(("rep", "fsdp"), None),
        P(("rep", "fsdp", "seq"), None),
        P(),
        P(("fsdp", "seq"), None),
        P(("fsdp", "seq"), None),
        P(("fsdp", "seq"), None),
        P(("fsdp", "seq"), None),
        P(None, ("fsdp", "seq"), None),
        P(None, ("fsdp", "seq"), None),
        P(),
        P(),
        P(),
        P(),
        P(("rep", "fsdp", "seq"), None),
    )
    out_specs = (
        P(("rep", "fsdp", "seq"), None),
        P(("rep", "fsdp", "seq"), None),
        P(("fsdp", "seq"), None),
        P(("fsdp", "seq"), None),
        P(("fsdp", "seq"), None),
        P(("fsdp", "seq"), None),
        P(None, ("fsdp", "seq"), None),
        P(None, ("fsdp", "seq"), None),
        P(),
        P(),
        P(),
        P(),
    )
    return jax.shard_map(
        per_device, mesh=mesh, in_specs=in_specs, out_specs=out_specs, check_vma=False
    )
```

profile of v0, /device:TPU:0, one launch (start us, length us, event | category | flops | bytes accessed | tf_op | source)
XLA Modules:
  0.0 3771.2 jit_solution(5801377877686230623)
XLA Ops:
  11.3 42.7 %all-gather.17.cloned.1.call-done = bf16[768,768]{1,0:T(8,128)(2,1)} async-done(((bf16[96,768]{1,0:T(8,128)(2,1)}), bf16[768,768]{1,0:T(8,128)(2,1)}) %all-gather.17.cloned.1.call-update) | async-done | bytes 1179664 | tf_op jit(solution)/shard_map/all_gather | solution.py:72
  57.0 39.0 %all-gather.11.cloned.1.call-done = bf16[768,768]{1,0:T(8,128)(2,1)} async-done(((bf16[96,768]{1,0:T(8,128)(2,1)}), bf16[768,768]{1,0:T(8,128)(2,1)}) %all-gather.11.cloned.1.call-update) | async-done | bytes 1179664 | tf_op jit(solution)/shard_map/all_gather | solution.py:73
  104.3 1630.7 %gather_fusion = s32[294912]{0:T(1024)S(1)} fusion(s32[1535]{0:T(1024)S(1)} %copy-done.1, s32[294912]{0:T(1024)S(1)} %broadcast_clamp_fusion), kind=kCustom, calls=%fused_computation | custom fusion | bytes 3538944 | tf_op jit(solution)/shard_map/while/body/eval_jaxpr/gather | solution.py:96
  1737.9 14.4 fusion
  1752.4 17.4 copy.105
  1785.9 7.0 fusion.67
  1806.7 6.8 gather_fusion.3
  1814.8 11.3 scatter_custom_fusion.1
  1830.2 7.0 scatter_custom_fusion
  1840.4 12.5 fusion.69
  1852.9 26.9 fusion.10
  1879.8 15.6 convolution_convert_fusion
  1901.8 6.9 multiply_reduce_fusion.1
  1909.3 36.3 scatter_fusion
  1945.6 13.2 fusion.70
  1977.0 10.2 multiply_reduce_fusion
  1987.3 7.1 fusion.21
  1995.9 10.6 multiply_convert_fusion
  2026.6 14.4 reduce-scatter.25.cloned.1.call-done
  2044.5 21.8 fusion.65
  2066.4 20.7 fusion.72
  2087.3 26.4 reduce-scatter.19.cloned.1.call-done
  2115.4 70.2 %reduce-scatter.13.cloned.1.call-done = f32[96,768]{1,0:T(8,128)} async-done(((f32[768,768]{1,0:T(8,128)}), f32[96,768]{1,0:T(8,128)}) %reduce-scatter.13.cloned.1.call-update) | async-done | bytes 294928 | tf_op jit(solution)/shard_map/reduce_scatter | solution.py:261
  2187.3 69.8 %reduce-scatter.17.cloned.1.call-done = f32[96,768]{1,0:T(8,128)} async-done(((f32[768,768]{1,0:T(8,128)}), f32[96,768]{1,0:T(8,128)}) %reduce-scatter.17.cloned.1.call-update) | async-done | bytes 294928 | tf_op jit(solution)/shard_map/reduce_scatter | solution.py:263
  2258.9 70.2 %reduce-scatter.15.cloned.1.call-done = f32[96,768]{1,0:T(8,128)} async-done(((f32[768,768]{1,0:T(8,128)}), f32[96,768]{1,0:T(8,128)}) %reduce-scatter.15.cloned.1.call-update) | async-done | bytes 294928 | tf_op jit(solution)/shard_map/reduce_scatter | solution.py:262
  2330.8 605.3 %reduce-scatter.23.cloned.1.call-done = f32[4,384,768]{2,1,0:T(8,128)} async-done(((f32[4,3072,768]{2,1,0:T(8,128)}), f32[4,384,768]{2,1,0:T(8,128)}) %reduce-scatter.23.cloned.1.call-update) | async-done | bytes 4718608 | tf_op jit(solution)/shard_map/reduce_scatter | solution.py:266
  2945.7 598.2 %reduce-scatter.21.cloned.1.call-done = f32[4,96,3072]{2,1,0:T(8,128)} async-done(((f32[4,768,3072]{2,1,0:T(8,128)}), f32[4,96,3072]{2,1,0:T(8,128)}) %reduce-scatter.21.cloned.1.call-update) | async-done | bytes 4718608 | tf_op jit(solution)/shard_map/reduce_scatter | solution.py:265
  3550.5 102.0 %all-reduce.10.cloned.1.call-done = (bf16[73728]{0:T(1024)(128)(2,1)}, bf16[73728]{0:T(1024)(128)(2,1)}, bf16[73728]{0:T(1024)(128)(2,1)}, bf16[73728]{0:T(1024)...) async-done(((bf16[73728]{0:T(1024)(128)(2,1)}, bf16[73728]{0:T(1024)(128)(2,1)}, bf16[73728]{0:T(1024)(128)(2,1)}, bf16[73728]{0:T(1024)(128)(2,1)}, ...) | async-done | bytes 5308432
  3657.0 13.5 copy.118
  3672.9 7.6 fusion.37
  3682.9 40.8 %all-reduce.6 = (f32[768]{0:T(1024)}, f32[768]{0:T(1024)}, f32[32,12]{0,1:T(8,128)}, f32[768,4]{0,1:T(4,128)}) all-reduce(f32[768]{0:T(1024)S(1)} %get-tuple-element.89, f32[768]{0:T(1024)S(1)} %get-tuple-element.68, f32[32,12]{0,1:T(8,128)S(1)} %fusion.37, ...), channel_id=1, replica_groups=mesh['rep'=4,'fsdp'=4,'seq'=2] {'rep','fsdp','seq'}, use_global_device_ids=true, to_apply=%region_40.41 | all-reduce | flops 4992 | bytes 39936 | tf_op jit(solution)/shard_map/psum | solution.py:257
  3725.6 6.1 all_gather.56
  (326 shorter events, 171.9 us)
Async XLA Ops:
  7.2 1798.3 %copy-start = (f32[768,4]{0,1:T(4,128)S(1)}, f32[768,4]{0,1:T(4,128)}, u32[]{:S(2)}) copy-start(f32[768,4]{0,1:T(4,128)} %param.28) | copy-start | bytes 36868
  7.2 46.8 %all-gather.17.cloned.1.call-start = ((), (), s32[]{:S(2)}) async-start(), calls=%async_computation.11 | async-start | bytes 1327104 | tf_op jit(solution)/shard_map/all_gather | solution.py:72
  7.9 88.1 %all-gather.11.cloned.1.call-start = ((), (), s32[]{:S(2)}) async-start(), calls=%async_computation.8 | async-start | bytes 1327104 | tf_op jit(solution)/shard_map/all_gather | solution.py:73
  8.7 1770.2 %all-gather.15.cloned.1.call-start = ((), (), s32[]{:S(2)}) async-start(), calls=%async_computation.10 | async-start | bytes 1327104 | tf_op jit(solution)/shard_map/all_gather | solution.py:71
  9.4 1771.8 %all-gather.19.cloned.1.call-start = ((), (), s32[]{:S(2)}) async-start(), calls=%async_computation.12 | async-start | bytes 1769472 | tf_op jit(solution)/shard_map/all_gather | solution.py:81
  11.3 84.7 %copy-start.45 = (f32[384]{0:T(512)}, f32[384]{0:T(512)S(1)}, u32[]{:S(2)}) copy-start(f32[384]{0:T(512)S(1)} %fusion.51) | copy-start | bytes 4612
  11.3 84.7 %copy-start.5 = (bf16[384,768]{1,0:T(8,128)(2,1)S(1)}, bf16[384,768]{1,0:T(8,128)(2,1)}, u32[]{:S(2)}) copy-start(bf16[384,768]{1,0:T(8,128)(2,1)} %param.15) | copy-start | bytes 1769476
  11.3 84.7 %copy-start.41 = (f32[768]{0:T(1024)S(1)}, f32[768]{0:T(1024)}, u32[]{:S(2)}) copy-start(f32[768]{0:T(1024)} %param.25) | copy-start | bytes 9220
  57.0 1726.0 %all-gather.13.cloned.1.call-start = ((), (), s32[]{:S(2)}) async-start(), calls=%async_computation.9 | async-start | bytes 1769472 | tf_op jit(solution)/shard_map/all_gather | solution.py:82
  98.8 1704.2 %all-gather.21.cloned.1.call-start = ((), (), s32[]{:S(2)}) async-start(), calls=%async_computation.13 | async-start | bytes 1327104 | tf_op jit(solution)/shard_map/all_gather | solution.py:74
  99.4 1741.0 %all-gather.25.cloned.1.call-start = ((), (), s32[]{:S(2)}) async-start(), calls=%async_computation.15 | async-start | bytes 21233664 | tf_op jit(solution)/shard_map/all_gather | solution.py:139
  100.2 1752.7 %all-gather.23.cloned.1.call-start = ((), (), s32[]{:S(2)}) async-start(), calls=%async_computation.14 | async-start | bytes 21233664 | tf_op jit(solution)/shard_map/all_gather | solution.py:138
  100.9 1922.2 %reduce-scatter.27.cloned.1.call-start = ((), (), s32[]{:S(2)}) async-start(), calls=%async_computation.25 | async-start | bytes 1769472
  1752.4 17.8 copy-start.67
  1752.4 19.7 copy-start.20
  1777.6 36.6 copy-start.69
  1805.5 22.7 copy-start.13
  1806.7 31.7 copy-start.50
  1909.2 36.3 copy-start.40
  1909.3 36.3 copy-start.49
  1909.3 36.3 copy-start.73
  1995.9 45.2 %reduce-scatter.25.cloned.1.call-start = ((), (), s32[]{:S(2)}) async-start(), calls=%async_computation.24 | async-start | bytes 1769472
  2011.0 102.6 %reduce-scatter.19.cloned.1.call-start = ((), (), s32[]{:S(2)}) async-start(), calls=%async_computation.19 | async-start | bytes 2654208 | tf_op jit(solution)/shard_map/reduce_scatter | solution.py:264
  2013.4 172.1 %reduce-scatter.13.cloned.1.call-start = ((), (), s32[]{:S(2)}) async-start(), calls=%async_computation.16 | async-start | bytes 2654208 | tf_op jit(solution)/shard_map/reduce_scatter | solution.py:261
  2023.1 234.0 %reduce-scatter.17.cloned.1.call-start = ((), (), s32[]{:S(2)}) async-start(), calls=%async_computation.18 | async-start | bytes 2654208 | tf_op jit(solution)/shard_map/reduce_scatter | solution.py:263
  2026.6 302.5 %reduce-scatter.15.cloned.1.call-start = ((), (), s32[]{:S(2)}) async-start(), calls=%async_computation.17 | async-start | bytes 2654208 | tf_op jit(solution)/shard_map/reduce_scatter | solution.py:262
  2044.5 891.7 %reduce-scatter.23.cloned.1.call-start = ((), (), s32[]{:S(2)}) async-start(), calls=%async_computation.22 | async-start | bytes 42467328 | tf_op jit(solution)/shard_map/reduce_scatter | solution.py:266
  2066.4 1477.5 %reduce-scatter.21.cloned.1.call-start = ((), (), s32[]{:S(2)}) async-start(), calls=%async_computation.20 | async-start | bytes 42467328 | tf_op jit(solution)/shard_map/reduce_scatter | solution.py:265
  2087.2 1565.2 %all-reduce.10.cloned.1.call-start = ((), (), s32[]{:S(2)}) async-start(), calls=%async_computation.26 | async-start | bytes 10616832
  3548.6 205.3 %all-gather.27.cloned.1.call-start = ((), (), s32[]{:S(2)}) async-start(), calls=%async_computation.21 | async-start | bytes 2949120 | tf_op jit(solution)/shard_map/all_gather | solution.py:301
  3654.4 104.5 %all-gather.29.cloned.1.call-start = ((), (), s32[]{:S(2)}) async-start(), calls=%async_computation.23 | async-start | bytes 2949120 | tf_op jit(solution)/shard_map/all_gather | solution.py:304
  3681.9 41.7 %copy-start.66 = (f32[384]{0:T(512)S(1)}, f32[384]{0:T(512)}, u32[]{:S(2)}) copy-start(f32[384]{0:T(512)} %copy-done.65) | copy-start | bytes 4612
  (64 other events, 338.9 us)
Sparse Core Ops, SparseCore 0:
  10.2 43.7 all-gather.16
  56.2 39.8 all-gather.10
  98.2 39.8 all-gather.14
  140.1 21.5 all-gather.18
  163.6 22.7 all-gather.12
  188.5 41.0 all-gather.20
  231.1 361.2 all-gather.24
  593.9 362.4 all-gather.22
  1996.0 20.5 reduce-scatter.26
  2019.3 21.7 reduce-scatter.24
  2044.6 68.9 reduce-scatter.18
  2117.5 67.9 reduce-scatter.12
  2189.0 67.9 reduce-scatter.16
  2261.0 67.9 reduce-scatter.14
  2332.8 603.3 reduce-scatter.22
  2940.4 603.4 reduce-scatter.20
  3548.7 103.6 all-reduce.9
  3654.5 24.2 all-gather.26
  3680.4 24.5 all-gather.28
where the time goes:
time: 3780 us; the launch traced here: 3770 us
  local copies, waits for them, and re-layouts  1750 us (46%)
  waiting for transfers between devices  1640 us (43%)
  matrix products  197 us (5%)
  other arithmetic  97 us (3%)
  blocking collectives  63.4 us (2%)
    gather x3, local copies, waits for them, and re-layouts, block_scores(): bucket_ids = buckets[offset]  1630 us
    reduce_scatter x1, waiting for transfers between devices, per_device(): lax.psum_scatter(grad_w_out, ('fsdp', 'seq'), scatter_dimension=1, tiled=...  605 us
    reduce_scatter x1, waiting for transfers between devices, per_device(): lax.psum_scatter(grad_w_in, ('fsdp', 'seq'), scatter_dimension=1, tiled=T...  598 us
    unnamed x22, waiting for transfers between devices  121 us
  transfers between devices with their start and end apart: 19, of which 10 were waited for; matrix products, arithmetic and copies ran while one was open for 50% of the time, Pallas kernels for 0%

commit v1 on v0

v1 whole, which is shorter than its diff:
```python
import functools

import jax
import jax.numpy as jnp
from jax import lax
from jax.experimental import pallas as pl
from jax.experimental.pallas import tpu as pltpu
from jax.sharding import PartitionSpec as P

PIECE = 256
LANES = 128
epsilon = 1e-06
masked_out = -1e30
highest = lax.Precision.HIGHEST
f32 = jnp.float32
bf16 = jnp.bfloat16
VMEM_LIMIT = 58 * 1024 * 1024


def dot(a, b):
    return jnp.dot(a, b, preferred_element_type=f32)


def dot_t(a, b):
    return lax.dot_general(a, b, (((1,), (1,)), ((), ())), preferred_element_type=f32)


def t_dot(a, b):
    return lax.dot_general(a, b, (((0,), (0,)), ((), ())), preferred_element_type=f32)


def exact_dot(a, b):
    return jnp.dot(a, b, precision=highest, preferred_element_type=f32)


def exact_dot_t(a, b):
    return lax.dot_general(
        a, b, (((1,), (1,)), ((), ())), precision=highest, preferred_element_type=f32
    )


def inverse_rms(values):
    return lax.rsqrt(jnp.mean(values * values, -1, keepdims=True) + epsilon)


def norm_back(values, gain, grad):
    scale = inverse_rms(values)
    scaled = values * scale
    grad_gain = jnp.sum(grad * scaled, 0, keepdims=True)
    weighted = gain * grad
    grad_values = scale * weighted - (
        values * (scale * scale * scale) * jnp.mean(weighted * values, -1, keepdims=True)
    )
    return grad_values, grad_gain


def make_mask(place_ref, mask_ref):
    shape = mask_ref.shape
    pos_q = place_ref[0] + lax.broadcasted_iota(jnp.int32, shape, 0)
    pos_k = lax.broadcasted_iota(jnp.int32, shape, 1)
    allowed = pos_k <= pos_q
    for piece in range(2):
        start = place_ref[1 + piece]
        in_q = (pos_q >= start) & (pos_q < start + PIECE)
        in_k = (pos_k >= start) & (pos_k < start + PIECE)
        allowed = allowed | (in_q & in_k)
    mask_ref[...] = jnp.where(allowed, 0.0, masked_out)


def spread(row, block, width):
    return pltpu.roll(
        jnp.broadcast_to(row, (block, width)), width - (block - 1), 1, stride=1, stride_axis=0
    )


def gather_diagonals(sums):
    rows = sums.shape[0]
    while rows > 1:
        half = rows // 2
        sums = pltpu.roll(sums[:half], half, 1) + sums[half:]
        rows = half
    return sums


def chosen_experts(routes_ref, shape):
    lane = lax.broadcasted_iota(jnp.int32, shape, 1)
    return (lane == routes_ref[:, 0:1]) | (lane == routes_ref[:, 1:2])


def forward_kernel(
    n_experts,
    head_dim,
    place_ref,
    x_ref,
    gain_one_ref,
    gain_two_ref,
    wq_ref,
    wk_ref,
    wv_ref,
    wo_ref,
    dist_ref,
    routes_ref,
    router_ref,
    q_out,
    k_out,
    v_out,
    o_out,
    lse_out,
    x_mid_out,
    message_out,
    probs_out,
    h_out,
    total_ref,
    mask_ref,
    bias_ref,
):
    step = pl.program_id(0)
    rows = x_mid_out.shape[0]
    length, width = x_ref.shape
    own = pl.ds(pl.multiple_of(place_ref[0], rows), rows)

    @pl.when(step == 0)
    def _():
        values = x_ref[...].astype(f32)
        h_out[...] = (values * inverse_rms(values) * gain_one_ref[...]).astype(bf16)
        total_ref[...] = jnp.zeros_like(total_ref)
        make_mask(place_ref, mask_ref)

    h_all = h_out[...]
    q_low = dot(h_out[own, :], wq_ref[...]).astype(bf16) * (head_dim**-0.5)
    k_low = dot(h_all, wk_ref[...]).astype(bf16)
    v_low = dot(h_all, wv_ref[...]).astype(bf16)
    q_out[...] = q_low
    k_out[...] = k_low
    v_out[...] = v_low
    block = LANES
    span = dist_ref.shape[2]
    first_half = lax.broadcasted_iota(jnp.int32, (block, LANES), 1) < head_dim
    for head in range(2):
        bias_ref[head] = spread(dist_ref[0, head : head + 1, :], block, span)
    for b in range(rows // block):
        here = slice(b * block, (b + 1) * block)
        offset = pl.multiple_of(length - LANES - block * b - place_ref[0], LANES)
        halves = []
        tops = []
        for head in range(2):
            mine = first_half if head == 0 else ~first_half
            q_head = jnp.where(mine, q_low[here], jnp.zeros((), bf16))
            scores = dot_t(q_head, k_low)
            scores = scores + bias_ref[head, :, pl.ds(offset, length)] + mask_ref[here, :]
            top = jnp.max(scores, -1, keepdims=True)
            exp_scores = jnp.exp(scores - top)
            total = jnp.sum(exp_scores, -1, keepdims=True)
            probs = (exp_scores * (1.0 / total)).astype(bf16)
            halves.append(dot(probs, v_low))
            tops.append(top + jnp.log(total))
        o_out[here, :] = jnp.where(first_half, halves[0], halves[1]).astype(bf16)
        lse_out[here, :] = jnp.where(first_half, tops[0], tops[1])
    total_ref[...] += dot(o_out[...], wo_ref[...])

    @pl.when(step == pl.num_programs(0) - 1)
    def _():
        x_mid = x_ref[own, :].astype(f32) + total_ref[...]
        x_mid_out[...] = x_mid
        h_two = (x_mid * inverse_rms(x_mid) * gain_two_ref[...]).astype(bf16)
        message_out[:, :width] = h_two
        logits = exact_dot(h_two.astype(f32), router_ref[...])
        lane = lax.broadcasted_iota(jnp.int32, logits.shape, 1)
        logits = jnp.where(lane < n_experts, logits, masked_out)
        exp_logits = jnp.exp(logits - jnp.max(logits, -1, keepdims=True))
        probs = exp_logits / jnp.sum(exp_logits, -1, keepdims=True)
        probs_out[...] = probs
        chosen = jnp.where(chosen_experts(routes_ref, probs.shape), probs, 0.0)
        gate = chosen / jnp.sum(chosen, -1, keepdims=True)
        high = gate.astype(bf16)
        low = gate - high.astype(f32)
        message_out[:, width:] = (high.astype(f32) + pltpu.roll(low, n_experts, 1)).astype(bf16)


def attention_forward(
    place, x_all, gain_one, gain_two, weights, dist, routes, router, n_rows, n_experts, head_dim
):
    length, width = x_all.shape
    pairs = width // LANES
    span = dist.shape[2]
    whole = lambda shape: pl.BlockSpec(shape, lambda p, *_: (0,) * len(shape))
    columns = lambda rows: pl.BlockSpec((rows, LANES), lambda p, *_: (0, p))
    matrix = lambda i: pl.BlockSpec((None, width, LANES), lambda p, *_: (i, 0, p))
    out_shape = [
        jax.ShapeDtypeStruct((n_rows, width), bf16),
        jax.ShapeDtypeStruct((length, width), bf16),
        jax.ShapeDtypeStruct((length, width), bf16),
        jax.ShapeDtypeStruct((n_rows, width), bf16),
        jax.ShapeDtypeStruct((n_rows, width), f32),
        jax.ShapeDtypeStruct((n_rows, width), f32),
        jax.ShapeDtypeStruct((n_rows, width + LANES), bf16),
        jax.ShapeDtypeStruct((n_rows, LANES), f32),
        jax.ShapeDtypeStruct((length, width), bf16),
    ]
    return pl.pallas_call(
        functools.partial(forward_kernel, n_experts, head_dim),
        out_shape=out_shape,
        grid_spec=pltpu.PrefetchScalarGridSpec(
            num_scalar_prefetch=1,
            grid=(pairs,),
            in_specs=[
                whole((length, width)),
                whole((1, width)),
                whole((1, width)),
                matrix(0),
                matrix(1),
                matrix(2),
                pl.BlockSpec((None, LANES, width), lambda p, *_: (3, p, 0)),
                pl.BlockSpec((1, 2, span), lambda p, *_: (p, 0, 0)),
                whole((n_rows, 2)),
                whole((width, LANES)),
            ],
            out_specs=[
                columns(n_rows),
                columns(length),
                columns(length),
                columns(n_rows),
                columns(n_rows),
                whole((n_rows, width)),
                whole((n_rows, width + LANES)),
                whole((n_rows, LANES)),
                whole((length, width)),
            ],
            scratch_shapes=[
                pltpu.VMEM((n_rows, width), f32),
                pltpu.VMEM((n_rows, length), f32),
                pltpu.VMEM((2, LANES, span), f32),
            ],
        ),
        compiler_params=pltpu.CompilerParams(vmem_limit_bytes=VMEM_LIMIT),
        cost_estimate=pl.CostEstimate(
            flops=20_000_000_000, transcendentals=0, bytes_accessed=20_000_000
        ),
        name="attention_forward",
    )(place, x_all, gain_one, gain_two, weights, weights, weights, weights, dist, routes, router)


GELU_A = 0.7978845608028654
GELU_B = 0.044715 * GELU_A


def experts_kernel(
    n_experts,
    chunk,
    expert_ref,
    message_ref,
    dy_ref,
    w_in_ref,
    w_out_ref,
    out_ref,
    dh_ref,
    dw_in_ref,
    dw_out_ref,
    dw_in_acc,
    dw_out_acc,
):
    step = pl.program_id(0)
    width = dy_ref.shape[1]
    hidden = w_in_ref.shape[1]
    expert = expert_ref[0]

    @pl.when(step == 0)
    def _():
        dw_in_acc[...] = jnp.zeros_like(dw_in_acc)
        dw_out_acc[...] = jnp.zeros_like(dw_out_acc)

    h = message_ref[:, :width]
    extra = message_ref[:, width:].astype(f32)
    lane = lax.broadcasted_iota(jnp.int32, extra.shape, 1)
    mine = (lane == expert) | (lane == expert + n_experts)
    gate = jnp.sum(jnp.where(mine, extra, 0.0), -1, keepdims=True)
    dy = dy_ref[...]
    out_total = None
    dh_total = None
    dgate = None
    for start in range(0, hidden, chunk):
        part = slice(start, start + chunk)
        up = dot(h, w_in_ref[:, part])
        dact = dot_t(dy, w_out_ref[part, :])
        square = up * up
        tanh = jnp.tanh(up * (GELU_A + GELU_B * square))
        half = 0.5 * up
        more = 1.0 + tanh
        act = half * more
        slope = 0.5 * more + half * (1.0 - tanh * tanh) * (GELU_A + 3.0 * GELU_B * square)
        gated = (gate * act).astype(bf16)
        dgate_part = jnp.sum(act * dact, -1, keepdims=True)
        dup = (gate * dact * slope).astype(bf16)
        out_part = dot(gated, w_out_ref[part, :])
        dh_part = dot_t(dup, w_in_ref[:, part])
        out_total = out_part if out_total is None else out_total + out_part
        dh_total = dh_part if dh_total is None else dh_total + dh_part
        dgate = dgate_part if dgate is None else dgate + dgate_part
        dw_out_acc[part, :] += t_dot(gated, dy)
        dw_in_acc[:, part] += t_dot(h, dup)
    out_ref[...] = out_total.astype(bf16)
    dh_ref[:, :width] = dh_total.astype(bf16)
    high = dgate.astype(bf16).astype(f32)
    low = dgate - high
    dh_ref[:, width:] = jnp.where(
        lane == expert, high, jnp.where(lane == expert + n_experts, low, 0.0)
    ).astype(bf16)

    @pl.when(step == pl.num_programs(0) - 1)
    def _():
        dw_in_ref[...] = dw_in_acc[...].astype(bf16)
        dw_out_ref[...] = dw_out_acc[...].astype(bf16)


def experts(expert, message, dy, w_in, w_out, n_experts, block):
    tokens, width = dy.shape
    hidden = w_in.shape[1]
    whole = lambda shape: pl.BlockSpec(shape, lambda i, *_: (0,) * len(shape))
    rows = lambda columns: pl.BlockSpec((block, columns), lambda i, *_: (i, 0))
    return pl.pallas_call(
        functools.partial(experts_kernel, n_experts, 512),
        out_shape=[
            jax.ShapeDtypeStruct((tokens, width), bf16),
            jax.ShapeDtypeStruct((tokens, width + LANES), bf16),
            jax.ShapeDtypeStruct((width, hidden), bf16),
            jax.ShapeDtypeStruct((hidden, width), bf16),
        ],
        grid_spec=pltpu.PrefetchScalarGridSpec(
            num_scalar_prefetch=1,
            grid=(tokens // block,),
            in_specs=[
                rows(width + LANES),
                rows(width),
                whole((width, hidden)),
                whole((hidden, width)),
            ],
            out_specs=[
                rows(width),
                rows(width + LANES),
                whole((width, hidden)),
                whole((hidden, width)),
            ],
            scratch_shapes=[
                pltpu.VMEM((width, hidden), f32),
                pltpu.VMEM((hidden, width), f32),
            ],
        ),
        compiler_params=pltpu.CompilerParams(vmem_limit_bytes=VMEM_LIMIT),
        cost_estimate=pl.CostEstimate(
            flops=60_000_000_000, transcendentals=0, bytes_accessed=30_000_000
        ),
        name="experts",
    )(expert, message, dy, w_in, w_out)


def backward_kernel(
    n_experts,
    head_dim,
    place_ref,
    back_ref,
    dy_ref,
    x_mid_ref,
    message_ref,
    probs_ref,
    routes_ref,
    router_ref,
    gain_two_ref,
    h_ref,
    wq_ref,
    wk_ref,
    wv_ref,
    wo_ref,
    q_ref,
    k_ref,
    v_ref,
    o_ref,
    lse_ref,
    dist_ref,
    dwq_out,
    dwk_out,
    dwv_out,
    dwo_out,
    dh_own_out,
    dh_other_out,
    dx_mid_out,
    gain_out,
    router_out,
    ddist_out,
    da_ref,
    dh_all_ref,
    dh_mine_ref,
    mask_ref,
    bias_ref,
    dbias_ref,
    dq_ref,
):
    step = pl.program_id(0)
    rows, width = x_mid_ref.shape
    length = h_ref.shape[0]
    own = pl.ds(pl.multiple_of(place_ref[0], rows), rows)

    @pl.when(step == 0)
    def _():
        probs = probs_ref[...]
        chosen = chosen_experts(routes_ref, probs.shape)
        picked = jnp.where(chosen, probs, 0.0)
        total = jnp.sum(picked, -1, keepdims=True)
        gate = picked / total
        extra = back_ref[:, width:].astype(f32)
        dgate = extra + pltpu.roll(extra, LANES - n_experts, 1)
        dgate = jnp.where(chosen, dgate, 0.0)
        shared = jnp.sum(dgate * gate, -1, keepdims=True)
        dprobs = jnp.where(chosen, (dgate - shared) / total, 0.0)
        dlogits = probs * (dprobs - jnp.sum(probs * dprobs, -1, keepdims=True))
        h_two = message_ref[:, :width].astype(f32)
        router_out[...] = lax.dot_general(
            dlogits,
            h_two,
            (((0,), (0,)), ((), ())),
            precision=highest,
            preferred_element_type=f32,
        )
        dh_two = back_ref[:, :width].astype(f32) + exact_dot_t(dlogits, router_ref[...])
        dx, dgain = norm_back(x_mid_ref[...], gain_two_ref[...], dh_two)
        gain_out[...] = dgain
        dx_mid = dx + dy_ref[...].astype(f32)
        dx_mid_out[...] = dx_mid
        da_ref[...] = dx_mid.astype(bf16)
        dh_all_ref[...] = jnp.zeros_like(dh_all_ref)
        dh_mine_ref[...] = jnp.zeros_like(dh_mine_ref)
        make_mask(place_ref, mask_ref)

    da = da_ref[...]
    do = dot_t(da, wo_ref[...]).astype(bf16)
    dwo_out[...] = t_dot(o_ref[...], da).astype(bf16)
    block = LANES
    span = dist_ref.shape[2]
    first_half = lax.broadcasted_iota(jnp.int32, (block, LANES), 1) < head_dim
    zero = jnp.zeros((), bf16)
    k_low = k_ref[...]
    v_low = v_ref[...]
    dk = None
    dv = None
    for head in range(2):
        bias_ref[head] = spread(dist_ref[0, head : head + 1, :], block, span)
        dbias_ref[head] = jnp.zeros_like(dbias_ref[head])
    for b in range(rows // block):
        here = slice(b * block, (b + 1) * block)
        offset = pl.multiple_of(length - LANES - block * b - place_ref[0], LANES)
        halves = []
        for head in range(2):
            mine = first_half if head == 0 else ~first_half
            q_head = jnp.where(mine, q_ref[here, :], zero)
            do_head = jnp.where(mine, do[here], zero)
            scores = dot_t(q_head, k_low)
            scores = scores + bias_ref[head, :, pl.ds(offset, length)] + mask_ref[here, :]
            at = head * head_dim
            probs = jnp.exp(scores - lse_ref[here, at : at + 1])
            dprobs = dot_t(do_head, v_low)
            weighted = probs * dprobs
            ds = weighted - probs * jnp.sum(weighted, -1, keepdims=True)
            ds_low = ds.astype(bf16)
            dbias_ref[head, :, pl.ds(offset, length)] += ds
            halves.append(dot(ds_low, k_low))
            dk_part = t_dot(ds_low, q_head)
            dv_part = t_dot(probs.astype(bf16), do_head)
            dk = dk_part if dk is None else dk + dk_part
            dv = dv_part if dv is None else dv + dv_part
        dq_ref[here, :] = (
            jnp.where(first_half, halves[0], halves[1]) * (head_dim**-0.5)
        ).astype(bf16)
    for head in range(2):
        ddist_out[0, head : head + 1, :] = gather_diagonals(dbias_ref[head])
    dq = dq_ref[...]
    dk = dk.astype(bf16)
    dv = dv.astype(bf16)
    h_all = h_ref[...]
    dwq_out[...] = t_dot(h_ref[own, :], dq).astype(bf16)
    dwk_out[...] = t_dot(h_all, dk).astype(bf16)
    dwv_out[...] = t_dot(h_all, dv).astype(bf16)
    dh_all_ref[...] += dot_t(dk, wk_ref[...]) + dot_t(dv, wv_ref[...])
    dh_mine_ref[...] += dot_t(dq, wq_ref[...])

    @pl.when(step == pl.num_programs(0) - 1)
    def _():
        other = pl.ds(pl.multiple_of(length - rows - place_ref[0], rows), rows)
        dh_own_out[...] = dh_mine_ref[...] + dh_all_ref[own, :]
        dh_other_out[...] = dh_all_ref[other, :].astype(bf16)


def attention_backward(
    place,
    back,
    dy,
    x_mid,
    message,
    probs,
    routes,
    router,
    gain_two,
    h_all,
    weights,
    q,
    k,
    v,
    o,
    lse,
    dist,
    n_experts,
    head_dim,
):
    n_rows, width = x_mid.shape
    length = h_all.shape[0]
    pairs = width // LANES
    span = dist.shape[2]
    whole = lambda shape: pl.BlockSpec(shape, lambda p, *_: (0,) * len(shape))
    columns = lambda rows: pl.BlockSpec((rows, LANES), lambda p, *_: (0, p))
    matrix = lambda i: pl.BlockSpec((None, width, LANES), lambda p, *_: (i, 0, p))
    return pl.pallas_call(
        functools.partial(backward_kernel, n_experts, head_dim),
        out_shape=[
            jax.ShapeDtypeStruct((width, width), bf16),
            jax.ShapeDtypeStruct((width, width), bf16),
            jax.ShapeDtypeStruct((width, width), bf16),
            jax.ShapeDtypeStruct((width, width), bf16),
            jax.ShapeDtypeStruct((n_rows, width), f32),
            jax.ShapeDtypeStruct((n_rows, width), bf16),
            jax.ShapeDtypeStruct((n_rows, width), f32),
            jax.ShapeDtypeStruct((1, width), f32),
            jax.ShapeDtypeStruct((LANES, width), f32),
            jax.ShapeDtypeStruct((pairs, 2, span), f32),
        ],
        grid_spec=pltpu.PrefetchScalarGridSpec(
            num_scalar_prefetch=1,
            grid=(pairs,),
            in_specs=[
                whole((n_rows, width + LANES)),
                whole((n_rows, width)),
                whole((n_rows, width)),
                whole((n_rows, width + LANES)),
                whole((n_rows, LANES)),
                whole((n_rows, 2)),
                whole((width, LANES)),
                whole((1, width)),
                whole((length, width)),
                matrix(0),
                matrix(1),
                matrix(2),
                pl.BlockSpec((None, LANES, width), lambda p, *_: (3, p, 0)),
                columns(n_rows),
                columns(length),
                columns(length),
                columns(n_rows),
                columns(n_rows),
                pl.BlockSpec((1, 2, span), lambda p, *_: (p, 0, 0)),
            ],
            out_specs=[
                columns(width),
                columns(width),
                columns(width),
                pl.BlockSpec((LANES, width), lambda p, *_: (p, 0)),
                whole((n_rows, width)),
                whole((n_rows, width)),
                whole((n_rows, width)),
                whole((1, width)),
                whole((LANES, width)),
                pl.BlockSpec((1, 2, span), lambda p, *_: (p, 0, 0)),
            ],
            scratch_shapes=[
                pltpu.VMEM((n_rows, width), bf16),
                pltpu.VMEM((length, width), f32),
                pltpu.VMEM((n_rows, width), f32),
                pltpu.VMEM((n_rows, length), f32),
                pltpu.VMEM((2, LANES, span), f32),
                pltpu.VMEM((2, LANES, span), f32),
                pltpu.VMEM((n_rows, LANES), bf16),
            ],
        ),
        compiler_params=pltpu.CompilerParams(vmem_limit_bytes=VMEM_LIMIT),
        cost_estimate=pl.CostEstimate(
            flops=40_000_000_000, transcendentals=0, bytes_accessed=30_000_000
        ),
        name="attention_backward",
    )(
        place,
        back,
        dy,
        x_mid,
        message,
        probs,
        routes,
        router,
        gain_two,
        h_all,
        weights,
        weights,
        weights,
        weights,
        q,
        k,
        v,
        o,
        lse,
        dist,
    )


def per_device(
    tokens,
    piece_starts,
    routes,
    buckets,
    attn_q,
    attn_k,
    attn_v,
    attn_o,
    expert_in,
    expert_out,
    gain_attn,
    gain_ffn,
    rel_table,
    router,
    cotangent,
):
    n_rep, n_fsdp, n_seq = (lax.axis_size(a) for a in ("rep", "fsdp", "seq"))
    rep = lax.axis_index("rep")
    seq = lax.axis_index("seq")
    plane = ("rep", "seq")
    n_rows, width = tokens.shape
    n_buckets, n_heads = rel_table.shape
    head_dim = width // n_heads
    n_experts, part_in, hidden = expert_in.shape
    part_out = expert_out.shape[1]
    part_attn = attn_q.shape[0]
    length = n_rows * n_seq
    assert n_experts == n_rep == 4 and n_seq == 2 and 2 * head_dim == LANES
    pairs = n_heads // 2

    place = jnp.concatenate([(seq * n_rows)[None], piece_starts[0]]).astype(jnp.int32)
    pick = lambda array: lax.dynamic_index_in_dim(array, rep, 0, keepdims=False)
    attn_own = pick(jnp.stack([attn_q, attn_k, attn_v, attn_o]))
    attn_line = lax.all_gather(attn_own, "fsdp", axis=0, tiled=False)
    attn_all = lax.all_gather(attn_line, plane, axis=0, tiled=False)
    attn_all = attn_all.reshape(n_rep, n_seq, n_fsdp, part_attn, width)
    weights = attn_all.transpose(0, 2, 1, 3, 4).reshape(n_rep, width, width)
    x_all = lax.all_gather(tokens, "seq", axis=0, tiled=True)

    in_own = pick(expert_in).reshape(part_in, n_fsdp, n_seq, part_out)
    in_own = in_own.transpose(2, 0, 1, 3).reshape(n_seq, part_in, n_fsdp * part_out)
    in_pair = lax.all_to_all(in_own, "seq", split_axis=0, concat_axis=0, tiled=True)
    in_pair = in_pair.reshape(n_seq * part_in, n_fsdp * part_out)
    w_in = lax.all_gather(in_pair, "fsdp", axis=0, tiled=True)
    w_out = lax.all_gather(pick(expert_out), "fsdp", axis=0, tiled=True)
    dy_all = lax.all_gather(cotangent, plane, axis=0, tiled=True)

    match = (buckets[:, None] == jnp.arange(n_buckets, dtype=jnp.int32)[None, :]).astype(f32)
    dist = lax.dot_general(
        rel_table, match, (((0,), (1,)), ((), ())), precision=highest, preferred_element_type=f32
    )
    span = -(-dist.shape[1] // LANES) * LANES
    dist = jnp.pad(dist, ((0, 0), (0, span - dist.shape[1]))).reshape(pairs, 2, span)
    router_wide = jnp.pad(router, ((0, 0), (0, LANES - n_experts)))
    gain_one = gain_attn[None, :]
    gain_two = gain_ffn[None, :]

    q, k, v, o, lse, x_mid, message, probs, h_all = attention_forward(
        place,
        x_all,
        gain_one,
        gain_two,
        weights,
        dist,
        routes,
        router_wide,
        n_rows,
        n_experts,
        head_dim,
    )
    message_all = lax.all_gather(message, plane, axis=0, tiled=True)
    out_part, back_part, dw_in, dw_out = experts(
        rep[None].astype(jnp.int32), message_all, dy_all, w_in, w_out, n_experts, n_rows
    )
    back = lax.psum_scatter(back_part, plane, scatter_dimension=0, tiled=True)
    out_sum = lax.psum_scatter(out_part, plane, scatter_dimension=0, tiled=True)
    out_rows = (x_mid + out_sum.astype(f32)).astype(bf16)

    dwq, dwk, dwv, dwo, dh_own, dh_other, dx_mid, dgain_two, drouter, ddist = attention_backward(
        place,
        back,
        cotangent,
        x_mid,
        message,
        probs,
        routes,
        router_wide,
        gain_two,
        h_all,
        weights,
        q,
        k,
        v,
        o,
        lse,
        dist,
        n_experts,
        head_dim,
    )
    sum_out = lax.psum_scatter(dw_out, "fsdp", scatter_dimension=0, tiled=True)
    sum_in = lax.psum_scatter(dw_in, "fsdp", scatter_dimension=0, tiled=True)
    sum_in = sum_in.reshape(n_seq, part_in, n_fsdp * part_out)
    sum_in = lax.all_to_all(sum_in, "seq", split_axis=0, concat_axis=0, tiled=True)
    sum_in = sum_in.reshape(n_seq, part_in, n_fsdp, part_out).transpose(1, 2, 0, 3)
    sum_in = sum_in.reshape(part_in, hidden)
    grad_out = lax.all_gather(sum_out, "rep", axis=0, tiled=False).astype(f32)
    grad_in = lax.all_gather(sum_in, "rep", axis=0, tiled=False).astype(f32)

    swap = [(0, 1), (1, 0)]
    dh_one = dh_own + lax.ppermute(dh_other, "seq", swap).astype(f32)
    dx, dgain_one = norm_back(tokens.astype(f32), gain_one, dh_one)
    grad_tokens = (dx_mid + dx).astype(bf16)

    attn_grads = jnp.stack([dwq, dwk, dwv, dwo]).reshape(n_rep, n_fsdp, n_seq, part_attn, width)
    attn_grads = attn_grads.transpose(0, 2, 1, 3, 4).reshape(
        n_rep * n_seq * n_fsdp * part_attn, width
    )
    attn_sum = lax.psum_scatter(attn_grads, plane, scatter_dimension=0, tiled=True)
    attn_sum = lax.psum_scatter(attn_sum, "fsdp", scatter_dimension=0, tiled=True)
    attn_sum = lax.all_gather(attn_sum, "rep", axis=0, tiled=False).astype(f32)

    ddist = ddist.reshape(n_heads, span)[:, : buckets.shape[0]]
    table = lax.dot_general(
        match, ddist, (((0,), (1,)), ((), ())), precision=highest, preferred_element_type=f32
    )
    grad_one, grad_two, grad_table, grad_router = lax.psum(
        (dgain_one[0], dgain_two[0], table, drouter[:n_experts].T), ("rep", "fsdp", "seq")
    )
    return (
        out_rows,
        grad_tokens,
        attn_sum[0],
        attn_sum[1],
        attn_sum[2],
        attn_sum[3],
        grad_in,
        grad_out,
        grad_one,
        grad_two,
        grad_table,
        grad_router,
    )


def solution(mesh):
    rows = P(("rep", "fsdp", "seq"), None)
    owned = P(("fsdp", "seq"), None)
    expert = P(None, ("fsdp", "seq"), None)
    in_specs = (
        rows,
        P(("rep", "fsdp"), None),
        rows,
        P(),
        owned,
        owned,
        owned,
        owned,
        expert,
        expert,
        P(),
        P(),
        P(),
        P(),
        rows,
    )
    out_specs = (
        rows,
        rows,
        owned,
        owned,
        owned,
        owned,
        expert,
        expert,
        P(),
        P(),
        P(),
        P(),
    )
    return jax.shard_map(
        per_device, mesh=mesh, in_specs=in_specs, out_specs=out_specs, check_vma=False
    )
```

time: 3780 us -> 734 us (0.19)
  local copies, waits for them, and re-layouts: 1750 us -> 18.1 us
  waiting for transfers between devices: 1640 us -> 451 us
  matrix products: 197 us -> 2.28 us
  Pallas kernels: 0 us -> 133 us
  other arithmetic: 97 us -> 20.2 us
    gather x12 -> x0, local copies, waits for them, and re-layouts: 1650 us -> none  [the longest x3 1630 us: block_scores(): bucket_ids = buckets[offset]]
    reduce_scatter x6, waiting for transfers between devices: 1440 us -> 204 us  [the longest x1 60.5 us: per_device(): back = lax.psum_scatter(back_part, plane, scatter_dimension=0, tiled=True)]
    dot_general x29 -> x2, matrix products: 197 us -> 2.28 us  [the longest x1 1.18 us: per_device(): lax.dot_general(rel_table, match, (((0,), (1,)), ((), ())), precision=hig...]
    all_gather x10 -> x8, waiting for transfers between devices: 81.8 us -> 243 us  [the longest x1 50.8 us: per_device(): w_in = lax.all_gather(in_pair, 'fsdp', axis=0, tiled=True)]
    pallas_call x0 -> x3, Pallas kernels: none -> 133 us  [the longest x1 61.1 us: experts(): pl.pallas_call(functools.partial(experts_kernel, n_experts, 512), out_sha...]
    unnamed x22 -> x14, waiting for transfers between devices: 121 us -> 3.29 us
  transfers between devices with their start and end apart: 19 -> 15, of which waited for: 10 -> 13; matrix products, arithmetic and copies ran while one was open for 50% -> 5% of each run, Pallas kernels for 0% -> 10%
where the time goes in v1:
time: 734 us
  waiting for transfers between devices  451 us (61%)
  Pallas kernels  133 us (18%)
  blocking collectives  94.2 us (13%)
  other arithmetic  20.2 us (3%)
  local copies, waits for them, and re-layouts  18.1 us (2%)
  between operations  14.2 us (2%)
    pallas_call x1, Pallas kernels, experts(): pl.pallas_call(functools.partial(experts_kernel, n_experts, 512), out_sha...  61.1 us
    reduce_scatter x1, waiting for transfers between devices, per_device(): back = lax.psum_scatter(back_part, plane, scatter_dimension=0, tiled=True)  60.5 us
    reduce_scatter x1, waiting for transfers between devices, per_device(): lax.psum_scatter(attn_grads, plane, scatter_dimension=0, tiled=True)  52.3 us
    all_gather x1, waiting for transfers between devices, per_device(): w_in = lax.all_gather(in_pair, 'fsdp', axis=0, tiled=True)  50.8 us
    reduce_scatter x1, waiting for transfers between devices, per_device(): sum_out = lax.psum_scatter(dw_out, 'fsdp', scatter_dimension=0, tiled=True)  46.1 us
    all_gather x1, waiting for transfers between devices, per_device(): message_all = lax.all_gather(message, plane, axis=0, tiled=True)  44 us
    reduce_scatter x1, waiting for transfers between devices, per_device(): out_sum = lax.psum_scatter(out_part, plane, scatter_dimension=0, tiled=True)  41.9 us
    pallas_call x1, Pallas kernels, attention_backward(): pl.pallas_call(functools.partial(backward_kernel, n_experts, head_dim), o...  41.6 us
  transfers between devices with their start and end apart: 15, of which 13 were waited for; matrix products, arithmetic and copies ran while one was open for 5% of the time, Pallas kernels for 10%

profile of v1, /device:TPU:0, one launch (start us, length us, event | category | flops | bytes accessed | tf_op | source)
XLA Modules:
  0.0 733.6 jit_solution(13542212158008074549)
XLA Ops:
  7.2 1.2 fusion.13
  8.4 18.4 %all_gather.41 = bf16[4,96,768]{2,1,0:T(8,128)(2,1)} all-gather(bf16[1,96,768]{2,1,0:T(8,128)(2,1)S(1)} %fusion.13), channel_id=1, replica_groups=mesh['rep'=4,'fsdp'=4,'seq'=2] {'fsdp'}, dimensions={0}, use_global_device_ids=true | all-gather | bytes 737280 | tf_op jit(solution)/shard_map/all_gather | solution.py:642
  28.6 1.1 constant_dynamic-slice_fusion.1
  30.7 14.3 %all_to_all.10 = bf16[2,96,1536]{2,1,0:T(8,128)(2,1)} all-to-all(bf16[2,96,1536]{2,1,0:T(8,128)(2,1)S(1)} %reshape.88), channel_id=1, replica_groups=mesh['rep'=4,'fsdp'=4,'seq'=2] {'seq'}, dimensions={0} | all-to-all | bytes 1179648 | tf_op jit(solution)/shard_map/all_to_all | solution.py:650
  46.6 1.2 convolution_bitcast_fusion
  51.1 18.8 %all-gather.23.cloned.1.call-done = bf16[32,96,768]{2,1,0:T(8,128)(2,1)} async-done(((bf16[4,96,768]{2,1,0:T(8,128)(2,1)}), bf16[32,96,768]{2,1,0:T(8,128)(2,1)}) %all-gather.23.cloned.1.call-update) | async-done | bytes 4718608 | tf_op jit(solution)/shard_map/all_gather | solution.py:643
  69.9 4.9 copy.46
  74.8 19.4 %all-gather.13.cloned.1.call-done.x_ref = bf16[768,768]{1,0:T(8,128)(2,1)} async-done(((bf16[384,768]{1,0:T(8,128)(2,1)}), bf16[768,768]{1,0:T(8,128)(2,1)}) %all-gather.13.cloned.1.call-update) | async-done | bytes 1179664 | tf_op jit(solution)/shard_map/all_gather | solution.py:646
  94.2 30.1 %attention_forward.1 = (bf16[384,768]{1,0:T(8,128)(2,1)}, bf16[768,768]{1,0:T(8,128)(2,1)}, bf16[768,768]{1,0:T(8,128)(2,1)}, bf16[384,768]{1,0:T(8,128)(2,1)}, ...) custom-call(s32[3]{0:T(128)} %pad_add_fusion.place_ref, ...), custom_call_target="tpu_custom_call" | custom-call | flops 20000000000 | bytes 20000000 | tf_op jit(solution)/shard_map/attention_forward/pallas_call | solution.py:200
  124.6 22.3 %all-gather.25.cloned.1.call-done = bf16[1,1536,768]{2,1,0:T(8,128)(2,1)} async-done(((bf16[1,384,768]{2,1,0:T(8,128)(2,1)}), bf16[1,1536,768]{2,1,0:T(8,128)(2,1)}) %all-gather.25.cloned.1.call-update) | async-done | bytes 2359312 | tf_op jit(solution)/shard_map/all_gather | solution.py:653
  146.9 50.8 %all-gather.19.cloned.1.call-done.w_in_ref = bf16[768,1536]{1,0:T(8,128)(2,1)} async-done(((bf16[192,1536]{1,0:T(8,128)(2,1)}), bf16[768,1536]{1,0:T(8,128)(2,1)}) %all-gather.19.cloned.1.call-update) | async-done | bytes 2359312 | tf_op jit(solution)/shard_map/all_gather | solution.py:652
  197.6 39.5 %all-gather.17.cloned.1.call-done.dy_ref = bf16[3072,768]{1,0:T(8,128)(2,1)} async-done(((bf16[384,768]{1,0:T(8,128)(2,1)}), bf16[3072,768]{1,0:T(8,128)(2,1)}) %all-gather.17.cloned.1.call-update) | async-done | bytes 4718608 | tf_op jit(solution)/shard_map/all_gather | solution.py:654
  237.1 44.0 %all-gather.15.cloned.1.call-done.message_ref = bf16[3072,896]{1,0:T(8,128)(2,1)} async-done(((bf16[384,896]{1,0:T(8,128)(2,1)}), bf16[3072,896]{1,0:T(8,128)(2,1)}) %all-gather.15.cloned.1.call-update) | async-done | bytes 5505040 | tf_op jit(solution)/shard_map/all_gather | solution.py:679
  281.1 61.1 %experts.1 = (bf16[3072,768]{1,0:T(8,128)(2,1)}, bf16[3072,896]{1,0:T(8,128)(2,1)}, bf16[768,1536]{1,0:T(8,128)(2,1)}, bf16[1536,768]{1,0:T(8,128)(2,1)}) custom-call(s32[1]{0:T(128)} %bitcast.10.expert_ref, bf16[3072,896]{1,0:T(8,128)(2,1)} %all-gather.15.cloned.1.call-done.message_ref, bf16[3072,768]{1,0:T(8,128)(2,1)} %all-gather.17.cloned.1.call-done.dy_ref, ...), custom_call_target="tpu_custom_call" | custom-call | flops 60000002048 | bytes 30000000 | tf_op jit(solution)/shard_map/experts/pallas_call | solution.py:320
  344.3 46.1 %reduce-scatter.17.cloned.1.call-done = bf16[384,768]{1,0:T(8,128)(2,1)} async-done(((bf16[1536,768]{1,0:T(8,128)(2,1)}), bf16[384,768]{1,0:T(8,128)(2,1)}) %reduce-scatter.17.cloned.1.call-update) | async-done | bytes 589840 | tf_op jit(solution)/shard_map/reduce_scatter | solution.py:708
  390.7 60.5 %reduce-scatter.9.cloned.1.call-done.back_ref = bf16[384,896]{1,0:T(8,128)(2,1)} async-done(((bf16[3072,896]{1,0:T(8,128)(2,1)}), bf16[384,896]{1,0:T(8,128)(2,1)}) %reduce-scatter.9.cloned.1.call-update) | async-done | bytes 688144 | tf_op jit(solution)/shard_map/reduce_scatter | solution.py:683
  451.2 41.6 %attention_backward.1 = (bf16[768,768]{1,0:T(8,128)(2,1)}, bf16[768,768]{1,0:T(8,128)(2,1)}, bf16[768,768]{1,0:T(8,128)(2,1)}, bf16[768,768]{1,0:T(8,128)(2,1)},...) custom-call(s32[3]{0:T(128)} %pad_add_fusion.place_ref, ...), custom_call_target="tpu_custom_call" | custom-call | flops 40000000000 | bytes 30000000 | tf_op jit(solution)/shard_map/attention_backward/pallas_call | solution.py:519
  492.9 2.6 maximum_bitcast_fusion
  495.5 2.5 copy.51
  498.1 3.6 reduce-scatter.15.cloned.1.call-done
  501.7 12.3 %all_to_all.11 = bf16[2,96,1536]{2,1,0:T(8,128)(2,1)S(1)} all-to-all(bf16[2,96,1536]{2,1,0:T(8,128)(2,1)} %bitcast.50), channel_id=1, replica_groups=mesh['rep'=4,'fsdp'=4,'seq'=2] {'seq'}, dimensions={0} | all-to-all | bytes 1179648 | tf_op jit(solution)/shard_map/all_to_all | solution.py:711
  515.0 1.2 all_gather_reshape.3
  517.7 41.9 %reduce-scatter.7.cloned.1.call-done = bf16[384,768]{1,0:T(8,128)(2,1)} async-done(((bf16[3072,768]{1,0:T(8,128)(2,1)}), bf16[384,768]{1,0:T(8,128)(2,1)}) %reduce-scatter.7.cloned.1.call-update) | async-done | bytes 589840 | tf_op jit(solution)/shard_map/reduce_scatter | solution.py:684
  559.6 2.0 add_convert_fusion
  561.6 23.6 %all-gather.27.cloned.1.call-done = bf16[1536,768]{1,0:T(8,128)(2,1)} async-done(((bf16[384,768]{1,0:T(8,128)(2,1)}), bf16[1536,768]{1,0:T(8,128)(2,1)}) %all-gather.27.cloned.1.call-update) | async-done | bytes 2359312 | tf_op jit(solution)/shard_map/all_gather | solution.py:714
  585.2 4.3 convert
  590.1 52.3 %reduce-scatter.11.cloned.1.call-done = bf16[384,768]{1,0:T(8,128)(2,1)} async-done(((bf16[3072,768]{1,0:T(8,128)(2,1)}), bf16[384,768]{1,0:T(8,128)(2,1)}) %reduce-scatter.11.cloned.1.call-update) | async-done | bytes 589840 | tf_op jit(solution)/shard_map/reduce_scatter | solution.py:726
  644.3 24.4 %all-gather.21.cloned.1.call-done = bf16[4,96,3072]{2,1,0:T(8,128)(2,1)} async-done(((bf16[1,96,3072]{2,1,0:T(8,128)(2,1)}), bf16[4,96,3072]{2,1,0:T(8,128)(2,1)}) %all-gather.21.cloned.1.call-update) | async-done | bytes 2359312 | tf_op jit(solution)/shard_map/all_gather | solution.py:715
  668.7 4.4 convert_element_type.35
  674.3 40.4 %all-reduce.2 = (f32[768]{0:T(1024)}, f32[768]{0:T(1024)}, f32[32,12]{0,1:T(8,128)}, f32[768,4]{0,1:T(4,128)}) all-reduce(f32[768]{0:T(1024)} %get-tuple-element.58, f32[768]{0:T(1024)} %reduce, f32[32,12]{0,1:T(8,128)} %fusion.8, f32[768,4]{0,1:T(4,128)S(1)} %slice_bitcast_fusion), channel_id=1, replica_groups=mesh['rep'=4,'fsdp'=4,'seq'=2] {'rep','fsdp','seq'}, use_global_device_ids=true, to_apply=%region_9.10 | all-reduce | flops 4992 | bytes 39936 | tf_op jit(solution)/shard_map/psum | solution.py:734
  715.3 1.9 fusion.4
  717.3 8.8 %all-gather.2 = bf16[384,768]{1,0:T(8,128)(2,1)S(1)} all-gather(bf16[96,768]{1,0:T(8,128)(2,1)} %reduce-scatter.13.cloned.1.call-done), channel_id=4, replica_groups=mesh['rep'=4,'fsdp'=4,'seq'=2] {'rep'}, dimensions={0}, use_global_device_ids=true | all-gather | bytes 737280 | tf_op jit(solution)/shard_map/all_gather | solution.py:728
  (88 shorter events, 17.9 us)
Async XLA Ops:
  7.2 20.5 %copy-start = (bf16[4,384,768]{2,1,0:T(8,128)(2,1)S(1)}, bf16[4,384,768]{2,1,0:T(8,128)(2,1)}, u32[]{:S(2)}) copy-start(bf16[4,384,768]{2,1,0:T(8,128)(2,1)} %param.24) | copy-start | bytes 7077892
  7.2 62.7 %all-gather.23.cloned.1.call-start = ((), (), s32[]{:S(2)}) async-start(), calls=%async_computation.19 | async-start | bytes 5308416 | tf_op jit(solution)/shard_map/all_gather | solution.py:643
  26.9 67.3 %all-gather.13.cloned.1.call-start = ((), (), s32[]{:S(2)}) async-start(), calls=%async_computation.8 | async-start | bytes 1769472 | tf_op jit(solution)/shard_map/all_gather | solution.py:646
  27.6 119.2 %all-gather.25.cloned.1.call-start = ((), (), s32[]{:S(2)}) async-start(), calls=%async_computation.20 | async-start | bytes 2949120 | tf_op jit(solution)/shard_map/all_gather | solution.py:653
  28.6 169.1 %all-gather.19.cloned.1.call-start = ((), (), s32[]{:S(2)}) async-start(), calls=%async_computation.11 | async-start | bytes 2949120 | tf_op jit(solution)/shard_map/all_gather | solution.py:652
  30.7 15.0 %copy-start.9 = (f32[768,4]{0,1:T(4,128)S(1)}, f32[768,4]{0,1:T(4,128)}, u32[]{:S(2)}) copy-start(f32[768,4]{0,1:T(4,128)} %param.28) | copy-start | bytes 36868
  44.9 1.7 copy-start.14
  44.9 1.7 copy-start.15
  44.9 3.6 copy-start.12
  45.0 4.4 copy-start.10
  45.0 5.0 copy-start.7
  45.0 5.5 copy-start.16
  45.0 192.1 %all-gather.17.cloned.1.call-start = ((), (), s32[]{:S(2)}) async-start(), calls=%async_computation.10 | async-start | bytes 5308416 | tf_op jit(solution)/shard_map/all_gather | solution.py:654
  45.6 235.5 %all-gather.15.cloned.1.call-start = ((), (), s32[]{:S(2)}) async-start(), calls=%async_computation.9 | async-start | bytes 6193152 | tf_op jit(solution)/shard_map/all_gather | solution.py:679
  124.3 266.1 %reduce-scatter.17.cloned.1.call-start = ((), (), s32[]{:S(2)}) async-start(), calls=%async_computation.18 | async-start | bytes 2949120 | tf_op jit(solution)/shard_map/reduce_scatter | solution.py:708
  342.2 109.0 %reduce-scatter.9.cloned.1.call-start = ((), (), s32[]{:S(2)}) async-start(), calls=%async_computation.13 | async-start | bytes 6193152 | tf_op jit(solution)/shard_map/reduce_scatter | solution.py:683
  343.0 158.8 %reduce-scatter.15.cloned.1.call-start = ((), (), s32[]{:S(2)}) async-start(), calls=%async_computation.16 | async-start | bytes 2949120 | tf_op jit(solution)/shard_map/reduce_scatter | solution.py:709
  343.7 215.9 %reduce-scatter.7.cloned.1.call-start = ((), (), s32[]{:S(2)}) async-start(), calls=%async_computation.12 | async-start | bytes 5308416 | tf_op jit(solution)/shard_map/reduce_scatter | solution.py:684
  344.3 240.9 %all-gather.27.cloned.1.call-start = ((), (), s32[]{:S(2)}) async-start(), calls=%async_computation.21 | async-start | bytes 2949120 | tf_op jit(solution)/shard_map/all_gather | solution.py:714
  390.4 252.0 %reduce-scatter.11.cloned.1.call-start = ((), (), s32[]{:S(2)}) async-start(), calls=%async_computation.14 | async-start | bytes 5308416 | tf_op jit(solution)/shard_map/reduce_scatter | solution.py:726
  498.0 170.7 %all-gather.21.cloned.1.call-start = ((), (), s32[]{:S(2)}) async-start(), calls=%async_computation.17 | async-start | bytes 2949120 | tf_op jit(solution)/shard_map/all_gather | solution.py:715
  514.9 1.6 copy-start.2
  515.0 2.4 copy-start.13
  515.0 44.6 %copy-start.5 = (f32[384,768]{1,0:T(8,128)S(1)}, f32[384,768]{1,0:T(8,128)}, u32[]{:S(2)}) copy-start(f32[384,768]{1,0:T(8,128)} %get-tuple-element.35.x_mid_ref) | copy-start | bytes 3538948
  516.2 201.0 %reduce-scatter.13.cloned.1.call-start = ((), (), s32[]{:S(2)}) async-start(), calls=%async_computation.15 | async-start | bytes 737280 | tf_op jit(solution)/shard_map/reduce_scatter | solution.py:727
  517.4 44.2 %copy-start.6 = (f32[6,2,1536]{2,1,0:T(2,128)S(1)}, f32[6,2,1536]{2,1,0:T(2,128)}, u32[]{:S(2)}) copy-start(f32[6,2,1536]{2,1,0:T(2,128)} %get-tuple-element.56) | copy-start | bytes 221188
  517.4 155.8 %collective-permute-start = (bf16[384,768]{1,0:T(8,128)(2,1)S(1)}, bf16[384,768]{1,0:T(8,128)(2,1)S(1)}, u32[]{:S(2)}, u32[]{:S(2)}) collective-permute-start(bf16[384,768]{1,0:T(8,128)(2,1)S(1)} %copy-done.13), channel_id=1, source_target_pairs={{0,1},{1,0},{2,3},{3,2},{4,5},{5,4},{6,7},{7,6},{8,9},{9,8},{10,11... | collective-permute-start | bytes 1769480 | tf_op jit(solution)/shard_map/ppermute | solution.py:718
  585.2 4.3 copy-start.11
  644.3 28.9 %copy-start.3 = (f32[384,768]{1,0:T(8,128)S(1)}, f32[384,768]{1,0:T(8,128)}, u32[]{:S(2)}) copy-start(f32[384,768]{1,0:T(8,128)} %get-tuple-element.47) | copy-start | bytes 3538948
  668.7 4.4 copy-start.8
  673.2 42.1 %copy-start.4 = (f32[384,768]{1,0:T(8,128)S(1)}, f32[384,768]{1,0:T(8,128)}, u32[]{:S(2)}) copy-start(f32[384,768]{1,0:T(8,128)} %get-tuple-element.46) | copy-start | bytes 3538948
  717.3 9.9 %copy-start.1 = (bf16[4,384,768]{2,1,0:T(8,128)(2,1)S(1)}, bf16[4,384,768]{2,1,0:T(8,128)(2,1)}, u32[]{:S(2)}) copy-start(bf16[4,384,768]{2,1,0:T(8,128)(2,1)} %param.24) | copy-start | bytes 7077892
Sparse Core Ops, SparseCore 0:
  27.0 42.8 all-gather.22
  71.4 22.7 all-gather.12
  96.4 50.4 all-gather.24
  148.3 49.2 all-gather.18
  199.4 37.7 all-gather.16
  238.9 42.2 all-gather.14
  342.3 48.0 reduce-scatter.16
  393.9 57.3 reduce-scatter.8
  453.6 48.0 reduce-scatter.14
  506.0 53.5 reduce-scatter.6
  561.1 24.0 all-gather.26
  588.5 53.8 reduce-scatter.10
  644.6 24.0 all-gather.20
  671.0 21.9 reduce-scatter.12

commit v2 on v1

--- a/solution.py
+++ b/solution.py
@@ -54,13 +54,17 @@
     return grad_values, grad_gain
 
 
+def first_row(rows):
+    return lax.axis_index("seq") * rows
+
+
 def make_mask(place_ref, mask_ref):
     shape = mask_ref.shape
-    pos_q = place_ref[0] + lax.broadcasted_iota(jnp.int32, shape, 0)
+    pos_q = first_row(shape[0]) + lax.broadcasted_iota(jnp.int32, shape, 0)
     pos_k = lax.broadcasted_iota(jnp.int32, shape, 1)
     allowed = pos_k <= pos_q
     for piece in range(2):
-        start = place_ref[1 + piece]
+        start = place_ref[piece]
         in_q = (pos_q >= start) & (pos_q < start + PIECE)
         in_k = (pos_k >= start) & (pos_k < start + PIECE)
         allowed = allowed | (in_q & in_k)
@@ -87,7 +91,309 @@
     return (lane == routes_ref[:, 0:1]) | (lane == routes_ref[:, 1:2])
 
 
+MESH = pl.DeviceIdType.MESH
+
+
+class Place:
+    def __init__(self, n_fsdp):
+        self.rep = lax.axis_index("rep")
+        self.line = lax.axis_index("fsdp")
+        self.seq = lax.axis_index("seq")
+        self.n_fsdp = n_fsdp
+        self.row = self.rep // 2
+        self.core = self.rep % 2
+
+    def mate(self):
+        return (self.row * 2 + 1 - self.core, self.line, self.seq)
+
+    def chip(self, rows, columns, core=None):
+        core = self.core if core is None else core
+        row = (self.row + rows) % 2
+        return (row * 2 + core, self.line, (self.seq + columns) % 2)
+
+    def along(self, steps):
+        return (self.rep, (self.line + steps) % self.n_fsdp, self.seq)
+
+
+def meet(partners):
+    barrier = pltpu.get_barrier_semaphore()
+    for partner in partners:
+        pl.semaphore_signal(barrier, inc=1, device_id=partner, device_id_type=MESH)
+    pl.semaphore_wait(barrier, len(partners))
+
+
+class Wires:
+    def __init__(self, send, recv):
+        self.send, self.recv = send, recv
+        self.names = {}
+
+    def copy(self, name, source, target, device):
+        index = self.names.setdefault(name, len(self.names))
+        return pltpu.make_async_remote_copy(
+            src_ref=source,
+            dst_ref=target,
+            send_sem=self.send.at[index],
+            recv_sem=self.recv.at[index],
+            device_id=device,
+            device_id_type=MESH,
+        )
+
+
+class Planned:
+    def __init__(self, plan, send, recv):
+        self.plan, self.send, self.recv = plan, send, recv
+        self.order = list(plan)
+
+    def __getitem__(self, name):
+        source, target, device = self.plan[name]
+        index = self.order.index(name)
+        return pltpu.make_async_remote_copy(
+            src_ref=source,
+            dst_ref=target,
+            send_sem=self.send.at[index],
+            recv_sem=self.recv.at[index],
+            device_id=device,
+            device_id_type=MESH,
+        )
+
+
+def gather_kernel(
+    n_fsdp,
+    attn_q,
+    attn_k,
+    attn_v,
+    attn_o,
+    tokens,
+    expert_in,
+    expert_out,
+    weights,
+    x_all,
+    in_pair,
+    w_out,
+    send,
+    recv,
+    local,
+):
+    me = Place(n_fsdp)
+    rep, line, seq = me.rep, me.line, me.seq
+    far_row = (me.row + 1) % 2 * 2 + me.core
+    mate, across, beside = me.mate(), me.chip(1, 0), me.chip(0, 1)
+    part_out = expert_out.shape[1]
+    wires = Wires(send, recv)
+    meet([mate, across, beside, me.along(1), me.along(-1), me.along(2)])
+    started = []
+
+    def start(copy):
+        copy.start()
+        started.append(copy)
+        return copy
+
+    for i, matrix in enumerate((attn_q, attn_k, attn_v, attn_o)):
+
+        @pl.when(rep == i)
+        def _():
+            own = pltpu.make_async_copy(matrix, weights.at[i, line, seq], local.at[n_fsdp])
+            own.start()
+            own.wait()
+
+    mine = lambda z, r=rep, x=seq: weights.at[r, z, x]
+    shifts = (0, 1, -1, 2)
+    at = {0: line}
+    z_copies = {}
+    for shift in shifts[1:]:
+        at[shift] = (line - shift) % n_fsdp
+        z_copies[shift] = start(
+            wires.copy(("z", shift), mine(line), mine(line), me.along(shift))
+        )
+    x_copies, y_copies, c_copies, far_copies = {}, {}, [], {}
+
+    def spread_out(shift):
+        z = at[shift]
+        x_copies[shift] = start(wires.copy(("x", shift), mine(z), mine(z), beside))
+        y_copies[shift] = start(wires.copy(("y", shift), mine(z), mine(z), across))
+        c_copies.append(start(wires.copy(("c", shift), mine(z), mine(z), mate)))
+
+    spread_out(0)
+    x_own = pltpu.make_async_copy(tokens, x_all.at[seq], local.at[n_fsdp + 2])
+    x_own.start()
+    for shift in shifts[1:]:
+        z_copies[shift].wait_recv()
+        spread_out(shift)
+    columns = lambda z, x: pl.ds(pl.multiple_of((z * 2 + x) * part_out, LANES), part_out)
+    in_x, in_own = [], []
+    for z in range(n_fsdp):
+        here = pl.ds(z * part_out, part_out)
+        copy = wires.copy(
+            ("in", z),
+            expert_in.at[rep, :, columns(z, 1 - seq)],
+            in_pair.at[seq, :, here],
+            beside,
+        )
+        in_x.append(start(copy))
+        copy = pltpu.make_async_copy(
+            expert_in.at[rep, :, columns(z, seq)], in_pair.at[seq, :, here], local.at[z]
+        )
+        copy.start()
+        in_own.append(copy)
+    out_own = pltpu.make_async_copy(expert_out.at[rep], w_out.at[line], local.at[n_fsdp + 1])
+    out_own.start()
+    out_copies = {}
+    for shift in (1, -1):
+        out_copies[shift] = start(
+            wires.copy(("out", shift), expert_out.at[rep], w_out.at[line], me.along(shift))
+        )
+    token_copy = start(wires.copy("tokens", tokens, x_all.at[seq], beside))
+    for shift in shifts:
+        z = at[shift]
+        x_copies[shift].wait_recv()
+        near = mine(z, rep, 1 - seq)
+        far_copies[shift] = start(wires.copy(("far", shift), near, near, across))
+        c_copies.append(start(wires.copy(("cx", shift), near, near, mate)))
+    for shift in shifts:
+        z = at[shift]
+        y_copies[shift].wait_recv()
+        there = mine(z, far_row, seq)
+        c_copies.append(start(wires.copy(("cy", shift), there, there, mate)))
+    for shift in shifts:
+        z = at[shift]
+        far_copies[shift].wait_recv()
+        there = mine(z, far_row, 1 - seq)
+        c_copies.append(start(wires.copy(("cf", shift), there, there, mate)))
+    half = part_out // 2
+    relays = []
+    for shift, rows in ((1, pl.ds(0, half)), (-1, pl.ds(half, half))):
+        out_copies[shift].wait_recv()
+        piece = w_out.at[(line - shift) % n_fsdp, rows]
+        relays.append(start(wires.copy(("relay", shift), piece, piece, me.along(shift))))
+    for copy in c_copies + relays + in_x + [token_copy]:
+        copy.wait_recv()
+    for copy in in_own + [out_own, x_own]:
+        copy.wait()
+    for copy in started:
+        copy.wait_send()
+
+
+def gather(attn, tokens, expert_in, expert_out, n_fsdp):
+    part_attn, width = attn[0].shape
+    n_rows = tokens.shape[0]
+    n_experts, part_in, hidden = expert_in.shape
+    part_out = expert_out.shape[1]
+    anywhere = pl.BlockSpec(memory_space=pl.ANY)
+    weights, x_all, in_pair, w_out = pl.pallas_call(
+        functools.partial(gather_kernel, n_fsdp),
+        out_shape=[
+            jax.ShapeDtypeStruct((4, n_fsdp, 2, part_attn, width), bf16),
+            jax.ShapeDtypeStruct((2, n_rows, width), bf16),
+            jax.ShapeDtypeStruct((2, part_in, n_fsdp * part_out), bf16),
+            jax.ShapeDtypeStruct((n_fsdp, part_out, width), bf16),
+        ],
+        in_specs=[anywhere] * 7,
+        out_specs=[anywhere] * 4,
+        scratch_shapes=[
+            pltpu.SemaphoreType.DMA((48,)),
+            pltpu.SemaphoreType.DMA((48,)),
+            pltpu.SemaphoreType.DMA((8,)),
+        ],
+        compiler_params=pltpu.CompilerParams(collective_id=0, has_side_effects=True),
+        name="gather_weights",
+    )(*attn, tokens, expert_in, expert_out)
+    return (
+        weights.reshape(4, n_fsdp * 2 * part_attn, width),
+        x_all.reshape(2 * n_rows, width),
+        in_pair.reshape(2 * part_in, n_fsdp * part_out),
+        w_out.reshape(n_fsdp * part_out, width),
+    )
+
+
+class Background:
+    n_in, n_out = 2, 2
+
+    def __init__(self, n_fsdp):
+        self.n_fsdp = n_fsdp
+
+    def out_shape(self, n_rows, width, pair_rows, columns):
+        return [
+            jax.ShapeDtypeStruct((8, n_rows, width), bf16),
+            jax.ShapeDtypeStruct((self.n_fsdp, pair_rows, columns), bf16),
+        ]
+
+    scratch = (
+        pltpu.SemaphoreType.DMA((16,)),
+        pltpu.SemaphoreType.DMA((16,)),
+        pltpu.SemaphoreType.DMA((2,)),
+    )
+
+    def run(self, step, before, ins, outs, scratch):
+        dy, in_pair = ins
+        dy_all, w_in = outs
+        send, recv, local = scratch
+        me = Place(self.n_fsdp)
+        n_rows = dy.shape[0]
+        half = n_rows // 2
+        first, second = pl.ds(0, half), pl.ds(half, half)
+        core = me.core
+        own = 7 * (1 - core)
+        mate, across, beside = me.mate(), me.chip(1, 0), me.chip(0, 1)
+        slot = dy_all.at
+        rows = w_in.shape[1] // 2
+        parts = {1: pl.ds(0, rows), -1: pl.ds(rows, rows)}
+        passed = {s: w_in.at[(me.line - s) % self.n_fsdp, parts[s]] for s in (1, -1)}
+        plan = {
+            "x": (dy, slot[1 + core], beside),
+            "y": (dy, slot[3 + core], across),
+            "c0": (dy, slot[own], mate),
+            "c1": (slot[1 + core], slot[1 + core], mate),
+            "c2": (slot[3 + core], slot[3 + core], mate),
+            "c3": (slot[5 + core], slot[5 + core], mate),
+            "xy": (slot[1 + core, first], slot[5 + core, first], across),
+            "yx": (slot[3 + core, second], slot[5 + core, second], beside),
+            ("z", 1): (in_pair, w_in.at[me.line], me.along(1)),
+            ("z", -1): (in_pair, w_in.at[me.line], me.along(-1)),
+            ("relay", 1): (passed[1], passed[1], me.along(1)),
+            ("relay", -1): (passed[-1], passed[-1], me.along(-1)),
+        }
+        copies = Planned(plan, send, recv)
+        if before:
+
+            @pl.when(step == 0)
+            def _():
+                meet([mate, across, beside, me.along(1), me.along(-1)])
+                for name in (("z", 1), ("z", -1), "x", "y", "c0"):
+                    copies[name].start()
+                pltpu.make_async_copy(dy, slot[own], local.at[0]).start()
+                pltpu.make_async_copy(in_pair, w_in.at[me.line], local.at[1]).start()
+
+            @pl.when(step == 3)
+            def _():
+                copies["x"].wait_recv()
+                copies["xy"].start()
+                copies["c1"].start()
+                copies["y"].wait_recv()
+                copies["yx"].start()
+                copies["c2"].start()
+                for shift in (1, -1):
+                    copies["z", shift].wait_recv()
+                    copies["relay", shift].start()
+
+            return
+
+        @pl.when(step == pl.num_programs(0) - 1)
+        def _():
+            copies["xy"].wait_recv()
+            copies["yx"].wait_recv()
+            copies["c3"].start()
+            for shift in (1, -1):
+                copies["relay", shift].wait_recv()
+            for name in ("c0", "c1", "c2", "c3"):
+                copies[name].wait_recv()
+            pltpu.make_async_copy(dy, slot[own], local.at[0]).wait()
+            pltpu.make_async_copy(in_pair, w_in.at[me.line], local.at[1]).wait()
+            for name in plan:
+                copies[name].wait_send()
+
+
 def forward_kernel(
+    background,
     n_experts,
     head_dim,
     place_ref,
@@ -101,23 +407,19 @@
     dist_ref,
     routes_ref,
     router_ref,
-    q_out,
-    k_out,
-    v_out,
-    o_out,
-    lse_out,
-    x_mid_out,
-    message_out,
-    probs_out,
-    h_out,
-    total_ref,
-    mask_ref,
-    bias_ref,
+    *refs,
 ):
     step = pl.program_id(0)
+    n_in, n_out = (background.n_in, background.n_out) if background else (0, 0)
+    behind_in, refs = refs[:n_in], refs[n_in:]
+    q_out, k_out, v_out, o_out, lse_out, x_mid_out, message_out, probs_out, h_out = refs[:9]
+    behind_out, refs = refs[9 : 9 + n_out], refs[9 + n_out :]
+    total_ref, mask_ref, bias_ref = refs[:3]
+    if background:
+        background.run(step, True, behind_in, behind_out, refs[3:])
     rows = x_mid_out.shape[0]
     length, width = x_ref.shape
-    own = pl.ds(pl.multiple_of(place_ref[0], rows), rows)
+    own = pl.ds(pl.multiple_of(first_row(rows), rows), rows)
 
     @pl.when(step == 0)
     def _():
@@ -140,7 +442,7 @@
         bias_ref[head] = spread(dist_ref[0, head : head + 1, :], block, span)
     for b in range(rows // block):
         here = slice(b * block, (b + 1) * block)
-        offset = pl.multiple_of(length - LANES - block * b - place_ref[0], LANES)
+        offset = pl.multiple_of(length - LANES - block * b - first_row(rows), LANES)
         halves = []
         tops = []
         for head in range(2):
@@ -176,9 +478,24 @@
         low = gate - high.astype(f32)
         message_out[:, width:] = (high.astype(f32) + pltpu.roll(low, n_experts, 1)).astype(bf16)
 
+    if background:
+        background.run(step, False, behind_in, behind_out, refs[3:])
+
 
 def attention_forward(
-    place, x_all, gain_one, gain_two, weights, dist, routes, router, n_rows, n_experts, head_dim
+    place,
+    x_all,
+    gain_one,
+    gain_two,
+    weights,
+    dist,
+    routes,
+    router,
+    n_rows,
+    n_experts,
+    head_dim,
+    background=None,
+    behind=(),
 ):
     length, width = x_all.shape
     pairs = width // LANES
@@ -197,8 +514,13 @@
         jax.ShapeDtypeStruct((n_rows, LANES), f32),
         jax.ShapeDtypeStruct((length, width), bf16),
     ]
+    anywhere = pl.BlockSpec(memory_space=pl.ANY)
+    params = {}
+    if background:
+        out_shape += background.out_shape(n_rows, width, *behind[1].shape)
+        params = {"collective_id": 1, "has_side_effects": True}
     return pl.pallas_call(
-        functools.partial(forward_kernel, n_experts, head_dim),
+        functools.partial(forward_kernel, background, n_experts, head_dim),
         out_shape=out_shape,
         grid_spec=pltpu.PrefetchScalarGridSpec(
             num_scalar_prefetch=1,
@@ -214,7 +536,8 @@
                 pl.BlockSpec((1, 2, span), lambda p, *_: (p, 0, 0)),
                 whole((n_rows, 2)),
                 whole((width, LANES)),
-            ],
+            ]
+            + [anywhere] * len(behind),
             out_specs=[
                 columns(n_rows),
                 columns(length),
@@ -225,19 +548,34 @@
                 whole((n_rows, width + LANES)),
                 whole((n_rows, LANES)),
                 whole((length, width)),
-            ],
+            ]
+            + [anywhere] * (background.n_out if background else 0),
             scratch_shapes=[
                 pltpu.VMEM((n_rows, width), f32),
                 pltpu.VMEM((n_rows, length), f32),
                 pltpu.VMEM((2, LANES, span), f32),
-            ],
+            ]
+            + list(background.scratch if background else ()),
         ),
-        compiler_params=pltpu.CompilerParams(vmem_limit_bytes=VMEM_LIMIT),
+        compiler_params=pltpu.CompilerParams(vmem_limit_bytes=VMEM_LIMIT, **params),
         cost_estimate=pl.CostEstimate(
             flops=20_000_000_000, transcendentals=0, bytes_accessed=20_000_000
         ),
         name="attention_forward",
-    )(place, x_all, gain_one, gain_two, weights, weights, weights, weights, dist, routes, router)
+    )(
+        place,
+        x_all,
+        gain_one,
+        gain_two,
+        weights,
+        weights,
+        weights,
+        weights,
+        dist,
+        routes,
+        router,
+        *behind,
+    )
 
 
 GELU_A = 0.7978845608028654
@@ -353,7 +691,477 @@
     )(expert, message, dy, w_in, w_out)
 
 
+def plane_slot(j):
+    return (j + 1) // 2 % 4, (j + 1) % 2
+
+
+def plane_experts_kernel(
+    n_experts,
+    chunk,
+    n_fsdp,
+    message_ref,
+    dy_ref,
+    w_in_ref,
+    w_out_ref,
+    back_ref,
+    out_half,
+    dw_in_ref,
+    dw_out_ref,
+    h_ref,
+    part_ref,
+    tx_ref,
+    rx_ref,
+    fin_ref,
+    fin_out_ref,
+    land_ref,
+    dw_in_acc,
+    dw_out_acc,
+    send,
+    recv,
+    tx_sem,
+    rx_sem,
+    fin_sem,
+    land_sem,
+    local,
+):
+    step = pl.program_id(0)
+    last = 7
+    me = Place(n_fsdp)
+    core = me.core
+    rows, width = dy_ref.shape
+    hidden = w_in_ref.shape[1]
+    long = message_ref.shape[1]
+    half = rows // 2
+    first, second = pl.ds(0, half), pl.ds(half, half)
+    mate, across, beside = me.mate(), me.chip(1, 0), me.chip(0, 1)
+    own = 7 * (1 - core)
+    slot = h_ref.at
+    plan = {
+        "x": (message_ref, slot[1 + core], beside),
+        "y": (message_ref, slot[3 + core], across),
+        "c0": (message_ref, slot[own], mate),
+        "c1": (slot[1 + core], slot[1 + core], mate),
+        "c2": (slot[3 + core], slot[3 + core], mate),
+        "c3": (slot[5 + core], slot[5 + core], mate),
+        "xy": (slot[1 + core, first], slot[5 + core, first], across),
+        "yx": (slot[3 + core, second], slot[5 + core, second], beside),
+    }
+    copies = Planned(plan, send, recv)
+
+    def to_mate(j):
+        return pltpu.make_async_remote_copy(
+            src_ref=tx_ref.at[j % 2],
+            dst_ref=rx_ref.at[j],
+            send_sem=tx_sem.at[j],
+            recv_sem=rx_sem.at[j],
+            device_id=mate,
+            device_id_type=MESH,
+        )
+
+    def to_owner(j):
+        q, k = plane_slot(j)
+        return pltpu.make_async_remote_copy(
+            src_ref=fin_ref.at[j % 2],
+            dst_ref=land_ref.at[q, core],
+            send_sem=fin_sem.at[j],
+            recv_sem=land_sem.at[q, core],
+            device_id=me.chip(q // 2, q % 2, k),
+            device_id_type=MESH,
+        )
+
+    def keep_out(j):
+        return pltpu.make_async_copy(fin_out_ref.at[j % 2], out_half.at[j], local.at[j])
+
+    def stays(j):
+        q, k = plane_slot(j)
+        return (q == 0) & (k == core)
+
+    def finish(j):
+        to_mate(j).wait_recv()
+        mine = part_ref.at[j % 2, pl.ds(core * half, half)]
+
+        @pl.when(j >= 2)
+        def _():
+            keep_out(j - 2).wait()
+
+        @pl.when((j >= 2) & ~stays(j - 2))
+        def _():
+            to_owner(j - 2).wait_send()
+
+        fin_out_ref[j % 2] = (mine[:, long:] + rx_ref[j, :, long:].astype(f32)).astype(bf16)
+        keep_out(j).start()
+        fin_ref[j % 2] = (mine[:, :long] + rx_ref[j, :, :long].astype(f32)).astype(bf16)
+
+        @pl.when(stays(j))
+        def _():
+            land_ref[0, core] = fin_ref[j % 2]
+
+        @pl.when(~stays(j))
+        def _():
+            to_owner(j).start()
+
+    @pl.when(step == 0)
+    def _():
+        meet([mate, across, beside, me.chip(1, 1), me.chip(1, 0, 1 - core), me.chip(0, 1, 1 - core), me.chip(1, 1, 1 - core)])
+        copies["x"].start()
+        copies["y"].start()
+        copies["c0"].start()
+        h_ref[own] = message_ref[...]
+        dw_in_acc[...] = jnp.zeros_like(dw_in_acc)
+        dw_out_acc[...] = jnp.zeros_like(dw_out_acc)
+        copies["c0"].wait_recv()
+
+    @pl.when(step == 1)
+    def _():
+        copies["x"].wait_recv()
+        copies["c1"].start()
+        copies["xy"].start()
+
+    @pl.when(step == 2)
+    def _():
+        copies["y"].wait_recv()
+        copies["c2"].start()
+        copies["yx"].start()
+
+    @pl.when(step == 4)
+    def _():
+        copies["xy"].wait_recv()
+        copies["yx"].wait_recv()
+        copies["c3"].start()
+
+    for q in (1, 2, 3):
+
+        @pl.when(step == 2 * q - core)
+        def _():
+            copies[f"c{q}"].wait_recv()
+
+    expert = me.rep
+    h = h_ref[step, :, :width]
+    extra = h_ref[step, :, width:].astype(f32)
+    lane = lax.broadcasted_iota(jnp.int32, extra.shape, 1)
+    mine = (lane == expert) | (lane == expert + n_experts)
+    gate = jnp.sum(jnp.where(mine, extra, 0.0), -1, keepdims=True)
+    dy = dy_ref[...]
+    dgate = None
+    part = part_ref.at[step % 2]
+    for start in range(0, hidden, chunk):
+        piece = slice(start, start + chunk)
+        up = dot(h, w_in_ref[:, piece])
+        dact = dot_t(dy, w_out_ref[piece, :])
+        square = up * up
+        tanh = jnp.tanh(up * (GELU_A + GELU_B * square))
+        halved = 0.5 * up
+        more = 1.0 + tanh
+        act = halved * more
+        slope = 0.5 * more + halved * (1.0 - tanh * tanh) * (GELU_A + 3.0 * GELU_B * square)
+        gated = (gate * act).astype(bf16)
+        dgate_part = jnp.sum(act * dact, -1, keepdims=True)
+        dup = (gate * dact * slope).astype(bf16)
+        out_part = dot(gated, w_out_ref[piece, :])
+        dh_part = dot_t(dup, w_in_ref[:, piece])
+        if start == 0:
+            part[:, long:] = out_part
+            part[:, :width] = dh_part
+        else:
+            part[:, long:] += out_part
+            part[:, :width] += dh_part
+        dgate = dgate_part if dgate is None else dgate + dgate_part
+        dw_out_acc[piece, :] += t_dot(gated, dy)
+        dw_in_acc[:, piece] += t_dot(h, dup)
+        if start == 0:
+
+            @pl.when(step >= 1)
+            def _():
+                finish(step - 1)
+
+    high = dgate.astype(bf16).astype(f32)
+    low = dgate - high
+    part[:, width:long] = jnp.where(
+        lane == expert, high, jnp.where(lane == expert + n_experts, low, 0.0)
+    )
+
+    @pl.when(step >= 2)
+    def _():
+        to_mate(step - 2).wait_send()
+
+    tx_ref[step % 2] = part_ref[step % 2, pl.ds((1 - core) * half, half)].astype(bf16)
+    to_mate(step).start()
+
+    @pl.when(step == last)
+    def _():
+        dw_in_ref[...] = dw_in_acc[...].astype(bf16)
+        dw_out_ref[...] = dw_out_acc[...].astype(bf16)
+        finish(last)
+        to_mate(last - 1).wait_send()
+        to_mate(last).wait_send()
+        keep_out(last - 1).wait()
+        keep_out(last).wait()
+        to_owner(last - 1).wait_send()
+
+        @pl.when(~stays(last))
+        def _():
+            to_owner(last).wait_send()
+
+        for name in plan:
+            copies[name].wait_send()
+        for side in range(2):
+            total = None
+            for q in range(4):
+                arrived = pltpu.make_async_remote_copy(
+                    src_ref=fin_ref.at[0],
+                    dst_ref=land_ref.at[q, side],
+                    send_sem=fin_sem.at[0],
+                    recv_sem=land_sem.at[q, side],
+                    device_id=mate,
+                    device_id_type=MESH,
+                )
+                if q == 0:
+
+                    @pl.when(core != side)
+                    def _():
+                        arrived.wait_recv()
+
+                else:
+                    arrived.wait_recv()
+                landed = land_ref[q, side].astype(f32)
+                total = landed if total is None else total + landed
+            back_ref[side * half : (side + 1) * half, :] = total
+
+
+def plane_experts(message, dy_all, w_in, w_out, n_experts, n_fsdp):
+    blocks, rows, width = dy_all.shape
+    long = message.shape[1]
+    hidden = w_in.shape[1]
+    half = rows // 2
+    once = pl.Buffered(1)
+    whole = lambda shape: pl.BlockSpec(shape, lambda i: (0,) * len(shape), pipeline_mode=once)
+    both = long + width
+    dma = lambda *shape: pltpu.SemaphoreType.DMA(shape)
+    return pl.pallas_call(
+        functools.partial(plane_experts_kernel, n_experts, 512, n_fsdp),
+        out_shape=[
+            jax.ShapeDtypeStruct((rows, long), f32),
+            jax.ShapeDtypeStruct((blocks, half, width), bf16),
+            jax.ShapeDtypeStruct((width, hidden), bf16),
+            jax.ShapeDtypeStruct((hidden, width), bf16),
+        ],
+        grid=(blocks,),
+        in_specs=[
+            whole((rows, long)),
+            pl.BlockSpec((None, rows, width), lambda i: (i, 0, 0)),
+            whole((width, hidden)),
+            whole((hidden, width)),
+        ],
+        out_specs=[
+            whole((rows, long)),
+            pl.BlockSpec(memory_space=pl.ANY),
+            whole((width, hidden)),
+            whole((hidden, width)),
+        ],
+        scratch_shapes=[
+            pltpu.VMEM((blocks, rows, long), bf16),
+            pltpu.VMEM((2, rows, both), f32),
+            pltpu.VMEM((2, half, both), bf16),
+            pltpu.VMEM((blocks, half, both), bf16),
+            pltpu.VMEM((2, half, long), bf16),
+            pltpu.VMEM((2, half, width), bf16),
+            pltpu.VMEM((4, 2, half, long), bf16),
+            pltpu.VMEM((width, hidden), f32),
+            pltpu.VMEM((hidden, width), f32),
+            dma(8),
+            dma(8),
+            dma(8),
+            dma(8),
+            dma(8),
+            dma(4, 2),
+            dma(8),
+        ],
+        compiler_params=pltpu.CompilerParams(
+            vmem_limit_bytes=VMEM_LIMIT, collective_id=2, has_side_effects=True
+        ),
+        cost_estimate=pl.CostEstimate(
+            flops=60_000_000_000, transcendentals=0, bytes_accessed=30_000_000
+        ),
+        name="plane_experts",
+    )(message, dy_all, w_in, w_out)
+
+
+class LineSum:
+    def __init__(self, me, whole, near, mid, far, mine, send, recv, local):
+        self.me, self.whole, self.near, self.mid, self.far = me, whole, near, mid, far
+        self.mine, self.local = mine, local
+        rows = whole.shape[1]
+        half = rows // 2
+        self.parts = {1: slice(0, half), -1: slice(half, rows)}
+        plan = {}
+        for i, shift in enumerate((1, -1)):
+            part = pl.ds(i * half, half)
+            target = (me.line + 2) % me.n_fsdp
+            plan["near", shift] = (whole.at[target, part], near.at[i], me.along(shift))
+            plan["far", shift] = (mid.at[i], far.at[i], me.along(shift))
+        self.copies = Planned(plan, send, recv)
+
+    def loads(self):
+        me = self.me
+        for i, shift in enumerate((1, -1)):
+            source = self.whole.at[(me.line + shift) % me.n_fsdp]
+            yield pltpu.make_async_copy(source, self.mid.at[i], self.local.at[i])
+        yield pltpu.make_async_copy(self.whole.at[me.line], self.mine, self.local.at[2])
+
+    def start(self):
+        for shift in (1, -1):
+            self.copies["near", shift].start()
+        for load in self.loads():
+            load.start()
+
+    def turn(self):
+        for load in self.loads():
+            load.wait()
+        for i, shift in enumerate((1, -1)):
+            self.copies["near", shift].wait_recv()
+            part = self.parts[shift]
+            total = self.mid[i, part, :].astype(f32) + self.near[i].astype(f32)
+            self.mid[i, part, :] = total.astype(bf16)
+            self.copies["far", shift].start()
+
+    def total(self):
+        for shift in (1, -1):
+            self.copies["far", shift].wait_recv()
+        total = self.mine[...].astype(f32) + self.far[0].astype(f32) + self.far[1].astype(f32)
+        for shift in (1, -1):
+            self.copies["near", shift].wait_send()
+            self.copies["far", shift].wait_send()
+        return total.astype(bf16)
+
+    @staticmethod
+    def scratch(rows, columns):
+        return [
+            pltpu.VMEM((2, rows // 2, columns), bf16),
+            pltpu.VMEM((2, rows, columns), bf16),
+            pltpu.VMEM((2, rows, columns), bf16),
+            pltpu.VMEM((rows, columns), bf16),
+            pltpu.SemaphoreType.DMA((4,)),
+            pltpu.SemaphoreType.DMA((4,)),
+            pltpu.SemaphoreType.DMA((3,)),
+        ]
+
+
+class BackgroundBack:
+    n_in, n_out = 3, 2
+
+    def __init__(self, n_fsdp):
+        self.n_fsdp = n_fsdp
+
+    def out_shape(self, out_half, dw_out, x_mid):
+        return [
+            jax.ShapeDtypeStruct(x_mid.shape, bf16),
+            jax.ShapeDtypeStruct(dw_out.shape[1:], bf16),
+        ]
+
+    def scratch(self, out_half, dw_out, x_mid):
+        half, width = out_half.shape[1:]
+        return [
+            pltpu.VMEM((4, 2, half, width), bf16),
+            pltpu.SemaphoreType.DMA((8,)),
+            pltpu.SemaphoreType.DMA((4, 2)),
+        ] + LineSum.scratch(*dw_out.shape[1:])
+
+    def run(self, step, before, ins, outs, scratch, x_mid):
+        out_half, dw_out, _ = ins
+        out_rows, sum_out = outs
+        land, send, recv = scratch[:3]
+        near, mid, far, mine, line_send, line_recv, line_local = scratch[3:]
+        me = Place(self.n_fsdp)
+        core = me.core
+        half = out_half.shape[1]
+        line = LineSum(me, dw_out, near, mid, far, mine, line_send, line_recv, line_local)
+
+        def to_owner(j):
+            q, k = plane_slot(j)
+            return pltpu.make_async_remote_copy(
+                src_ref=out_half.at[j],
+                dst_ref=land.at[q, core],
+                send_sem=send.at[j],
+                recv_sem=recv.at[q, core],
+                device_id=me.chip(q // 2, q % 2, k),
+                device_id_type=MESH,
+            )
+
+        def stay(j):
+            return pltpu.make_async_copy(out_half.at[j], land.at[0, core], send.at[j])
+
+        if before:
+
+            @pl.when(step == 0)
+            def _():
+                partners = [me.mate(), me.along(1), me.along(-1)]
+                for q in (1, 2, 3):
+                    for k in (0, 1):
+                        partners.append(me.chip(q // 2, q % 2, (core + k) % 2))
+                meet(partners)
+                line.start()
+                for j in range(8):
+                    if j in (0, 7):
+
+                        @pl.when(core == (j + 1) % 2)
+                        def _():
+                            stay(j).start()
+
+                        @pl.when(core != (j + 1) % 2)
+                        def _():
+                            to_owner(j).start()
+
+                    else:
+                        to_owner(j).start()
+
+            @pl.when(step == 2)
+            def _():
+                line.turn()
+
+            return
+
+        @pl.when(step == pl.num_programs(0) - 1)
+        def _():
+            for j in range(8):
+                if j in (0, 7):
+
+                    @pl.when(core == (j + 1) % 2)
+                    def _():
+                        stay(j).wait()
+
+                    @pl.when(core != (j + 1) % 2)
+                    def _():
+                        to_owner(j).wait_send()
+
+                else:
+                    to_owner(j).wait_send()
+            for side in range(2):
+                here = slice(side * half, (side + 1) * half)
+                total = x_mid[here, :]
+                for q in range(4):
+                    arrived = pltpu.make_async_remote_copy(
+                        src_ref=out_half.at[0],
+                        dst_ref=land.at[q, side],
+                        send_sem=send.at[0],
+                        recv_sem=recv.at[q, side],
+                        device_id=me.mate(),
+                        device_id_type=MESH,
+                    )
+                    if q == 0:
+
+                        @pl.when(core != side)
+                        def _():
+                            arrived.wait_recv()
+
+                    else:
+                        arrived.wait_recv()
+                    total = total + land[q, side].astype(f32)
+                out_rows[here, :] = total.astype(bf16)
+            sum_out[...] = line.total()
+
+
 def backward_kernel(
+    background,
     n_experts,
     head_dim,
     place_ref,
@@ -376,28 +1184,20 @@
     o_ref,
     lse_ref,
     dist_ref,
-    dwq_out,
-    dwk_out,
-    dwv_out,
-    dwo_out,
-    dh_own_out,
-    dh_other_out,
-    dx_mid_out,
-    gain_out,
-    router_out,
-    ddist_out,
-    da_ref,
-    dh_all_ref,
-    dh_mine_ref,
-    mask_ref,
-    bias_ref,
-    dbias_ref,
-    dq_ref,
+    *refs,
 ):
     step = pl.program_id(0)
+    n_in, n_out = (background.n_in, background.n_out) if background else (0, 0)
+    behind_in, refs = refs[:n_in], refs[n_in:]
+    dwq_out, dwk_out, dwv_out, dwo_out, dh_own_out, dh_other_out = refs[:6]
+    dx_mid_out, gain_out, router_out, ddist_out = refs[6:10]
+    behind_out, refs = refs[10 : 10 + n_out], refs[10 + n_out :]
+    da_ref, dh_all_ref, dh_mine_ref, mask_ref, bias_ref, dbias_ref, dq_ref = refs[:7]
+    if background:
+        background.run(step, True, behind_in, behind_out, refs[7:], x_mid_ref)
     rows, width = x_mid_ref.shape
     length = h_ref.shape[0]
-    own = pl.ds(pl.multiple_of(place_ref[0], rows), rows)
+    own = pl.ds(pl.multiple_of(first_row(rows), rows), rows)
 
     @pl.when(step == 0)
     def _():
@@ -446,7 +1246,7 @@
         dbias_ref[head] = jnp.zeros_like(dbias_ref[head])
     for b in range(rows // block):
         here = slice(b * block, (b + 1) * block)
-        offset = pl.multiple_of(length - LANES - block * b - place_ref[0], LANES)
+        offset = pl.multiple_of(length - LANES - block * b - first_row(rows), LANES)
         halves = []
         for head in range(2):
             mine = first_half if head == 0 else ~first_half
@@ -483,9 +1283,12 @@
 
     @pl.when(step == pl.num_programs(0) - 1)
     def _():
-        other = pl.ds(pl.multiple_of(length - rows - place_ref[0], rows), rows)
+        other = pl.ds(pl.multiple_of(length - rows - first_row(rows), rows), rows)
         dh_own_out[...] = dh_mine_ref[...] + dh_all_ref[own, :]
         dh_other_out[...] = dh_all_ref[other, :].astype(bf16)
+
+    if background:
+        background.run(step, False, behind_in, behind_out, refs[7:], x_mid_ref)
 
 
 def attention_backward(
@@ -508,16 +1311,24 @@
     dist,
     n_experts,
     head_dim,
+    background=None,
+    behind=(),
 ):
     n_rows, width = x_mid.shape
     length = h_all.shape[0]
     pairs = width // LANES
     span = dist.shape[2]
+    more_shapes, more_scratch, params = [], [], {}
+    if background:
+        more_shapes = background.out_shape(*behind)
+        more_scratch = background.scratch(*behind)
+        params = {"collective_id": 3, "has_side_effects": True}
+    anywhere = pl.BlockSpec(memory_space=pl.ANY)
     whole = lambda shape: pl.BlockSpec(shape, lambda p, *_: (0,) * len(shape))
     columns = lambda rows: pl.BlockSpec((rows, LANES), lambda p, *_: (0, p))
     matrix = lambda i: pl.BlockSpec((None, width, LANES), lambda p, *_: (i, 0, p))
     return pl.pallas_call(
-        functools.partial(backward_kernel, n_experts, head_dim),
+        functools.partial(backward_kernel, background, n_experts, head_dim),
         out_shape=[
             jax.ShapeDtypeStruct((width, width), bf16),
             jax.ShapeDtypeStruct((width, width), bf16),
@@ -529,7 +1340,8 @@
             jax.ShapeDtypeStruct((1, width), f32),
             jax.ShapeDtypeStruct((LANES, width), f32),
             jax.ShapeDtypeStruct((pairs, 2, span), f32),
-        ],
+        ]
+        + more_shapes,
         grid_spec=pltpu.PrefetchScalarGridSpec(
             num_scalar_prefetch=1,
             grid=(pairs,),
@@ -553,7 +1365,8 @@
                 columns(n_rows),
                 columns(n_rows),
                 pl.BlockSpec((1, 2, span), lambda p, *_: (p, 0, 0)),
-            ],
+            ]
+            + [anywhere] * len(behind),
             out_specs=[
                 columns(width),
                 columns(width),
@@ -565,7 +1378,8 @@
                 whole((1, width)),
                 whole((LANES, width)),
                 pl.BlockSpec((1, 2, span), lambda p, *_: (p, 0, 0)),
-            ],
+            ]
+            + [whole(s.shape) for s in more_shapes],
             scratch_shapes=[
                 pltpu.VMEM((n_rows, width), bf16),
                 pltpu.VMEM((length, width), f32),
@@ -574,9 +1388,10 @@
                 pltpu.VMEM((2, LANES, span), f32),
                 pltpu.VMEM((2, LANES, span), f32),
                 pltpu.VMEM((n_rows, LANES), bf16),
-            ],
+            ]
+            + more_scratch,
         ),
-        compiler_params=pltpu.CompilerParams(vmem_limit_bytes=VMEM_LIMIT),
+        compiler_params=pltpu.CompilerParams(vmem_limit_bytes=VMEM_LIMIT, **params),
         cost_estimate=pl.CostEstimate(
             flops=40_000_000_000, transcendentals=0, bytes_accessed=30_000_000
         ),
@@ -602,6 +1417,261 @@
         o,
         lse,
         dist,
+        *behind,
+    )
+
+
+def finish_kernel(
+    n_fsdp,
+    n_experts,
+    n_heads,
+    dwq,
+    dwk,
+    dwv,
+    dwo,
+    sum_out,
+    dw_in,
+    dh_other,
+    dh_own_ref,
+    dx_mid_ref,
+    tokens_ref,
+    gain_one_ref,
+    dgain_two_ref,
+    drouter_ref,
+    ddist_ref,
+    match_ref,
+    attn_out,
+    grad_in,
+    grad_out,
+    tokens_out,
+    small_ref,
+    mine_ref,
+    rx_ref,
+    land_ref,
+    line_ref,
+    line_land,
+    dh_land,
+    in_ref,
+    small_land,
+    near,
+    mid,
+    far,
+    own_ref,
+    line_send,
+    line_recv,
+    line_local,
+    send,
+    recv,
+    local,
+):
+    me = Place(n_fsdp)
+    rep, line, seq, core, row = me.rep, me.line, me.seq, me.core, me.row
+    mate, across, beside, corner = me.mate(), me.chip(1, 0), me.chip(0, 1), me.chip(1, 1)
+    far_row = (row + 1) % 2
+    far_rep = far_row * 2 + core
+    pieces = dw_in.shape[0]
+    part_out = grad_out.shape[1]
+    part_in = grad_in.shape[1]
+    columns = lambda z, x: pl.ds(pl.multiple_of((z * 2 + x) * part_out, LANES), part_out)
+    flip = lambda place: place + 1 - 2 * (place % 2)
+    hop = lambda place: (rep, place, seq)
+    cube = [mate, across, beside, hop(flip(line)), hop((line + 2) % n_fsdp)]
+    plan = {
+        "pair0": (None, rx_ref.at[0], mate),
+        "pair1": (None, rx_ref.at[1], mate),
+        "dh": (dh_other, dh_land, beside),
+        "out_c": (sum_out, grad_out.at[rep], mate),
+        "out_y": (sum_out, grad_out.at[rep], across),
+        "out_f": (grad_out.at[far_rep], grad_out.at[far_rep], mate),
+        "to_y": (mine_ref.at[far_row, :, seq], land_ref.at[1], across),
+        "to_xy": (mine_ref.at[far_row, :, 1 - seq], land_ref.at[2], corner),
+        "to_x": (mine_ref.at[row, :, 1 - seq], land_ref.at[0], beside),
+        "attn_c": (attn_out.at[rep], attn_out.at[rep], mate),
+        "attn_y": (attn_out.at[rep], attn_out.at[rep], across),
+        "attn_f": (attn_out.at[far_rep], attn_out.at[far_rep], mate),
+        "in_c": (grad_in.at[rep], grad_in.at[rep], mate),
+        "in_y": (grad_in.at[rep], grad_in.at[rep], across),
+        "in_f": (grad_in.at[far_rep], grad_in.at[far_rep], mate),
+    }
+    for i, shift in enumerate((1, -1, 2)):
+        target = (line + shift) % n_fsdp
+        plan["line", i] = (line_ref.at[target], line_land.at[i], me.along(shift))
+    for z in range(n_fsdp):
+        plan["in_x", z] = (
+            in_ref.at[1 - seq, :, pl.ds(z * part_out, part_out)],
+            grad_in.at[rep, :, columns(z, seq)],
+            beside,
+        )
+    for i, partner in enumerate(cube):
+        plan["small", i] = (small_ref, small_land.at[i], partner)
+    copies = Planned(plan, send, recv)
+    adds = LineSum(me, dw_in, near, mid, far, own_ref, line_send, line_recv, line_local)
+    matrices = (dwq, dwk, dwv, dwo)
+
+    def pair(side, i):
+        plan[f"pair{i}"] = (matrices[2 * i + 1 - side], rx_ref.at[i], mate)
+        return copies[f"pair{i}"]
+
+    keep = lambda side, i: pltpu.make_async_copy(
+        matrices[2 * i + side], mine_ref.at[i], local.at[i]
+    )
+    own_out = lambda: pltpu.make_async_copy(sum_out, grad_out.at[rep], local.at[2])
+
+    meet([mate, across, beside, corner, me.along(1), me.along(-1), me.along(2)])
+    for side in (0, 1):
+
+        @pl.when(core == side)
+        def _():
+            for i in (0, 1):
+                pair(side, i).start()
+                keep(side, i).start()
+
+    adds.start()
+    copies["dh"].start()
+    copies["out_y"].start()
+    copies["out_c"].start()
+    own_out().start()
+    for i in (0, 1):
+        keep(0, i).wait()
+        pair(0, i).wait_recv()
+    for i in (0, 1):
+        total = mine_ref[i].astype(f32) + rx_ref[i].astype(f32)
+        mine_ref[i] = total.astype(bf16)
+    copies["to_y"].start()
+    copies["to_x"].start()
+    copies["to_xy"].start()
+    small_ref[...] = jnp.zeros_like(small_ref)
+    small_ref[1:2, :] = dgain_two_ref[...]
+    small_ref[2 : 2 + n_experts, :] = drouter_ref[:n_experts, :]
+    small_ref[8 : 8 + n_heads, :LANES] = exact_dot_t(ddist_ref[...], match_ref[...])
+    adds.turn()
+    copies["dh"].wait_recv()
+    dh_one = dh_own_ref[...] + dh_land[...].astype(f32)
+    dx, dgain_one = norm_back(tokens_ref[...].astype(f32), gain_one_ref[...], dh_one)
+    tokens_out[...] = (dx_mid_ref[...] + dx).astype(bf16)
+    small_ref[0:1, :] = dgain_one
+    copies["out_y"].wait_recv()
+    copies["out_f"].start()
+    for i in range(len(cube)):
+        copies["small", i].start()
+        copies["small", i].wait_recv()
+        copies["small", i].wait_send()
+        small_ref[...] = small_ref[...] + small_land[i]
+    copies["to_x"].wait_recv()
+    copies["to_y"].wait_recv()
+    copies["to_xy"].wait_recv()
+    for z in range(n_fsdp):
+        total = mine_ref[row, z, seq].astype(f32)
+        for i in range(3):
+            total = total + land_ref[i, z].astype(f32)
+        line_ref[z] = total.astype(bf16)
+    for i in range(3):
+        copies["line", i].start()
+    in_ref[...] = adds.total().reshape(in_ref.shape)
+    for z in range(n_fsdp):
+        copies["in_x", z].start()
+    kept = []
+    for z in range(n_fsdp):
+        source = in_ref.at[seq, :, pl.ds(z * part_out, part_out)]
+        target = grad_in.at[rep, :, columns(z, seq)]
+        kept.append(pltpu.make_async_copy(source, target, local.at[4 + z]))
+        kept[-1].start()
+    total = line_ref[line].astype(f32)
+    for i in range(3):
+        copies["line", i].wait_recv()
+        total = total + line_land[i].astype(f32)
+    line_land[3] = total.astype(bf16)
+    own_attn = pltpu.make_async_copy(line_land.at[3], attn_out.at[rep], local.at[3])
+    own_attn.start()
+    own_attn.wait()
+    copies["attn_y"].start()
+    copies["attn_c"].start()
+    for copy in kept:
+        copy.wait()
+    for z in range(n_fsdp):
+        copies["in_x", z].wait_recv()
+    copies["in_y"].start()
+    copies["in_c"].start()
+    copies["attn_y"].wait_recv()
+    copies["attn_f"].start()
+    copies["in_y"].wait_recv()
+    copies["in_f"].start()
+    own_out().wait()
+    for name in ("out_c", "out_f", "attn_c", "attn_f", "in_c", "in_f"):
+        copies[name].wait_recv()
+    for name in plan:
+        if name[0] != "small":
+            copies[name].wait_send()
+
+
+def finish(
+    attn_grads,
+    sum_out,
+    dw_in,
+    dh_other,
+    dh_own,
+    dx_mid,
+    tokens,
+    gain_one,
+    dgain_two,
+    drouter,
+    ddist,
+    match,
+    n_fsdp,
+    n_experts,
+    part_in,
+    hidden,
+):
+    n_rows, width = tokens.shape
+    n_heads = ddist.shape[0]
+    part_attn = width // (2 * n_fsdp)
+    part_out = sum_out.shape[0]
+    pair_rows, columns = dw_in.shape[1:]
+    anywhere = pl.BlockSpec(memory_space=pl.ANY)
+    inside = pl.BlockSpec(memory_space=pltpu.VMEM)
+    dma = lambda n: pltpu.SemaphoreType.DMA((n,))
+    split = (n_fsdp, 2, part_attn, width)
+    attn_grads = [g.reshape(split) for g in attn_grads]
+    return pl.pallas_call(
+        functools.partial(finish_kernel, n_fsdp, n_experts, n_heads),
+        out_shape=[
+            jax.ShapeDtypeStruct((4, part_attn, width), bf16),
+            jax.ShapeDtypeStruct((n_experts, part_in, hidden), bf16),
+            jax.ShapeDtypeStruct((n_experts, part_out, width), bf16),
+            jax.ShapeDtypeStruct((n_rows, width), bf16),
+            jax.ShapeDtypeStruct((24, width), f32),
+        ],
+        in_specs=[anywhere] * 7 + [inside] * 8,
+        out_specs=[anywhere] * 3 + [inside] * 2,
+        scratch_shapes=[
+            pltpu.VMEM((2,) + split, bf16),
+            pltpu.VMEM((2,) + split, bf16),
+            pltpu.VMEM((3, n_fsdp, part_attn, width), bf16),
+            pltpu.VMEM((n_fsdp, part_attn, width), bf16),
+            pltpu.VMEM((4, part_attn, width), bf16),
+            pltpu.VMEM((n_rows, width), bf16),
+            pltpu.VMEM((2, part_in, columns), bf16),
+            pltpu.VMEM((5, 24, width), f32),
+        ]
+        + LineSum.scratch(pair_rows, columns)
+        + [dma(32), dma(32), dma(12)],
+        compiler_params=pltpu.CompilerParams(
+            vmem_limit_bytes=VMEM_LIMIT, collective_id=4, has_side_effects=True
+        ),
+        name="finish_gradients",
+    )(
+        *attn_grads,
+        sum_out,
+        dw_in,
+        dh_other,
+        dh_own,
+        dx_mid,
+        tokens,
+        gain_one,
+        dgain_two,
+        drouter,
+        ddist,
+        match,
     )
 
 
@@ -636,22 +1706,27 @@
     assert n_experts == n_rep == 4 and n_seq == 2 and 2 * head_dim == LANES
     pairs = n_heads // 2
 
-    place = jnp.concatenate([(seq * n_rows)[None], piece_starts[0]]).astype(jnp.int32)
+    place = piece_starts[0]
+    near = n_fsdp == 4 and part_attn % 16 == 0
     pick = lambda array: lax.dynamic_index_in_dim(array, rep, 0, keepdims=False)
-    attn_own = pick(jnp.stack([attn_q, attn_k, attn_v, attn_o]))
-    attn_line = lax.all_gather(attn_own, "fsdp", axis=0, tiled=False)
-    attn_all = lax.all_gather(attn_line, plane, axis=0, tiled=False)
-    attn_all = attn_all.reshape(n_rep, n_seq, n_fsdp, part_attn, width)
-    weights = attn_all.transpose(0, 2, 1, 3, 4).reshape(n_rep, width, width)
-    x_all = lax.all_gather(tokens, "seq", axis=0, tiled=True)
-
-    in_own = pick(expert_in).reshape(part_in, n_fsdp, n_seq, part_out)
-    in_own = in_own.transpose(2, 0, 1, 3).reshape(n_seq, part_in, n_fsdp * part_out)
-    in_pair = lax.all_to_all(in_own, "seq", split_axis=0, concat_axis=0, tiled=True)
-    in_pair = in_pair.reshape(n_seq * part_in, n_fsdp * part_out)
-    w_in = lax.all_gather(in_pair, "fsdp", axis=0, tiled=True)
-    w_out = lax.all_gather(pick(expert_out), "fsdp", axis=0, tiled=True)
-    dy_all = lax.all_gather(cotangent, plane, axis=0, tiled=True)
+    if near:
+        weights, x_all, in_pair, w_out = gather(
+            (attn_q, attn_k, attn_v, attn_o), tokens, expert_in, expert_out, n_fsdp
+        )
+    else:
+        attn_own = pick(jnp.stack([attn_q, attn_k, attn_v, attn_o]))
+        attn_line = lax.all_gather(attn_own, "fsdp", axis=0, tiled=False)
+        attn_all = lax.all_gather(attn_line, plane, axis=0, tiled=False)
+        attn_all = attn_all.reshape(n_rep, n_seq, n_fsdp, part_attn, width)
+        weights = attn_all.transpose(0, 2, 1, 3, 4).reshape(n_rep, width, width)
+        x_all = lax.all_gather(tokens, "seq", axis=0, tiled=True)
+        in_own = pick(expert_in).reshape(part_in, n_fsdp, n_seq, part_out)
+        in_own = in_own.transpose(2, 0, 1, 3).reshape(n_seq, part_in, n_fsdp * part_out)
+        in_pair = lax.all_to_all(in_own, "seq", split_axis=0, concat_axis=0, tiled=True)
+        in_pair = in_pair.reshape(n_seq * part_in, n_fsdp * part_out)
+        w_in = lax.all_gather(in_pair, "fsdp", axis=0, tiled=True)
+        w_out = lax.all_gather(pick(expert_out), "fsdp", axis=0, tiled=True)
+        dy_all = lax.all_gather(cotangent, plane, axis=0, tiled=True)
 
     match = (buckets[:, None] == jnp.arange(n_buckets, dtype=jnp.int32)[None, :]).astype(f32)
     dist = lax.dot_general(
@@ -663,7 +1738,7 @@
     gain_one = gain_attn[None, :]
     gain_two = gain_ffn[None, :]
 
-    q, k, v, o, lse, x_mid, message, probs, h_all = attention_forward(
+    q, k, v, o, lse, x_mid, message, probs, h_all, *gathered = attention_forward(
         place,
         x_all,
         gain_one,
@@ -675,16 +1750,28 @@
         n_rows,
         n_experts,
         head_dim,
+        Background(n_fsdp) if near else None,
+        (cotangent, in_pair) if near else (),
     )
-    message_all = lax.all_gather(message, plane, axis=0, tiled=True)
-    out_part, back_part, dw_in, dw_out = experts(
-        rep[None].astype(jnp.int32), message_all, dy_all, w_in, w_out, n_experts, n_rows
-    )
-    back = lax.psum_scatter(back_part, plane, scatter_dimension=0, tiled=True)
-    out_sum = lax.psum_scatter(out_part, plane, scatter_dimension=0, tiled=True)
-    out_rows = (x_mid + out_sum.astype(f32)).astype(bf16)
-
-    dwq, dwk, dwv, dwo, dh_own, dh_other, dx_mid, dgain_two, drouter, ddist = attention_backward(
+    if near:
+        dy_all = gathered[0]
+        w_in = gathered[1].reshape(width, n_fsdp * part_out)
+    behind = ()
+    if near:
+        back, out_half, dw_in, dw_out = plane_experts(
+            message, dy_all, w_in, w_out, n_experts, n_fsdp
+        )
+        behind = (out_half, dw_out.reshape(n_fsdp, part_out, width), x_mid)
+    else:
+        message_all = lax.all_gather(message, plane, axis=0, tiled=True)
+        out_part, back_part, dw_in, dw_out = experts(
+            rep[None].astype(jnp.int32), message_all, dy_all, w_in, w_out, n_experts, n_rows
+        )
+        back = lax.psum_scatter(back_part, plane, scatter_dimension=0, tiled=True)
+        out_sum = lax.psum_scatter(out_part, plane, scatter_dimension=0, tiled=True)
+        out_rows = (x_mid + out_sum.astype(f32)).astype(bf16)
+
+    grads = attention_backward(
         place,
         back,
         cotangent,
@@ -704,36 +1791,66 @@
         dist,
         n_experts,
         head_dim,
+        BackgroundBack(n_fsdp) if near else None,
+        behind,
     )
-    sum_out = lax.psum_scatter(dw_out, "fsdp", scatter_dimension=0, tiled=True)
-    sum_in = lax.psum_scatter(dw_in, "fsdp", scatter_dimension=0, tiled=True)
-    sum_in = sum_in.reshape(n_seq, part_in, n_fsdp * part_out)
-    sum_in = lax.all_to_all(sum_in, "seq", split_axis=0, concat_axis=0, tiled=True)
-    sum_in = sum_in.reshape(n_seq, part_in, n_fsdp, part_out).transpose(1, 2, 0, 3)
-    sum_in = sum_in.reshape(part_in, hidden)
-    grad_out = lax.all_gather(sum_out, "rep", axis=0, tiled=False).astype(f32)
-    grad_in = lax.all_gather(sum_in, "rep", axis=0, tiled=False).astype(f32)
-
-    swap = [(0, 1), (1, 0)]
-    dh_one = dh_own + lax.ppermute(dh_other, "seq", swap).astype(f32)
-    dx, dgain_one = norm_back(tokens.astype(f32), gain_one, dh_one)
-    grad_tokens = (dx_mid + dx).astype(bf16)
-
-    attn_grads = jnp.stack([dwq, dwk, dwv, dwo]).reshape(n_rep, n_fsdp, n_seq, part_attn, width)
-    attn_grads = attn_grads.transpose(0, 2, 1, 3, 4).reshape(
-        n_rep * n_seq * n_fsdp * part_attn, width
-    )
-    attn_sum = lax.psum_scatter(attn_grads, plane, scatter_dimension=0, tiled=True)
-    attn_sum = lax.psum_scatter(attn_sum, "fsdp", scatter_dimension=0, tiled=True)
-    attn_sum = lax.all_gather(attn_sum, "rep", axis=0, tiled=False).astype(f32)
-
-    ddist = ddist.reshape(n_heads, span)[:, : buckets.shape[0]]
-    table = lax.dot_general(
-        match, ddist, (((0,), (1,)), ((), ())), precision=highest, preferred_element_type=f32
-    )
-    grad_one, grad_two, grad_table, grad_router = lax.psum(
-        (dgain_one[0], dgain_two[0], table, drouter[:n_experts].T), ("rep", "fsdp", "seq")
-    )
+    dwq, dwk, dwv, dwo, dh_own, dh_other, dx_mid, dgain_two, drouter, ddist = grads[:10]
+    if near:
+        out_rows, sum_out = grads[10:]
+        match_wide = jnp.pad(match.T, ((0, LANES - n_buckets), (0, span - match.shape[0])))
+        attn_sum, grad_in, grad_out, grad_tokens, small = finish(
+            (dwq, dwk, dwv, dwo),
+            sum_out,
+            dw_in.reshape(n_fsdp, n_seq * part_in, n_fsdp * part_out),
+            dh_other,
+            dh_own,
+            dx_mid,
+            tokens,
+            gain_one,
+            dgain_two,
+            drouter,
+            ddist.reshape(n_heads, span),
+            match_wide,
+            n_fsdp,
+            n_experts,
+            part_in,
+            hidden,
+        )
+        grad_one, grad_two = small[0], small[1]
+        grad_router = small[2 : 2 + n_experts].T
+        grad_table = small[8 : 8 + n_heads, :n_buckets].T
+    else:
+        sum_out = lax.psum_scatter(dw_out, "fsdp", scatter_dimension=0, tiled=True)
+        sum_in = lax.psum_scatter(dw_in, "fsdp", scatter_dimension=0, tiled=True)
+        sum_in = sum_in.reshape(n_seq, part_in, n_fsdp * part_out)
+        sum_in = lax.all_to_all(sum_in, "seq", split_axis=0, concat_axis=0, tiled=True)
+        sum_in = sum_in.reshape(n_seq, part_in, n_fsdp, part_out).transpose(1, 2, 0, 3)
+        sum_in = sum_in.reshape(part_in, hidden)
+        grad_out = lax.all_gather(sum_out, "rep", axis=0, tiled=False)
+        grad_in = lax.all_gather(sum_in, "rep", axis=0, tiled=False)
+        swap = [(0, 1), (1, 0)]
+        dh_one = dh_own + lax.ppermute(dh_other, "seq", swap).astype(f32)
+        dx, dgain_one = norm_back(tokens.astype(f32), gain_one, dh_one)
+        grad_tokens = (dx_mid + dx).astype(bf16)
+        attn_grads = jnp.stack([dwq, dwk, dwv, dwo])
+        attn_grads = attn_grads.reshape(n_rep, n_fsdp, n_seq, part_attn, width)
+        attn_grads = attn_grads.transpose(0, 2, 1, 3, 4)
+        attn_grads = attn_grads.reshape(n_rep * n_seq * n_fsdp * part_attn, width)
+        attn_sum = lax.psum_scatter(attn_grads, plane, scatter_dimension=0, tiled=True)
+        attn_sum = lax.psum_scatter(attn_sum, "fsdp", scatter_dimension=0, tiled=True)
+        attn_sum = lax.all_gather(attn_sum, "rep", axis=0, tiled=False)
+        ddist = ddist.reshape(n_heads, span)[:, : buckets.shape[0]]
+        table = lax.dot_general(
+            match,
+            ddist,
+            (((0,), (1,)), ((), ())),
+            precision=highest,
+            preferred_element_type=f32,
+        )
+        grad_one, grad_two, grad_table, grad_router = lax.psum(
+            (dgain_one[0], dgain_two[0], table, drouter[:n_experts].T), ("rep", "fsdp", "seq")
+        )
+    attn_sum = attn_sum.astype(f32)
     return (
         out_rows,
         grad_tokens,
@@ -741,8 +1858,8 @@
         attn_sum[1],
         attn_sum[2],
         attn_sum[3],
-        grad_in,
-        grad_out,
+        grad_in.astype(f32),
+        grad_out.astype(f32),
         grad_one,
         grad_two,
         grad_table,

time: 734 us -> 366 us (0.50)
  waiting for transfers between devices: 451 us -> 0 us
  Pallas kernels: 133 us -> 344 us
  blocking collectives: 94.2 us -> 0 us
  between operations: 14.2 us -> 0.81 us
  other arithmetic: 20.2 us -> 8.23 us
    all_gather x8 -> x0, waiting for transfers between devices: 243 us -> none  [the longest x1 50.8 us: per_device(): w_in = lax.all_gather(in_pair, 'fsdp', axis=0, tiled=True)]
    pallas_call x3 -> x5, Pallas kernels: 133 us -> 344 us  [the longest x1 90.1 us: finish(): pl.pallas_call(functools.partial(finish_kernel, n_fsdp, n_experts, n_head...]
    reduce_scatter x6 -> x0, waiting for transfers between devices: 204 us -> none  [the longest x1 60.5 us: per_device(): back = lax.psum_scatter(back_part, plane, scatter_dimension=0, tiled=True)]
    psum x1 -> x0, blocking collectives: 40.4 us -> none  [per_device(): lax.psum((dgain_one[0], dgain_two[0], table, drouter[:n_experts].T), ('re...]
    all_gather x2 -> x0, blocking collectives: 27.3 us -> none  [the longest x1 18.4 us: per_device(): attn_line = lax.all_gather(attn_own, 'fsdp', axis=0, tiled=False)]
    all_to_all x2 -> x0, blocking collectives: 26.5 us -> none  [the longest x1 14.3 us: per_device(): lax.all_to_all(in_own, 'seq', split_axis=0, concat_axis=0, tiled=True)]
  transfers between devices with their start and end apart: 15 -> 0, of which waited for: 13 -> 0; matrix products, arithmetic and copies ran while one was open for 5% -> 0% of each run, Pallas kernels for 10% -> 0%
where the time goes in v2:
time: 366 us
  Pallas kernels  344 us (94%)
  local copies, waits for them, and re-layouts  12 us (3%)
  other arithmetic  8.23 us (2%)
    pallas_call x1, Pallas kernels, finish(): pl.pallas_call(functools.partial(finish_kernel, n_fsdp, n_experts, n_head...  90.1 us
    pallas_call x1, Pallas kernels, plane_experts(): pl.pallas_call(functools.partial(plane_experts_kernel, n_experts, 512, n_...  84.7 us
    pallas_call x1, Pallas kernels, gather(): pl.pallas_call(functools.partial(gather_kernel, n_fsdp), out_shape=[jax.S...  63.6 us
    pallas_call x1, Pallas kernels, attention_backward(): pl.pallas_call(functools.partial(backward_kernel, background, n_experts,...  57.3 us
    pallas_call x1, Pallas kernels, attention_forward(): pl.pallas_call(functools.partial(forward_kernel, background, n_experts, h...  48 us

profile of v2, /device:TPU:0, one launch (start us, length us, event | category | flops | bytes accessed | tf_op | source)
XLA Modules:
  0.0 366.0 jit_solution(15528251983673219870)
XLA Ops:
  0.6 0.0 copy-start
  0.7 0.0 copy-start.6
  0.7 0.0 copy-start.7
  0.7 63.6 %gather_weights.1 = (bf16[4,4,2,96,768]{4,3,2,1,0:T(8,128)(2,1)}, bf16[2,384,768]{2,1,0:T(8,128)(2,1)}, bf16[2,96,1536]{2,1,0:T(8,128)(2,1)}, bf16[4,384,768]{2,1,0:T(8,128)(2,1)}) custom-call(bf16[96,768]{1,0:T(8,128)(2,1)} %attn_q.1, bf16[96,768]{1,0:T(8,128)(2,1)} %attn_k.1, bf16[96,768]{1,0:T(8,128)(2,1)} %attn_v.1, bf16[96,768]{1,0:T(8,128)(2,1)} %attn_o.1, ...), custom_call_target="tpu_custom_call" | custom-call | tf_op jit(solution)/shard_map/gather_weights/pallas_call | solution.py:282
  64.3 0.0 copy-start.10
  64.3 0.0 copy-start.8
  64.3 0.0 copy-start.9
  64.4 0.2 copy.27
  64.6 0.8 pad.15.router_ref
  65.3 1.2 convolution_bitcast_fusion
  66.5 0.7 reshape.66.dist_ref
  67.2 0.8 copy.28.routes_ref
  68.0 0.6 broadcast_in_dim.8.gain_one_ref
  68.6 0.6 broadcast_in_dim.9.gain_two_ref
  69.2 48.0 %attention_forward.1 = (bf16[384,768]{1,0:T(8,128)(2,1)}, bf16[768,768]{1,0:T(8,128)(2,1)}, bf16[768,768]{1,0:T(8,128)(2,1)}, bf16[384,768]{1,0:T(8,128)(2,1)}, ...) custom-call(s32[2]{0:T(128)} %bitcast.43, ...), custom_call_target="tpu_custom_call" | custom-call | flops 20000000000 | bytes 20000000 | tf_op jit(solution)/shard_map/attention_forward/pallas_call | solution.py:522
  117.3 84.7 %plane_experts.1 = (f32[384,896]{1,0:T(8,128)}, bf16[8,192,768]{2,1,0:T(8,128)(2,1)}, bf16[768,1536]{1,0:T(8,128)(2,1)}, bf16[1536,768]{1,0:T(8,128)(2,1)}) custom-call(bf16[384,896]{1,0:T(8,128)(2,1)} %get-tuple-element.51.message_ref, bf16[8,384,768]{2,1,0:T(8,128)(2,1)} %get-tuple-element.52.dy_ref, bf16[768,1536]{1,0:T(8,128)(2,1)} %bitcast.46, ...), custom_call_target="tpu_custom_call" | custom-call | flops 60000002048 | bytes 30000000 | tf_op jit(solution)/shard_map/plane_experts/pallas_call | solution.py:940
  201.9 57.3 %attention_backward.1 = (bf16[768,768]{1,0:T(8,128)(2,1)}, bf16[768,768]{1,0:T(8,128)(2,1)}, bf16[768,768]{1,0:T(8,128)(2,1)}, bf16[768,768]{1,0:T(8,128)(2,1)},...) custom-call(s32[2]{0:T(128)} %bitcast.44, ...), custom_call_target="tpu_custom_call" | custom-call | flops 40000000000 | bytes 30000000 | tf_op jit(solution)/shard_map/attention_backward/pallas_call | solution.py:1330
  259.3 1.6 reshape.76.ddist_ref
  260.9 0.9 pad_convert_fusion.match_ref
  261.8 90.1 %finish_gradients.1 = (bf16[4,96,768]{2,1,0:T(8,128)(2,1)}, bf16[4,96,3072]{2,1,0:T(8,128)(2,1)}, bf16[4,384,768]{2,1,0:T(8,128)(2,1)}, bf16[384,768]{1,0:T(8,128)(2,1)}, f32[24,768]{1,0:T(8,128)}) custom-call(bf16[4,2,96,768]{3,2,1,0:T(8,128)(2,1)} %bitcast.28, bf16[4,2,96,768]{3,2,1,0:T(8,128)(2,1)} %bitcast.29, bf16[4,2,96,768]{3,2,1,0:T(8,128)(2,1)} %bitcast.30, ...), custom_call_target="tpu_custom_call" | custom-call | tf_op jit(solution)/shard_map/finish_gradients/pallas_call | solution.py:1635
  352.0 4.6 %convert_element_type.18 = f32[4,96,3072]{2,1,0:T(8,128)} convert(bf16[4,96,3072]{2,1,0:T(8,128)(2,1)} %get-tuple-element.81) | non-fusion elementwise | flops 1179648 | bytes 7077888 | tf_op jit(solution)/shard_map/convert_element_type | solution.py:1861
  356.6 0.0 copy-done.2
  356.6 2.6 convert_element_type.19
  359.2 0.1 convert_element_type.17
  359.3 0.0 copy-start.1
  359.3 1.0 slice_bitcast_fusion
  360.3 1.3 slice_bitcast_fusion.4
  361.7 1.4 slice_reduce_fusion
  363.1 1.3 slice_bitcast_fusion.5
  364.4 0.8 copy.32
  365.2 0.0 copy-done.5
  365.2 0.8 copy.33
  (15 shorter events, 0.1 us)
Async XLA Ops:
  0.6 64.7 %copy-start = (f32[32,12]{0,1:T(8,128)S(1)}, f32[32,12]{0,1:T(8,128)}, u32[]{:S(2)}) copy-start(f32[32,12]{0,1:T(8,128)} %param.27) | copy-start | bytes 4612
  0.7 63.7 %copy-start.6 = (f32[768,4]{0,1:T(4,128)S(1)}, f32[768,4]{0,1:T(4,128)}, u32[]{:S(2)}) copy-start(f32[768,4]{0,1:T(4,128)} %param.28) | copy-start | bytes 36868
  0.7 64.7 %copy-start.7 = (s32[1535]{0:T(1024)S(1)}, s32[1535]{0:T(1024)}, u32[]{:S(2)}) copy-start(s32[1535]{0:T(1024)} %param.18) | copy-start | bytes 18424
  64.3 2.9 copy-start.10
  64.3 3.7 %copy-start.8 = (f32[768]{0:T(1024)S(1)}, f32[768]{0:T(1024)}, u32[]{:S(2)}) copy-start(f32[768]{0:T(1024)} %param.25) | copy-start | bytes 9220
  64.3 4.3 %copy-start.9 = (f32[768]{0:T(1024)S(1)}, f32[768]{0:T(1024)}, u32[]{:S(2)}) copy-start(f32[768]{0:T(1024)} %param.26) | copy-start | bytes 9220
  352.0 4.6 %copy-start.2 = (bf16[4,384,768]{2,1,0:T(8,128)(2,1)S(1)}, bf16[4,384,768]{2,1,0:T(8,128)(2,1)}, u32[]{:S(2)}) copy-start(bf16[4,384,768]{2,1,0:T(8,128)(2,1)} %get-tuple-element.82) | copy-start | bytes 7077892
  356.6 2.6 copy-start.3
  359.3 5.1 %copy-start.4 = (bf16[384,768]{1,0:T(8,128)(2,1)S(1)}, bf16[384,768]{1,0:T(8,128)(2,1)}, u32[]{:S(2)}) copy-start(bf16[384,768]{1,0:T(8,128)(2,1)} %get-tuple-element.102) | copy-start | bytes 1769476
  359.3 5.9 %copy-start.5 = (bf16[384,768]{1,0:T(8,128)(2,1)S(1)}, bf16[384,768]{1,0:T(8,128)(2,1)}, u32[]{:S(2)}) copy-start(bf16[384,768]{1,0:T(8,128)(2,1)} %get-tuple-element.103) | copy-start | bytes 1769476
  359.3 6.7 %copy-start.1 = (f32[32,12]{0,1:T(8,128)S(1)}, f32[32,12]{0,1:T(8,128)}, u32[]{:S(2)}) copy-start(f32[32,12]{0,1:T(8,128)} %param.27) | copy-start | bytes 4612

commit v3 on v2

--- a/solution.py
+++ b/solution.py
@@ -86,9 +86,44 @@
     return sums
 
 
-def chosen_experts(routes_ref, shape):
-    lane = lax.broadcasted_iota(jnp.int32, shape, 1)
-    return (lane == routes_ref[:, 0:1]) | (lane == routes_ref[:, 1:2])
+def chosen_experts(pack_ref, shape):
+    lane = lax.broadcasted_iota(jnp.int32, shape, 1).astype(f32)
+    routes = pack_ref[24:32, : shape[0]].T
+    return (lane == routes[:, 0:1]) | (lane == routes[:, 1:2])
+
+
+def pack_small(router, gain_attn, gain_ffn, buckets, rel_table, routes, span):
+    def rows(array, count):
+        array = array.astype(f32)
+        return jnp.pad(array, ((0, count - array.shape[0]), (0, span - array.shape[1])))
+
+    return jnp.concatenate(
+        [
+            rows(router.T, 4),
+            rows(gain_attn[None, :], 1),
+            rows(gain_ffn[None, :], 1),
+            rows(buckets[None, :], 2),
+            rows(rel_table.T, 16),
+            rows(routes.T, 8),
+        ]
+    )
+
+
+def router_rows(pack_ref, n_experts, width):
+    first = pack_ref[0:8, :width]
+    row = lax.broadcasted_iota(jnp.int32, first.shape, 0)
+    first = jnp.where(row < n_experts, first, 0.0)
+    return jnp.concatenate([first, jnp.zeros((LANES - 8, width), f32)])
+
+
+def bucket_match(pack_ref):
+    shape = (LANES, pack_ref.shape[1])
+    bucket = lax.broadcasted_iota(jnp.int32, shape, 0).astype(f32)
+    return (bucket == pack_ref[6:7, :]).astype(f32)
+
+
+def distances(pack_ref):
+    return exact_dot(pack_ref[8:24, :LANES], bucket_match(pack_ref))
 
 
 MESH = pl.DeviceIdType.MESH
@@ -159,17 +194,19 @@
 
 def gather_kernel(
     n_fsdp,
+    part_out,
     attn_q,
     attn_k,
     attn_v,
     attn_o,
     tokens,
     expert_in,
-    expert_out,
     weights,
     x_all,
-    in_pair,
-    w_out,
+    w_in,
+    attn_held,
+    tokens_held,
+    in_held,
     send,
     recv,
     local,
@@ -178,7 +215,7 @@
     rep, line, seq = me.rep, me.line, me.seq
     far_row = (me.row + 1) % 2 * 2 + me.core
     mate, across, beside = me.mate(), me.chip(1, 0), me.chip(0, 1)
-    part_out = expert_out.shape[1]
+    part_in = expert_in.shape[1]
     wires = Wires(send, recv)
     meet([mate, across, beside, me.along(1), me.along(-1), me.along(2)])
     started = []
@@ -192,7 +229,7 @@
 
         @pl.when(rep == i)
         def _():
-            own = pltpu.make_async_copy(matrix, weights.at[i, line, seq], local.at[n_fsdp])
+            own = pltpu.make_async_copy(matrix, attn_held, local.at[0])
             own.start()
             own.wait()
 
@@ -203,45 +240,51 @@
     for shift in shifts[1:]:
         at[shift] = (line - shift) % n_fsdp
         z_copies[shift] = start(
-            wires.copy(("z", shift), mine(line), mine(line), me.along(shift))
+            wires.copy(("z", shift), attn_held, mine(line), me.along(shift))
         )
     x_copies, y_copies, c_copies, far_copies = {}, {}, [], {}
 
     def spread_out(shift):
         z = at[shift]
-        x_copies[shift] = start(wires.copy(("x", shift), mine(z), mine(z), beside))
-        y_copies[shift] = start(wires.copy(("y", shift), mine(z), mine(z), across))
-        c_copies.append(start(wires.copy(("c", shift), mine(z), mine(z), mate)))
+        source = mine(z) if shift else attn_held
+        x_copies[shift] = start(wires.copy(("x", shift), source, mine(z), beside))
+        y_copies[shift] = start(wires.copy(("y", shift), source, mine(z), across))
+        c_copies.append(start(wires.copy(("c", shift), source, mine(z), mate)))
 
     spread_out(0)
-    x_own = pltpu.make_async_copy(tokens, x_all.at[seq], local.at[n_fsdp + 2])
+    columns = lambda z, x: pl.ds(pl.multiple_of((z * 2 + x) * part_out, LANES), part_out)
+    rows = lambda x: pl.ds(pl.multiple_of(x * part_in, part_in), part_in)
+    in_x, in_own = [], []
+    for z in range(n_fsdp):
+        here = pl.ds(z * part_out, part_out)
+        target = w_in.at[line, rows(seq), here]
+        in_x.append(
+            start(wires.copy(("in", z), expert_in.at[rep, :, columns(z, 1 - seq)], target, beside))
+        )
+        copy = pltpu.make_async_copy(
+            expert_in.at[rep, :, columns(z, seq)], in_held.at[:, here], local.at[1 + z]
+        )
+        copy.start()
+        in_own.append(copy)
+    own_attn = pltpu.make_async_copy(attn_held, mine(line), local.at[0])
+    own_attn.start()
+    x_own = Bounce(tokens, tokens_held, x_all.at[seq], local.at[pl.ds(n_fsdp + 1, 2)])
     x_own.start()
+    for copy in in_own:
+        copy.wait()
+    own_in = pltpu.make_async_copy(in_held, w_in.at[line, rows(seq)], local.at[n_fsdp + 3])
+    own_in.start()
+    x_own.turn()
     for shift in shifts[1:]:
         z_copies[shift].wait_recv()
         spread_out(shift)
-    columns = lambda z, x: pl.ds(pl.multiple_of((z * 2 + x) * part_out, LANES), part_out)
-    in_x, in_own = [], []
-    for z in range(n_fsdp):
-        here = pl.ds(z * part_out, part_out)
-        copy = wires.copy(
-            ("in", z),
-            expert_in.at[rep, :, columns(z, 1 - seq)],
-            in_pair.at[seq, :, here],
-            beside,
-        )
-        in_x.append(start(copy))
-        copy = pltpu.make_async_copy(
-            expert_in.at[rep, :, columns(z, seq)], in_pair.at[seq, :, here], local.at[z]
-        )
-        copy.start()
-        in_own.append(copy)
-    out_own = pltpu.make_async_copy(expert_out.at[rep], w_out.at[line], local.at[n_fsdp + 1])
-    out_own.start()
-    out_copies = {}
-    for shift in (1, -1):
-        out_copies[shift] = start(
-            wires.copy(("out", shift), expert_out.at[rep], w_out.at[line], me.along(shift))
-        )
+    for copy in in_x:
+        copy.wait_recv()
+    own_in.wait()
+    in_copies = [
+        start(wires.copy(("line", shift), w_in.at[line], w_in.at[line], me.along(shift)))
+        for shift in (1, -1)
+    ]
     token_copy = start(wires.copy("tokens", tokens, x_all.at[seq], beside))
     for shift in shifts:
         z = at[shift]
@@ -259,85 +302,104 @@
         far_copies[shift].wait_recv()
         there = mine(z, far_row, 1 - seq)
         c_copies.append(start(wires.copy(("cf", shift), there, there, mate)))
-    half = part_out // 2
-    relays = []
-    for shift, rows in ((1, pl.ds(0, half)), (-1, pl.ds(half, half))):
-        out_copies[shift].wait_recv()
-        piece = w_out.at[(line - shift) % n_fsdp, rows]
-        relays.append(start(wires.copy(("relay", shift), piece, piece, me.along(shift))))
-    for copy in c_copies + relays + in_x + [token_copy]:
+    for copy in c_copies + in_copies + [token_copy]:
         copy.wait_recv()
-    for copy in in_own + [out_own, x_own]:
-        copy.wait()
+    x_own.wait()
+    own_attn.wait()
     for copy in started:
         copy.wait_send()
 
 
-def gather(attn, tokens, expert_in, expert_out, n_fsdp):
+def gather(attn, tokens, expert_in, part_out, n_fsdp):
     part_attn, width = attn[0].shape
     n_rows = tokens.shape[0]
     n_experts, part_in, hidden = expert_in.shape
-    part_out = expert_out.shape[1]
     anywhere = pl.BlockSpec(memory_space=pl.ANY)
-    weights, x_all, in_pair, w_out = pl.pallas_call(
-        functools.partial(gather_kernel, n_fsdp),
+    weights, x_all, w_in = pl.pallas_call(
+        functools.partial(gather_kernel, n_fsdp, part_out),
         out_shape=[
             jax.ShapeDtypeStruct((4, n_fsdp, 2, part_attn, width), bf16),
             jax.ShapeDtypeStruct((2, n_rows, width), bf16),
-            jax.ShapeDtypeStruct((2, part_in, n_fsdp * part_out), bf16),
-            jax.ShapeDtypeStruct((n_fsdp, part_out, width), bf16),
+            jax.ShapeDtypeStruct((n_fsdp, 2 * part_in, n_fsdp * part_out), bf16),
         ],
-        in_specs=[anywhere] * 7,
-        out_specs=[anywhere] * 4,
+        in_specs=[anywhere] * 6,
+        out_specs=[anywhere] * 3,
         scratch_shapes=[
+            pltpu.VMEM((part_attn, width), bf16),
+            pltpu.VMEM((n_rows, width), bf16),
+            pltpu.VMEM((part_in, n_fsdp * part_out), bf16),
             pltpu.SemaphoreType.DMA((48,)),
             pltpu.SemaphoreType.DMA((48,)),
             pltpu.SemaphoreType.DMA((8,)),
         ],
         compiler_params=pltpu.CompilerParams(collective_id=0, has_side_effects=True),
         name="gather_weights",
-    )(*attn, tokens, expert_in, expert_out)
+    )(*attn, tokens, expert_in)
     return (
         weights.reshape(4, n_fsdp * 2 * part_attn, width),
         x_all.reshape(2 * n_rows, width),
-        in_pair.reshape(2 * part_in, n_fsdp * part_out),
-        w_out.reshape(n_fsdp * part_out, width),
+        w_in,
     )
 
 
+class Bounce:
+    def __init__(self, source, held, target, sems):
+        self.load = lambda: pltpu.make_async_copy(source, held, sems.at[0])
+        self.store = lambda: pltpu.make_async_copy(held, target, sems.at[1])
+
+    def start(self):
+        self.load().start()
+
+    def turn(self):
+        self.load().wait()
+        self.store().start()
+
+    def wait(self):
+        self.store().wait()
+
+
+def relay_plan(me, pieces):
+    rows = pieces.shape[1] // 2
+    plan = {}
+    for i, shift in enumerate((1, -1)):
+        piece = pieces.at[(me.line - shift) % me.n_fsdp, pl.ds(i * rows, rows)]
+        plan["relay", shift] = (piece, piece, me.along(shift))
+    return plan
+
+
 class Background:
-    n_in, n_out = 2, 2
+    n_in, n_out = 3, 3
 
     def __init__(self, n_fsdp):
         self.n_fsdp = n_fsdp
 
-    def out_shape(self, n_rows, width, pair_rows, columns):
+    def out_shape(self, dy, w_in, expert_out):
         return [
-            jax.ShapeDtypeStruct((8, n_rows, width), bf16),
-            jax.ShapeDtypeStruct((self.n_fsdp, pair_rows, columns), bf16),
+            jax.ShapeDtypeStruct((8,) + dy.shape, bf16),
+            jax.ShapeDtypeStruct(w_in.shape, bf16),
+            jax.ShapeDtypeStruct((self.n_fsdp,) + expert_out.shape[1:], bf16),
         ]
 
-    scratch = (
-        pltpu.SemaphoreType.DMA((16,)),
-        pltpu.SemaphoreType.DMA((16,)),
-        pltpu.SemaphoreType.DMA((2,)),
-    )
+    def scratch(self, dy, w_in, expert_out):
+        return [
+            pltpu.SemaphoreType.DMA((16,)),
+            pltpu.SemaphoreType.DMA((16,)),
+            pltpu.SemaphoreType.DMA((4,)),
+            pltpu.VMEM(dy.shape, bf16),
+            pltpu.VMEM(expert_out.shape[1:], bf16),
+        ]
 
     def run(self, step, before, ins, outs, scratch):
-        dy, in_pair = ins
-        dy_all, w_in = outs
-        send, recv, local = scratch
+        dy, _, expert_out = ins
+        dy_all, w_in, w_out = outs
+        send, recv, local, dy_held, out_held = scratch
         me = Place(self.n_fsdp)
-        n_rows = dy.shape[0]
-        half = n_rows // 2
+        half = dy.shape[0] // 2
         first, second = pl.ds(0, half), pl.ds(half, half)
         core = me.core
         own = 7 * (1 - core)
         mate, across, beside = me.mate(), me.chip(1, 0), me.chip(0, 1)
         slot = dy_all.at
-        rows = w_in.shape[1] // 2
-        parts = {1: pl.ds(0, rows), -1: pl.ds(rows, rows)}
-        passed = {s: w_in.at[(me.line - s) % self.n_fsdp, parts[s]] for s in (1, -1)}
         plan = {
             "x": (dy, slot[1 + core], beside),
             "y": (dy, slot[3 + core], across),
@@ -347,33 +409,32 @@
             "c3": (slot[5 + core], slot[5 + core], mate),
             "xy": (slot[1 + core, first], slot[5 + core, first], across),
             "yx": (slot[3 + core, second], slot[5 + core, second], beside),
-            ("z", 1): (in_pair, w_in.at[me.line], me.along(1)),
-            ("z", -1): (in_pair, w_in.at[me.line], me.along(-1)),
-            ("relay", 1): (passed[1], passed[1], me.along(1)),
-            ("relay", -1): (passed[-1], passed[-1], me.along(-1)),
-        }
+            ("z", 1): (expert_out.at[me.rep], w_out.at[me.line], me.along(1)),
+            ("z", -1): (expert_out.at[me.rep], w_out.at[me.line], me.along(-1)),
+        } | relay_plan(me, w_in)
         copies = Planned(plan, send, recv)
+        own_dy = Bounce(dy, dy_held, slot[own], local.at[pl.ds(0, 2)])
+        own_out = Bounce(expert_out.at[me.rep], out_held, w_out.at[me.line], local.at[pl.ds(2, 2)])
         if before:
 
             @pl.when(step == 0)
             def _():
                 meet([mate, across, beside, me.along(1), me.along(-1)])
-                for name in (("z", 1), ("z", -1), "x", "y", "c0"):
+                for name in (("relay", 1), ("relay", -1), ("z", 1), ("z", -1), "x", "y", "c0"):
                     copies[name].start()
-                pltpu.make_async_copy(dy, slot[own], local.at[0]).start()
-                pltpu.make_async_copy(in_pair, w_in.at[me.line], local.at[1]).start()
+                own_dy.start()
+                own_out.start()
 
             @pl.when(step == 3)
             def _():
+                own_dy.turn()
+                own_out.turn()
                 copies["x"].wait_recv()
                 copies["xy"].start()
                 copies["c1"].start()
                 copies["y"].wait_recv()
                 copies["yx"].start()
                 copies["c2"].start()
-                for shift in (1, -1):
-                    copies["z", shift].wait_recv()
-                    copies["relay", shift].start()
 
             return
 
@@ -382,12 +443,11 @@
             copies["xy"].wait_recv()
             copies["yx"].wait_recv()
             copies["c3"].start()
-            for shift in (1, -1):
-                copies["relay", shift].wait_recv()
-            for name in ("c0", "c1", "c2", "c3"):
-                copies[name].wait_recv()
-            pltpu.make_async_copy(dy, slot[own], local.at[0]).wait()
-            pltpu.make_async_copy(in_pair, w_in.at[me.line], local.at[1]).wait()
+            for name in plan:
+                if name not in ("x", "y", "xy", "yx"):
+                    copies[name].wait_recv()
+            own_dy.wait()
+            own_out.wait()
             for name in plan:
                 copies[name].wait_send()
 
@@ -398,15 +458,11 @@
     head_dim,
     place_ref,
     x_ref,
-    gain_one_ref,
-    gain_two_ref,
     wq_ref,
     wk_ref,
     wv_ref,
     wo_ref,
-    dist_ref,
-    routes_ref,
-    router_ref,
+    pack_ref,
     *refs,
 ):
     step = pl.program_id(0)
@@ -414,9 +470,9 @@
     behind_in, refs = refs[:n_in], refs[n_in:]
     q_out, k_out, v_out, o_out, lse_out, x_mid_out, message_out, probs_out, h_out = refs[:9]
     behind_out, refs = refs[9 : 9 + n_out], refs[9 + n_out :]
-    total_ref, mask_ref, bias_ref = refs[:3]
+    total_ref, mask_ref, bias_ref, dist_ref = refs[:4]
     if background:
-        background.run(step, True, behind_in, behind_out, refs[3:])
+        background.run(step, True, behind_in, behind_out, refs[4:])
     rows = x_mid_out.shape[0]
     length, width = x_ref.shape
     own = pl.ds(pl.multiple_of(first_row(rows), rows), rows)
@@ -424,7 +480,9 @@
     @pl.when(step == 0)
     def _():
         values = x_ref[...].astype(f32)
-        h_out[...] = (values * inverse_rms(values) * gain_one_ref[...]).astype(bf16)
+        gain_one = pack_ref[4:5, :width]
+        h_out[...] = (values * inverse_rms(values) * gain_one).astype(bf16)
+        dist_ref[...] = distances(pack_ref)
         total_ref[...] = jnp.zeros_like(total_ref)
         make_mask(place_ref, mask_ref)
 
@@ -436,10 +494,10 @@
     k_out[...] = k_low
     v_out[...] = v_low
     block = LANES
-    span = dist_ref.shape[2]
+    span = pack_ref.shape[1]
     first_half = lax.broadcasted_iota(jnp.int32, (block, LANES), 1) < head_dim
     for head in range(2):
-        bias_ref[head] = spread(dist_ref[0, head : head + 1, :], block, span)
+        bias_ref[head] = spread(dist_ref[pl.ds(2 * step + head, 1), :], block, span)
     for b in range(rows // block):
         here = slice(b * block, (b + 1) * block)
         offset = pl.multiple_of(length - LANES - block * b - first_row(rows), LANES)
@@ -464,33 +522,29 @@
     def _():
         x_mid = x_ref[own, :].astype(f32) + total_ref[...]
         x_mid_out[...] = x_mid
-        h_two = (x_mid * inverse_rms(x_mid) * gain_two_ref[...]).astype(bf16)
+        h_two = (x_mid * inverse_rms(x_mid) * pack_ref[5:6, :width]).astype(bf16)
         message_out[:, :width] = h_two
-        logits = exact_dot(h_two.astype(f32), router_ref[...])
+        logits = exact_dot_t(h_two.astype(f32), router_rows(pack_ref, n_experts, width))
         lane = lax.broadcasted_iota(jnp.int32, logits.shape, 1)
         logits = jnp.where(lane < n_experts, logits, masked_out)
         exp_logits = jnp.exp(logits - jnp.max(logits, -1, keepdims=True))
         probs = exp_logits / jnp.sum(exp_logits, -1, keepdims=True)
         probs_out[...] = probs
-        chosen = jnp.where(chosen_experts(routes_ref, probs.shape), probs, 0.0)
+        chosen = jnp.where(chosen_experts(pack_ref, probs.shape), probs, 0.0)
         gate = chosen / jnp.sum(chosen, -1, keepdims=True)
         high = gate.astype(bf16)
         low = gate - high.astype(f32)
         message_out[:, width:] = (high.astype(f32) + pltpu.roll(low, n_experts, 1)).astype(bf16)
 
     if background:
-        background.run(step, False, behind_in, behind_out, refs[3:])
+        background.run(step, False, behind_in, behind_out, refs[4:])
 
 
 def attention_forward(
     place,
     x_all,
-    gain_one,
-    gain_two,
     weights,
-    dist,
-    routes,
-    router,
+    pack,
     n_rows,
     n_experts,
     head_dim,
@@ -499,7 +553,7 @@
 ):
     length, width = x_all.shape
     pairs = width // LANES
-    span = dist.shape[2]
+    span = pack.shape[1]
     whole = lambda shape: pl.BlockSpec(shape, lambda p, *_: (0,) * len(shape))
     columns = lambda rows: pl.BlockSpec((rows, LANES), lambda p, *_: (0, p))
     matrix = lambda i: pl.BlockSpec((None, width, LANES), lambda p, *_: (i, 0, p))
@@ -515,10 +569,11 @@
         jax.ShapeDtypeStruct((length, width), bf16),
     ]
     anywhere = pl.BlockSpec(memory_space=pl.ANY)
-    params = {}
+    params, aliases = {}, {}
     if background:
-        out_shape += background.out_shape(n_rows, width, *behind[1].shape)
+        out_shape += background.out_shape(*behind)
         params = {"collective_id": 1, "has_side_effects": True}
+        aliases = {8: 10}
     return pl.pallas_call(
         functools.partial(forward_kernel, background, n_experts, head_dim),
         out_shape=out_shape,
@@ -527,15 +582,11 @@
             grid=(pairs,),
             in_specs=[
                 whole((length, width)),
-                whole((1, width)),
-                whole((1, width)),
                 matrix(0),
                 matrix(1),
                 matrix(2),
                 pl.BlockSpec((None, LANES, width), lambda p, *_: (3, p, 0)),
-                pl.BlockSpec((1, 2, span), lambda p, *_: (p, 0, 0)),
-                whole((n_rows, 2)),
-                whole((width, LANES)),
+                whole(pack.shape),
             ]
             + [anywhere] * len(behind),
             out_specs=[
@@ -554,9 +605,11 @@
                 pltpu.VMEM((n_rows, width), f32),
                 pltpu.VMEM((n_rows, length), f32),
                 pltpu.VMEM((2, LANES, span), f32),
+                pltpu.VMEM((16, span), f32),
             ]
-            + list(background.scratch if background else ()),
+            + (background.scratch(*behind) if background else []),
         ),
+        input_output_aliases=aliases,
         compiler_params=pltpu.CompilerParams(vmem_limit_bytes=VMEM_LIMIT, **params),
         cost_estimate=pl.CostEstimate(
             flops=20_000_000_000, transcendentals=0, bytes_accessed=20_000_000
@@ -565,15 +618,11 @@
     )(
         place,
         x_all,
-        gain_one,
-        gain_two,
         weights,
         weights,
         weights,
         weights,
-        dist,
-        routes,
-        router,
+        pack,
         *behind,
     )
 
@@ -695,42 +744,30 @@
     return (j + 1) // 2 % 4, (j + 1) % 2
 
 
-def plane_experts_kernel(
+def experts_up_kernel(
     n_experts,
     chunk,
     n_fsdp,
     message_ref,
     dy_ref,
     w_in_ref,
-    w_out_ref,
-    back_ref,
-    out_half,
-    dw_in_ref,
+    _,
+    h_out,
+    act_out,
+    slope_out,
     dw_out_ref,
+    w_out,
     h_ref,
-    part_ref,
-    tx_ref,
-    rx_ref,
-    fin_ref,
-    fin_out_ref,
-    land_ref,
-    dw_in_acc,
     dw_out_acc,
     send,
     recv,
-    tx_sem,
-    rx_sem,
-    fin_sem,
-    land_sem,
-    local,
 ):
     step = pl.program_id(0)
-    last = 7
+    last = pl.num_programs(0) - 1
     me = Place(n_fsdp)
     core = me.core
     rows, width = dy_ref.shape
     hidden = w_in_ref.shape[1]
-    long = message_ref.shape[1]
     half = rows // 2
     first, second = pl.ds(0, half), pl.ds(half, half)
     mate, across, beside = me.mate(), me.chip(1, 0), me.chip(0, 1)
@@ -745,15 +782,160 @@
         "c3": (slot[5 + core], slot[5 + core], mate),
         "xy": (slot[1 + core, first], slot[5 + core, first], across),
         "yx": (slot[3 + core, second], slot[5 + core, second], beside),
-    }
+    } | relay_plan(me, w_out)
     copies = Planned(plan, send, recv)
+
+    @pl.when(step == 0)
+    def _():
+        meet([mate, across, beside, me.along(1), me.along(-1)])
+        for name in ("c0", "x", "y", ("relay", 1), ("relay", -1)):
+            copies[name].start()
+        h_ref[own] = message_ref[...]
+        dw_out_acc[...] = jnp.zeros_like(dw_out_acc)
+
+    @pl.when(step == 2)
+    def _():
+        copies["x"].wait_recv()
+        copies["c1"].start()
+        copies["xy"].start()
+        copies["y"].wait_recv()
+        copies["c2"].start()
+        copies["yx"].start()
+
+    @pl.when(step == 6)
+    def _():
+        copies["xy"].wait_recv()
+        copies["yx"].wait_recv()
+        copies["c3"].start()
+
+    for q in range(4):
+
+        @pl.when(step == 2 * q + 1 - core)
+        def _():
+            copies[f"c{q}"].wait_recv()
+
+    now = (step + 7) % 8
+    expert = me.rep
+    h_out[...] = h_ref[now]
+    h = h_ref[now, :, :width]
+    extra = h_ref[now, :, width:].astype(f32)
+    lane = lax.broadcasted_iota(jnp.int32, extra.shape, 1)
+    mine = (lane == expert) | (lane == expert + n_experts)
+    gate = jnp.sum(jnp.where(mine, extra, 0.0), -1, keepdims=True)
+    dy = dy_ref[...]
+    for start in range(0, hidden, chunk):
+        piece = slice(start, start + chunk)
+        up = dot(h, w_in_ref[:, piece])
+        square = up * up
+        tanh = jnp.tanh(up * (GELU_A + GELU_B * square))
+        halved = 0.5 * up
+        more = 1.0 + tanh
+        act = (halved * more).astype(bf16)
+        slope = 0.5 * more + halved * (1.0 - tanh * tanh) * (GELU_A + 3.0 * GELU_B * square)
+        act_out[:, piece] = act
+        slope_out[:, piece] = slope.astype(bf16)
+        gated = (gate * act.astype(f32)).astype(bf16)
+        dw_out_acc[piece, :] += t_dot(gated, dy)
+
+    @pl.when(step == last)
+    def _():
+        dw_out_ref[...] = dw_out_acc[...].astype(bf16)
+        for shift in (1, -1):
+            copies["relay", shift].wait_recv()
+        for name in plan:
+            copies[name].wait_send()
+
+
+def experts_up(message, dy_all, w_in, w_out, n_experts, n_fsdp):
+    blocks, rows, width = dy_all.shape
+    long = message.shape[1]
+    hidden = w_in.shape[1]
+    once = pl.Buffered(1)
+    whole = lambda shape: pl.BlockSpec(shape, lambda i: (0,) * len(shape), pipeline_mode=once)
+    turn = lambda columns: pl.BlockSpec((None, rows, columns), lambda i: ((i + 7) % 8, 0, 0))
+    anywhere = pl.BlockSpec(memory_space=pl.ANY)
+    dma = lambda *shape: pltpu.SemaphoreType.DMA(shape)
+    return pl.pallas_call(
+        functools.partial(experts_up_kernel, n_experts, hidden, n_fsdp),
+        out_shape=[
+            jax.ShapeDtypeStruct((blocks, rows, long), bf16),
+            jax.ShapeDtypeStruct((blocks, rows, hidden), bf16),
+            jax.ShapeDtypeStruct((blocks, rows, hidden), bf16),
+            jax.ShapeDtypeStruct((hidden, width), bf16),
+            jax.ShapeDtypeStruct(w_out.shape, bf16),
+        ],
+        grid=(blocks,),
+        in_specs=[whole((rows, long)), turn(width), whole((width, hidden)), anywhere],
+        out_specs=[turn(long), turn(hidden), turn(hidden), whole((hidden, width)), anywhere],
+        scratch_shapes=[
+            pltpu.VMEM((blocks, rows, long), bf16),
+            pltpu.VMEM((hidden, width), f32),
+            dma(12),
+            dma(12),
+        ],
+        input_output_aliases={3: 4},
+        compiler_params=pltpu.CompilerParams(
+            vmem_limit_bytes=VMEM_LIMIT, collective_id=2, has_side_effects=True
+        ),
+        cost_estimate=pl.CostEstimate(
+            flops=20_000_000_000, transcendentals=0, bytes_accessed=30_000_000
+        ),
+        name="experts_up",
+    )(message, dy_all, w_in, w_out)
+
+
+def experts_down_kernel(
+    n_experts,
+    chunk,
+    n_fsdp,
+    message_ref,
+    dy_ref,
+    act_ref,
+    slope_ref,
+    w_in_ref,
+    w_out_ref,
+    dw_out,
+    back_ref,
+    out_half,
+    dw_in_ref,
+    sum_out,
+    part_ref,
+    tx_ref,
+    rx_ref,
+    fin_ref,
+    fin_out_ref,
+    land_ref,
+    dw_in_acc,
+    tx_send,
+    tx_recv,
+    fin_sem,
+    land_sem,
+    local,
+    near,
+    mid,
+    far,
+    own_ref,
+    line_send,
+    line_recv,
+    line_local,
+):
+    step = pl.program_id(0)
+    last = 7
+    me = Place(n_fsdp)
+    core = me.core
+    rows, width = dy_ref.shape
+    hidden = w_in_ref.shape[1]
+    long = message_ref.shape[1]
+    half = rows // 2
+    mate = me.mate()
+    adds = LineSum(me, dw_out, near, mid, far, own_ref, line_send, line_recv, line_local)
 
     def to_mate(j):
         return pltpu.make_async_remote_copy(
             src_ref=tx_ref.at[j % 2],
             dst_ref=rx_ref.at[j],
-            send_sem=tx_sem.at[j],
-            recv_sem=rx_sem.at[j],
+            send_sem=tx_send.at[j],
+            recv_sem=tx_recv.at[j],
             device_id=mate,
             device_id_type=MESH,
         )
@@ -776,7 +958,7 @@
         q, k = plane_slot(j)
         return (q == 0) & (k == core)
 
-    def finish(j):
+    def finish_block(j):
         to_mate(j).wait_recv()
         mine = part_ref.at[j % 2, pl.ds(core * half, half)]
 
@@ -788,8 +970,6 @@
         def _():
             to_owner(j - 2).wait_send()
 
-        fin_out_ref[j % 2] = (mine[:, long:] + rx_ref[j, :, long:].astype(f32)).astype(bf16)
-        keep_out(j).start()
         fin_ref[j % 2] = (mine[:, :long] + rx_ref[j, :, :long].astype(f32)).astype(bf16)
 
         @pl.when(stays(j))
@@ -800,44 +980,26 @@
         def _():
             to_owner(j).start()
 
+        fin_out_ref[j % 2] = (mine[:, long:] + rx_ref[j, :, long:].astype(f32)).astype(bf16)
+        keep_out(j).start()
+
     @pl.when(step == 0)
     def _():
-        meet([mate, across, beside, me.chip(1, 1), me.chip(1, 0, 1 - core), me.chip(0, 1, 1 - core), me.chip(1, 1, 1 - core)])
-        copies["x"].start()
-        copies["y"].start()
-        copies["c0"].start()
-        h_ref[own] = message_ref[...]
+        partners = [mate, me.along(1), me.along(-1)]
+        for q in (1, 2, 3):
+            for k in (0, 1):
+                partners.append(me.chip(q // 2, q % 2, (core + k) % 2))
+        meet(partners)
+        adds.start()
         dw_in_acc[...] = jnp.zeros_like(dw_in_acc)
-        dw_out_acc[...] = jnp.zeros_like(dw_out_acc)
-        copies["c0"].wait_recv()
-
-    @pl.when(step == 1)
+
+    @pl.when(step == 3)
     def _():
-        copies["x"].wait_recv()
-        copies["c1"].start()
-        copies["xy"].start()
-
-    @pl.when(step == 2)
-    def _():
-        copies["y"].wait_recv()
-        copies["c2"].start()
-        copies["yx"].start()
-
-    @pl.when(step == 4)
-    def _():
-        copies["xy"].wait_recv()
-        copies["yx"].wait_recv()
-        copies["c3"].start()
-
-    for q in (1, 2, 3):
-
-        @pl.when(step == 2 * q - core)
-        def _():
-            copies[f"c{q}"].wait_recv()
+        adds.turn()
 
     expert = me.rep
-    h = h_ref[step, :, :width]
-    extra = h_ref[step, :, width:].astype(f32)
+    h_turned = message_ref[:, :width].T
+    extra = message_ref[:, width:].astype(f32)
     lane = lax.broadcasted_iota(jnp.int32, extra.shape, 1)
     mine = (lane == expert) | (lane == expert + n_experts)
     gate = jnp.sum(jnp.where(mine, extra, 0.0), -1, keepdims=True)
@@ -846,17 +1008,11 @@
     part = part_ref.at[step % 2]
     for start in range(0, hidden, chunk):
         piece = slice(start, start + chunk)
-        up = dot(h, w_in_ref[:, piece])
+        act = act_ref[:, piece].astype(f32)
         dact = dot_t(dy, w_out_ref[piece, :])
-        square = up * up
-        tanh = jnp.tanh(up * (GELU_A + GELU_B * square))
-        halved = 0.5 * up
-        more = 1.0 + tanh
-        act = halved * more
-        slope = 0.5 * more + halved * (1.0 - tanh * tanh) * (GELU_A + 3.0 * GELU_B * square)
         gated = (gate * act).astype(bf16)
         dgate_part = jnp.sum(act * dact, -1, keepdims=True)
-        dup = (gate * dact * slope).astype(bf16)
+        dup = (gate * dact * slope_ref[:, piece].astype(f32)).astype(bf16)
         out_part = dot(gated, w_out_ref[piece, :])
         dh_part = dot_t(dup, w_in_ref[:, piece])
         if start == 0:
@@ -866,13 +1022,12 @@
             part[:, long:] += out_part
             part[:, :width] += dh_part
         dgate = dgate_part if dgate is None else dgate + dgate_part
-        dw_out_acc[piece, :] += t_dot(gated, dy)
-        dw_in_acc[:, piece] += t_dot(h, dup)
+        dw_in_acc[:, piece] += dot(h_turned, dup)
         if start == 0:
 
             @pl.when(step >= 1)
             def _():
-                finish(step - 1)
+                finish_block(step - 1)
 
     high = dgate.astype(bf16).astype(f32)
     low = dgate - high
@@ -890,8 +1045,8 @@
     @pl.when(step == last)
     def _():
         dw_in_ref[...] = dw_in_acc[...].astype(bf16)
-        dw_out_ref[...] = dw_out_acc[...].astype(bf16)
-        finish(last)
+        finish_block(last)
+        sum_out[...] = adds.total()
         to_mate(last - 1).wait_send()
         to_mate(last).wait_send()
         keep_out(last - 1).wait()
@@ -902,8 +1057,6 @@
         def _():
             to_owner(last).wait_send()
 
-        for name in plan:
-            copies[name].wait_send()
         for side in range(2):
             total = None
             for q in range(4):
@@ -928,38 +1081,42 @@
             back_ref[side * half : (side + 1) * half, :] = total
 
 
-def plane_experts(message, dy_all, w_in, w_out, n_experts, n_fsdp):
+def experts_down(message_all, dy_all, act, slope, w_in, w_out, dw_out, n_experts, n_fsdp):
     blocks, rows, width = dy_all.shape
-    long = message.shape[1]
+    long = message_all.shape[2]
     hidden = w_in.shape[1]
     half = rows // 2
     once = pl.Buffered(1)
     whole = lambda shape: pl.BlockSpec(shape, lambda i: (0,) * len(shape), pipeline_mode=once)
+    block = lambda columns: pl.BlockSpec((None, rows, columns), lambda i: (i, 0, 0))
+    anywhere = pl.BlockSpec(memory_space=pl.ANY)
     both = long + width
     dma = lambda *shape: pltpu.SemaphoreType.DMA(shape)
     return pl.pallas_call(
-        functools.partial(plane_experts_kernel, n_experts, 512, n_fsdp),
+        functools.partial(experts_down_kernel, n_experts, 512, n_fsdp),
         out_shape=[
             jax.ShapeDtypeStruct((rows, long), f32),
             jax.ShapeDtypeStruct((blocks, half, width), bf16),
             jax.ShapeDtypeStruct((width, hidden), bf16),
-            jax.ShapeDtypeStruct((hidden, width), bf16),
+            jax.ShapeDtypeStruct(dw_out.shape[1:], bf16),
         ],
         grid=(blocks,),
         in_specs=[
-            whole((rows, long)),
-            pl.BlockSpec((None, rows, width), lambda i: (i, 0, 0)),
+            block(long),
+            block(width),
+            block(hidden),
+            block(hidden),
             whole((width, hidden)),
             whole((hidden, width)),
+            anywhere,
         ],
         out_specs=[
             whole((rows, long)),
-            pl.BlockSpec(memory_space=pl.ANY),
+            anywhere,
             whole((width, hidden)),
-            whole((hidden, width)),
+            whole(dw_out.shape[1:]),
         ],
         scratch_shapes=[
-            pltpu.VMEM((blocks, rows, long), bf16),
             pltpu.VMEM((2, rows, both), f32),
             pltpu.VMEM((2, half, both), bf16),
             pltpu.VMEM((blocks, half, both), bf16),
@@ -967,23 +1124,21 @@
             pltpu.VMEM((2, half, width), bf16),
             pltpu.VMEM((4, 2, half, long), bf16),
             pltpu.VMEM((width, hidden), f32),
-            pltpu.VMEM((hidden, width), f32),
-            dma(8),
-            dma(8),
             dma(8),
             dma(8),
             dma(8),
             dma(4, 2),
             dma(8),
-        ],
+        ]
+        + LineSum.scratch(*dw_out.shape[1:]),
         compiler_params=pltpu.CompilerParams(
-            vmem_limit_bytes=VMEM_LIMIT, collective_id=2, has_side_effects=True
+            vmem_limit_bytes=VMEM_LIMIT, collective_id=3, has_side_effects=True
         ),
         cost_estimate=pl.CostEstimate(
-            flops=60_000_000_000, transcendentals=0, bytes_accessed=30_000_000
+            flops=40_000_000_000, transcendentals=0, bytes_accessed=40_000_000
         ),
-        name="plane_experts",
-    )(message, dy_all, w_in, w_out)
+        name="experts_down",
+    )(message_all, dy_all, act, slope, w_in, w_out, dw_out)
 
 
 class LineSum:
@@ -1047,34 +1202,39 @@
 
 
 class BackgroundBack:
-    n_in, n_out = 3, 2
+    n_in, n_out = 2, 2
 
     def __init__(self, n_fsdp):
         self.n_fsdp = n_fsdp
 
-    def out_shape(self, out_half, dw_out, x_mid):
+    def out_shape(self, out_half, dw_in):
+        half, width = out_half.shape[1:]
         return [
-            jax.ShapeDtypeStruct(x_mid.shape, bf16),
-            jax.ShapeDtypeStruct(dw_out.shape[1:], bf16),
+            jax.ShapeDtypeStruct((2 * half, width), bf16),
+            jax.ShapeDtypeStruct(dw_in.shape[1:], bf16),
         ]
 
-    def scratch(self, out_half, dw_out, x_mid):
+    def out_specs(self, shapes):
+        whole = lambda shape: pl.BlockSpec(shape, lambda p, *_: (0,) * len(shape))
+        return [whole(s.shape) for s in shapes]
+
+    def scratch(self, out_half, dw_in):
         half, width = out_half.shape[1:]
         return [
             pltpu.VMEM((4, 2, half, width), bf16),
             pltpu.SemaphoreType.DMA((8,)),
             pltpu.SemaphoreType.DMA((4, 2)),
-        ] + LineSum.scratch(*dw_out.shape[1:])
+        ] + LineSum.scratch(*dw_in.shape[1:])
 
     def run(self, step, before, ins, outs, scratch, x_mid):
-        out_half, dw_out, _ = ins
-        out_rows, sum_out = outs
+        out_half, dw_in = ins
+        out_rows, sum_in = outs
         land, send, recv = scratch[:3]
         near, mid, far, mine, line_send, line_recv, line_local = scratch[3:]
         me = Place(self.n_fsdp)
         core = me.core
         half = out_half.shape[1]
-        line = LineSum(me, dw_out, near, mid, far, mine, line_send, line_recv, line_local)
+        line = LineSum(me, dw_in, near, mid, far, mine, line_send, line_recv, line_local)
 
         def to_owner(j):
             q, k = plane_slot(j)
@@ -1157,7 +1317,7 @@
                         arrived.wait_recv()
                     total = total + land[q, side].astype(f32)
                 out_rows[here, :] = total.astype(bf16)
-            sum_out[...] = line.total()
+            sum_in[...] = line.total()
 
 
 def backward_kernel(
@@ -1170,9 +1330,7 @@
     x_mid_ref,
     message_ref,
     probs_ref,
-    routes_ref,
-    router_ref,
-    gain_two_ref,
+    pack_ref,
     h_ref,
     wq_ref,
     wk_ref,
@@ -1183,7 +1341,6 @@
     v_ref,
     o_ref,
     lse_ref,
-    dist_ref,
     *refs,
 ):
     step = pl.program_id(0)
@@ -1192,9 +1349,9 @@
     dwq_out, dwk_out, dwv_out, dwo_out, dh_own_out, dh_other_out = refs[:6]
     dx_mid_out, gain_out, router_out, ddist_out = refs[6:10]
     behind_out, refs = refs[10 : 10 + n_out], refs[10 + n_out :]
-    da_ref, dh_all_ref, dh_mine_ref, mask_ref, bias_ref, dbias_ref, dq_ref = refs[:7]
+    da_ref, dh_all_ref, dh_mine_ref, mask_ref, bias_ref, dbias_ref, dq_ref, dist_ref = refs[:8]
     if background:
-        background.run(step, True, behind_in, behind_out, refs[7:], x_mid_ref)
+        background.run(step, True, behind_in, behind_out, refs[8:], x_mid_ref)
     rows, width = x_mid_ref.shape
     length = h_ref.shape[0]
     own = pl.ds(pl.multiple_of(first_row(rows), rows), rows)
@@ -1202,7 +1359,7 @@
     @pl.when(step == 0)
     def _():
         probs = probs_ref[...]
-        chosen = chosen_experts(routes_ref, probs.shape)
+        chosen = chosen_experts(pack_ref, probs.shape)
         picked = jnp.where(chosen, probs, 0.0)
         total = jnp.sum(picked, -1, keepdims=True)
         gate = picked / total
@@ -1220,21 +1377,25 @@
             precision=highest,
             preferred_element_type=f32,
         )
-        dh_two = back_ref[:, :width].astype(f32) + exact_dot_t(dlogits, router_ref[...])
-        dx, dgain = norm_back(x_mid_ref[...], gain_two_ref[...], dh_two)
+        dh_two = back_ref[:, :width].astype(f32) + exact_dot(
+            dlogits, router_rows(pack_ref, n_experts, width)
+        )
+        dx, dgain = norm_back(x_mid_ref[...], pack_ref[5:6, :width], dh_two)
         gain_out[...] = dgain
         dx_mid = dx + dy_ref[...].astype(f32)
         dx_mid_out[...] = dx_mid
         da_ref[...] = dx_mid.astype(bf16)
         dh_all_ref[...] = jnp.zeros_like(dh_all_ref)
         dh_mine_ref[...] = jnp.zeros_like(dh_mine_ref)
+        ddist_out[...] = jnp.zeros_like(ddist_out)
+        dist_ref[...] = distances(pack_ref)
         make_mask(place_ref, mask_ref)
 
     da = da_ref[...]
     do = dot_t(da, wo_ref[...]).astype(bf16)
     dwo_out[...] = t_dot(o_ref[...], da).astype(bf16)
     block = LANES
-    span = dist_ref.shape[2]
+    span = pack_ref.shape[1]
     first_half = lax.broadcasted_iota(jnp.int32, (block, LANES), 1) < head_dim
     zero = jnp.zeros((), bf16)
     k_low = k_ref[...]
@@ -1242,7 +1403,7 @@
     dk = None
     dv = None
     for head in range(2):
-        bias_ref[head] = spread(dist_ref[0, head : head + 1, :], block, span)
+        bias_ref[head] = spread(dist_ref[pl.ds(2 * step + head, 1), :], block, span)
         dbias_ref[head] = jnp.zeros_like(dbias_ref[head])
     for b in range(rows // block):
         here = slice(b * block, (b + 1) * block)
@@ -1270,7 +1431,7 @@
             jnp.where(first_half, halves[0], halves[1]) * (head_dim**-0.5)
         ).astype(bf16)
     for head in range(2):
-        ddist_out[0, head : head + 1, :] = gather_diagonals(dbias_ref[head])
+        ddist_out[pl.ds(2 * step + head, 1), :] = gather_diagonals(dbias_ref[head])
     dq = dq_ref[...]
     dk = dk.astype(bf16)
     dv = dv.astype(bf16)
@@ -1288,7 +1449,7 @@
         dh_other_out[...] = dh_all_ref[other, :].astype(bf16)
 
     if background:
-        background.run(step, False, behind_in, behind_out, refs[7:], x_mid_ref)
+        background.run(step, False, behind_in, behind_out, refs[8:], x_mid_ref)
 
 
 def attention_backward(
@@ -1298,9 +1459,7 @@
     x_mid,
     message,
     probs,
-    routes,
-    router,
-    gain_two,
+    pack,
     h_all,
     weights,
     q,
@@ -1308,7 +1467,6 @@
     v,
     o,
     lse,
-    dist,
     n_experts,
     head_dim,
     background=None,
@@ -1317,12 +1475,12 @@
     n_rows, width = x_mid.shape
     length = h_all.shape[0]
     pairs = width // LANES
-    span = dist.shape[2]
+    span = pack.shape[1]
     more_shapes, more_scratch, params = [], [], {}
     if background:
         more_shapes = background.out_shape(*behind)
         more_scratch = background.scratch(*behind)
-        params = {"collective_id": 3, "has_side_effects": True}
+        params = {"collective_id": 4, "has_side_effects": True}
     anywhere = pl.BlockSpec(memory_space=pl.ANY)
     whole = lambda shape: pl.BlockSpec(shape, lambda p, *_: (0,) * len(shape))
     columns = lambda rows: pl.BlockSpec((rows, LANES), lambda p, *_: (0, p))
@@ -1339,7 +1497,7 @@
             jax.ShapeDtypeStruct((n_rows, width), f32),
             jax.ShapeDtypeStruct((1, width), f32),
             jax.ShapeDtypeStruct((LANES, width), f32),
-            jax.ShapeDtypeStruct((pairs, 2, span), f32),
+            jax.ShapeDtypeStruct((16, span), f32),
         ]
         + more_shapes,
         grid_spec=pltpu.PrefetchScalarGridSpec(
@@ -1351,9 +1509,7 @@
                 whole((n_rows, width)),
                 whole((n_rows, width + LANES)),
                 whole((n_rows, LANES)),
-                whole((n_rows, 2)),
-                whole((width, LANES)),
-                whole((1, width)),
+                whole(pack.shape),
                 whole((length, width)),
                 matrix(0),
                 matrix(1),
@@ -1364,7 +1520,6 @@
                 columns(length),
                 columns(n_rows),
                 columns(n_rows),
-                pl.BlockSpec((1, 2, span), lambda p, *_: (p, 0, 0)),
             ]
             + [anywhere] * len(behind),
             out_specs=[
@@ -1377,9 +1532,9 @@
                 whole((n_rows, width)),
                 whole((1, width)),
                 whole((LANES, width)),
-                pl.BlockSpec((1, 2, span), lambda p, *_: (p, 0, 0)),
+                whole((16, span)),
             ]
-            + [whole(s.shape) for s in more_shapes],
+            + (background.out_specs(more_shapes) if background else []),
             scratch_shapes=[
                 pltpu.VMEM((n_rows, width), bf16),
                 pltpu.VMEM((length, width), f32),
@@ -1388,6 +1543,7 @@
                 pltpu.VMEM((2, LANES, span), f32),
                 pltpu.VMEM((2, LANES, span), f32),
                 pltpu.VMEM((n_rows, LANES), bf16),
+                pltpu.VMEM((16, span), f32),
             ]
             + more_scratch,
         ),
@@ -1403,9 +1559,7 @@
         x_mid,
         message,
         probs,
-        routes,
-        router,
-        gain_two,
+        pack,
         h_all,
         weights,
         weights,
@@ -1416,7 +1570,6 @@
         v,
         o,
         lse,
-        dist,
         *behind,
     )
 
@@ -1429,53 +1582,47 @@
     dwk,
     dwv,
     dwo,
+    sum_in,
     sum_out,
-    dw_in,
     dh_other,
     dh_own_ref,
     dx_mid_ref,
     tokens_ref,
-    gain_one_ref,
+    pack_ref,
     dgain_two_ref,
     drouter_ref,
     ddist_ref,
-    match_ref,
     attn_out,
     grad_in,
     grad_out,
     tokens_out,
-    small_ref,
+    small_out,
     mine_ref,
     rx_ref,
     land_ref,
     line_ref,
     line_land,
     dh_land,
-    in_ref,
-    small_land,
-    near,
-    mid,
-    far,
-    own_ref,
-    line_send,
-    line_recv,
-    line_local,
+    small_plane,
+    small_line,
+    in_held,
+    out_held,
     send,
     recv,
     local,
 ):
     me = Place(n_fsdp)
     rep, line, seq, core, row = me.rep, me.line, me.seq, me.core, me.row
+    width = tokens_ref.shape[1]
     mate, across, beside, corner = me.mate(), me.chip(1, 0), me.chip(0, 1), me.chip(1, 1)
     far_row = (row + 1) % 2
     far_rep = far_row * 2 + core
-    pieces = dw_in.shape[0]
-    part_out = grad_out.shape[1]
-    part_in = grad_in.shape[1]
+    part_out = sum_out.shape[0]
     columns = lambda z, x: pl.ds(pl.multiple_of((z * 2 + x) * part_out, LANES), part_out)
-    flip = lambda place: place + 1 - 2 * (place % 2)
-    hop = lambda place: (rep, place, seq)
-    cube = [mate, across, beside, hop(flip(line)), hop((line + 2) % n_fsdp)]
+    here = rep * 2 + seq
+    peers = [mate, across, beside, corner]
+    peers += [me.chip(1, 0, 1 - core), me.chip(0, 1, 1 - core), me.chip(1, 1, 1 - core)]
+    shifts = (1, -1, 2)
     plan = {
         "pair0": (None, rx_ref.at[0], mate),
         "pair1": (None, rx_ref.at[1], mate),
@@ -1486,26 +1633,26 @@
         "to_y": (mine_ref.at[far_row, :, seq], land_ref.at[1], across),
         "to_xy": (mine_ref.at[far_row, :, 1 - seq], land_ref.at[2], corner),
         "to_x": (mine_ref.at[row, :, 1 - seq], land_ref.at[0], beside),
-        "attn_c": (attn_out.at[rep], attn_out.at[rep], mate),
-        "attn_y": (attn_out.at[rep], attn_out.at[rep], across),
+        "attn_c": (line_land.at[3], attn_out.at[rep], mate),
+        "attn_y": (line_land.at[3], attn_out.at[rep], across),
         "attn_f": (attn_out.at[far_rep], attn_out.at[far_rep], mate),
         "in_c": (grad_in.at[rep], grad_in.at[rep], mate),
         "in_y": (grad_in.at[rep], grad_in.at[rep], across),
         "in_f": (grad_in.at[far_rep], grad_in.at[far_rep], mate),
     }
-    for i, shift in enumerate((1, -1, 2)):
+    for i, shift in enumerate(shifts):
         target = (line + shift) % n_fsdp
         plan["line", i] = (line_ref.at[target], line_land.at[i], me.along(shift))
+        plan["small_z", i] = (small_line.at[line], small_line.at[line], me.along(shift))
     for z in range(n_fsdp):
         plan["in_x", z] = (
-            in_ref.at[1 - seq, :, pl.ds(z * part_out, part_out)],
+            sum_in.at[1 - seq, :, pl.ds(z * part_out, part_out)],
             grad_in.at[rep, :, columns(z, seq)],
             beside,
         )
-    for i, partner in enumerate(cube):
-        plan["small", i] = (small_ref, small_land.at[i], partner)
+    for i, peer in enumerate(peers):
+        plan["small", i] = (small_plane.at[here], small_plane.at[here], peer)
     copies = Planned(plan, send, recv)
-    adds = LineSum(me, dw_in, near, mid, far, own_ref, line_send, line_recv, line_local)
     matrices = (dwq, dwk, dwv, dwo)
 
     def pair(side, i):
@@ -1515,9 +1662,8 @@
     keep = lambda side, i: pltpu.make_async_copy(
         matrices[2 * i + side], mine_ref.at[i], local.at[i]
     )
-    own_out = lambda: pltpu.make_async_copy(sum_out, grad_out.at[rep], local.at[2])
-
-    meet([mate, across, beside, corner, me.along(1), me.along(-1), me.along(2)])
+
+    meet(peers + [me.along(shift) for shift in shifts])
     for side in (0, 1):
 
         @pl.when(core == side)
@@ -1526,39 +1672,49 @@
                 pair(side, i).start()
                 keep(side, i).start()
 
-    adds.start()
-    copies["dh"].start()
+    for z in range(n_fsdp):
+        copies["in_x", z].start()
     copies["out_y"].start()
-    copies["out_c"].start()
-    own_out().start()
+    own_in = pltpu.make_async_copy(sum_in.at[seq], in_held, local.at[2])
+    own_in.start()
+    own_out = Bounce(sum_out, out_held, grad_out.at[rep], local.at[pl.ds(8, 2)])
+    own_out.start()
     for i in (0, 1):
         keep(0, i).wait()
         pair(0, i).wait_recv()
-    for i in (0, 1):
+    for i, names in ((far_row, ("to_y", "to_xy")), (row, ("to_x",))):
         total = mine_ref[i].astype(f32) + rx_ref[i].astype(f32)
         mine_ref[i] = total.astype(bf16)
-    copies["to_y"].start()
-    copies["to_x"].start()
-    copies["to_xy"].start()
-    small_ref[...] = jnp.zeros_like(small_ref)
-    small_ref[1:2, :] = dgain_two_ref[...]
-    small_ref[2 : 2 + n_experts, :] = drouter_ref[:n_experts, :]
-    small_ref[8 : 8 + n_heads, :LANES] = exact_dot_t(ddist_ref[...], match_ref[...])
-    adds.turn()
-    copies["dh"].wait_recv()
-    dh_one = dh_own_ref[...] + dh_land[...].astype(f32)
-    dx, dgain_one = norm_back(tokens_ref[...].astype(f32), gain_one_ref[...], dh_one)
-    tokens_out[...] = (dx_mid_ref[...] + dx).astype(bf16)
-    small_ref[0:1, :] = dgain_one
+        for name in names:
+            copies[name].start()
+    copies["out_c"].start()
+    own_out.turn()
+    own_in.wait()
+    kept = []
+    for z in range(n_fsdp):
+        source = in_held.at[:, pl.ds(z * part_out, part_out)]
+        target = grad_in.at[rep, :, columns(z, seq)]
+        kept.append(pltpu.make_async_copy(source, target, local.at[4 + z]))
+        kept[-1].start()
+    table = exact_dot_t(ddist_ref[...], bucket_match(pack_ref))
+    small = small_plane.at[here]
+    small[...] = jnp.zeros_like(small_out)
+    small[1:2, :] = dgain_two_ref[...]
+    small[2 : 2 + n_experts, :] = drouter_ref[:n_experts, :]
+    for head in range(n_heads):
+        at = head % 6 * LANES
+        small[6 + head // 6, at : at + LANES] = table[head]
+    for copy in kept:
+        copy.wait()
+    for z in range(n_fsdp):
+        copies["in_x", z].wait_recv()
+    copies["in_c"].start()
     copies["out_y"].wait_recv()
     copies["out_f"].start()
-    for i in range(len(cube)):
-        copies["small", i].start()
-        copies["small", i].wait_recv()
-        copies["small", i].wait_send()
-        small_ref[...] = small_ref[...] + small_land[i]
     copies["to_x"].wait_recv()
+    copies["dh"].start()
     copies["to_y"].wait_recv()
+    copies["in_y"].start()
     copies["to_xy"].wait_recv()
     for z in range(n_fsdp):
         total = mine_ref[row, z, seq].astype(f32)
@@ -1567,66 +1723,69 @@
         line_ref[z] = total.astype(bf16)
     for i in range(3):
         copies["line", i].start()
-    in_ref[...] = adds.total().reshape(in_ref.shape)
-    for z in range(n_fsdp):
-        copies["in_x", z].start()
-    kept = []
-    for z in range(n_fsdp):
-        source = in_ref.at[seq, :, pl.ds(z * part_out, part_out)]
-        target = grad_in.at[rep, :, columns(z, seq)]
-        kept.append(pltpu.make_async_copy(source, target, local.at[4 + z]))
-        kept[-1].start()
+    copies["dh"].wait_recv()
+    dh_one = dh_own_ref[...] + dh_land[...].astype(f32)
+    gain_one = pack_ref[4:5, :width]
+    dx, dgain_one = norm_back(tokens_ref[...].astype(f32), gain_one, dh_one)
+    small[0:1, :] = dgain_one
+    for i in range(len(peers)):
+        copies["small", i].start()
+    tokens_out[...] = (dx_mid_ref[...] + dx).astype(bf16)
     total = line_ref[line].astype(f32)
     for i in range(3):
         copies["line", i].wait_recv()
         total = total + line_land[i].astype(f32)
     line_land[3] = total.astype(bf16)
+    copies["attn_y"].start()
+    copies["attn_c"].start()
     own_attn = pltpu.make_async_copy(line_land.at[3], attn_out.at[rep], local.at[3])
     own_attn.start()
-    own_attn.wait()
-    copies["attn_y"].start()
-    copies["attn_c"].start()
-    for copy in kept:
-        copy.wait()
-    for z in range(n_fsdp):
-        copies["in_x", z].wait_recv()
-    copies["in_y"].start()
-    copies["in_c"].start()
+    for i in range(len(peers)):
+        copies["small", i].wait_recv()
+    total = small_plane[0]
+    for i in range(1, 8):
+        total = total + small_plane[i]
+    small_line[line] = total
+    for i in range(3):
+        copies["small_z", i].start()
+    copies["in_y"].wait_recv()
+    copies["in_f"].start()
     copies["attn_y"].wait_recv()
     copies["attn_f"].start()
-    copies["in_y"].wait_recv()
-    copies["in_f"].start()
-    own_out().wait()
-    for name in ("out_c", "out_f", "attn_c", "attn_f", "in_c", "in_f"):
+    for i in range(3):
+        copies["small_z", i].wait_recv()
+    total = small_line[0]
+    for i in range(1, n_fsdp):
+        total = total + small_line[i]
+    small_out[...] = total
+    own_attn.wait()
+    own_out.wait()
+    for name in ("attn_c", "attn_f", "in_c", "in_f", "out_c", "out_f"):
         copies[name].wait_recv()
     for name in plan:
-        if name[0] != "small":
-            copies[name].wait_send()
+        copies[name].wait_send()
 
 
 def finish(
     attn_grads,
+    sum_in,
     sum_out,
-    dw_in,
     dh_other,
     dh_own,
     dx_mid,
     tokens,
-    gain_one,
+    pack,
     dgain_two,
     drouter,
     ddist,
-    match,
     n_fsdp,
     n_experts,
-    part_in,
+    n_heads,
     hidden,
 ):
     n_rows, width = tokens.shape
-    n_heads = ddist.shape[0]
     part_attn = width // (2 * n_fsdp)
-    part_out = sum_out.shape[0]
-    pair_rows, columns = dw_in.shape[1:]
+    part_in = sum_in.shape[1]
     anywhere = pl.BlockSpec(memory_space=pl.ANY)
     inside = pl.BlockSpec(memory_space=pltpu.VMEM)
     dma = lambda n: pltpu.SemaphoreType.DMA((n,))
@@ -1637,11 +1796,11 @@
         out_shape=[
             jax.ShapeDtypeStruct((4, part_attn, width), bf16),
             jax.ShapeDtypeStruct((n_experts, part_in, hidden), bf16),
-            jax.ShapeDtypeStruct((n_experts, part_out, width), bf16),
+            jax.ShapeDtypeStruct((n_experts,) + sum_out.shape, bf16),
             jax.ShapeDtypeStruct((n_rows, width), bf16),
-            jax.ShapeDtypeStruct((24, width), f32),
+            jax.ShapeDtypeStruct((8, width), f32),
         ],
-        in_specs=[anywhere] * 7 + [inside] * 8,
+        in_specs=[anywhere] * 7 + [inside] * 7,
         out_specs=[anywhere] * 3 + [inside] * 2,
         scratch_shapes=[
             pltpu.VMEM((2,) + split, bf16),
@@ -1650,29 +1809,79 @@
             pltpu.VMEM((n_fsdp, part_attn, width), bf16),
             pltpu.VMEM((4, part_attn, width), bf16),
             pltpu.VMEM((n_rows, width), bf16),
-            pltpu.VMEM((2, part_in, columns), bf16),
-            pltpu.VMEM((5, 24, width), f32),
-        ]
-        + LineSum.scratch(pair_rows, columns)
-        + [dma(32), dma(32), dma(12)],
+            pltpu.VMEM((8, 8, width), f32),
+            pltpu.VMEM((n_fsdp, 8, width), f32),
+            pltpu.VMEM(sum_in.shape[1:], bf16),
+            pltpu.VMEM(sum_out.shape, bf16),
+            dma(40),
+            dma(40),
+            dma(12),
+        ],
         compiler_params=pltpu.CompilerParams(
-            vmem_limit_bytes=VMEM_LIMIT, collective_id=4, has_side_effects=True
+            vmem_limit_bytes=VMEM_LIMIT, collective_id=5, has_side_effects=True
         ),
         name="finish_gradients",
     )(
         *attn_grads,
+        sum_in,
         sum_out,
-        dw_in,
         dh_other,
         dh_own,
         dx_mid,
         tokens,
-        gain_one,
+        pack,
         dgain_two,
         drouter,
         ddist,
-        match,
     )
+
+
+def widen_kernel(
+    n_experts, n_heads, n_buckets, attn, grad_in, grad_out, small, q, k, v, o, win, wout, *rest
+):
+    step = pl.program_id(0)
+    for i, target in enumerate((q, k, v, o)):
+
+        @pl.when(step == i)
+        def _():
+            target[...] = attn[...].astype(f32)
+
+    win[...] = grad_in[...].astype(f32)
+    wout[...] = grad_out[...].astype(f32)
+    gain_one, gain_two, table, router = rest
+
+    @pl.when(step == 0)
+    def _():
+        gain_one[...] = small[0:1, :]
+        gain_two[...] = small[1:2, :]
+        router[...] = small[2 : 2 + n_experts, :]
+        for head in range(n_heads):
+            at = head % 6 * LANES
+            table[head : head + 1, :] = small[
+                6 + head // 6 : 7 + head // 6, at : at + n_buckets
+            ]
+
+
+def widen(attn, grad_in, grad_out, small, n_heads, n_buckets):
+    n_experts = grad_in.shape[0]
+    width = small.shape[1]
+    own = lambda a: pl.BlockSpec((None,) + a.shape[1:], lambda i: (i, 0, 0))
+    whole = lambda shape: pl.BlockSpec(shape, lambda i: (0,) * len(shape))
+    small_shapes = [(1, width), (1, width), (n_heads, n_buckets), (n_experts, width)]
+    wide = [attn.shape[1:]] * 4
+    return pl.pallas_call(
+        functools.partial(widen_kernel, n_experts, n_heads, n_buckets),
+        out_shape=[jax.ShapeDtypeStruct(shape, f32) for shape in wide]
+        + [jax.ShapeDtypeStruct(a.shape, f32) for a in (grad_in, grad_out)]
+        + [jax.ShapeDtypeStruct(shape, f32) for shape in small_shapes],
+        grid=(n_experts,),
+        in_specs=[own(attn), own(grad_in), own(grad_out), whole(small.shape)],
+        out_specs=[whole(shape) for shape in wide]
+        + [own(grad_in), own(grad_out)]
+        + [whole(shape) for shape in small_shapes],
+        compiler_params=pltpu.CompilerParams(vmem_limit_bytes=VMEM_LIMIT),
+        name="widen",
+    )(attn, grad_in, grad_out, small)
 
 
 def per_device(
@@ -1710,8 +1919,8 @@
     near = n_fsdp == 4 and part_attn % 16 == 0
     pick = lambda array: lax.dynamic_index_in_dim(array, rep, 0, keepdims=False)
     if near:
-        weights, x_all, in_pair, w_out = gather(
-            (attn_q, attn_k, attn_v, attn_o), tokens, expert_in, expert_out, n_fsdp
+        weights, x_all, w_in = gather(
+            (attn_q, attn_k, attn_v, attn_o), tokens, expert_in, part_out, n_fsdp
         )
     else:
         attn_own = pick(jnp.stack([attn_q, attn_k, attn_v, attn_o]))
@@ -1728,40 +1937,39 @@
         w_out = lax.all_gather(pick(expert_out), "fsdp", axis=0, tiled=True)
         dy_all = lax.all_gather(cotangent, plane, axis=0, tiled=True)
 
-    match = (buckets[:, None] == jnp.arange(n_buckets, dtype=jnp.int32)[None, :]).astype(f32)
-    dist = lax.dot_general(
-        rel_table, match, (((0,), (1,)), ((), ())), precision=highest, preferred_element_type=f32
-    )
-    span = -(-dist.shape[1] // LANES) * LANES
-    dist = jnp.pad(dist, ((0, 0), (0, span - dist.shape[1]))).reshape(pairs, 2, span)
-    router_wide = jnp.pad(router, ((0, 0), (0, LANES - n_experts)))
-    gain_one = gain_attn[None, :]
-    gain_two = gain_ffn[None, :]
+    span = -(-buckets.shape[0] // LANES) * LANES
+    pack = pack_small(router, gain_attn, gain_ffn, buckets, rel_table, routes, span)
 
     q, k, v, o, lse, x_mid, message, probs, h_all, *gathered = attention_forward(
         place,
         x_all,
-        gain_one,
-        gain_two,
         weights,
-        dist,
-        routes,
-        router_wide,
+        pack,
         n_rows,
         n_experts,
         head_dim,
         Background(n_fsdp) if near else None,
-        (cotangent, in_pair) if near else (),
+        (cotangent, w_in, expert_out) if near else (),
     )
-    if near:
-        dy_all = gathered[0]
-        w_in = gathered[1].reshape(width, n_fsdp * part_out)
     behind = ()
     if near:
-        back, out_half, dw_in, dw_out = plane_experts(
+        dy_all, w_in, w_out = gathered
+        w_in = w_in.reshape(width, n_fsdp * part_out)
+        message_all, act, slope, dw_out, w_out = experts_up(
             message, dy_all, w_in, w_out, n_experts, n_fsdp
         )
-        behind = (out_half, dw_out.reshape(n_fsdp, part_out, width), x_mid)
+        back, out_half, dw_in, sum_out = experts_down(
+            message_all,
+            dy_all,
+            act,
+            slope,
+            w_in,
+            w_out.reshape(n_fsdp * part_out, width),
+            dw_out.reshape(n_fsdp, part_out, width),
+            n_experts,
+            n_fsdp,
+        )
+        behind = (out_half, dw_in.reshape(n_fsdp, n_seq * part_in, n_fsdp * part_out))
     else:
         message_all = lax.all_gather(message, plane, axis=0, tiled=True)
         out_part, back_part, dw_in, dw_out = experts(
@@ -1778,9 +1986,7 @@
         x_mid,
         message,
         probs,
-        routes,
-        router_wide,
-        gain_two,
+        pack,
         h_all,
         weights,
         q,
@@ -1788,7 +1994,6 @@
         v,
         o,
         lse,
-        dist,
         n_experts,
         head_dim,
         BackgroundBack(n_fsdp) if near else None,
@@ -1796,60 +2001,67 @@
     )
     dwq, dwk, dwv, dwo, dh_own, dh_other, dx_mid, dgain_two, drouter, ddist = grads[:10]
     if near:
-        out_rows, sum_out = grads[10:]
-        match_wide = jnp.pad(match.T, ((0, LANES - n_buckets), (0, span - match.shape[0])))
+        out_rows, sum_in = grads[10:]
         attn_sum, grad_in, grad_out, grad_tokens, small = finish(
             (dwq, dwk, dwv, dwo),
+            sum_in.reshape(n_seq, part_in, n_fsdp * part_out),
             sum_out,
-            dw_in.reshape(n_fsdp, n_seq * part_in, n_fsdp * part_out),
             dh_other,
             dh_own,
             dx_mid,
             tokens,
-            gain_one,
+            pack,
             dgain_two,
             drouter,
-            ddist.reshape(n_heads, span),
-            match_wide,
+            ddist,
             n_fsdp,
             n_experts,
-            part_in,
+            n_heads,
             hidden,
         )
-        grad_one, grad_two = small[0], small[1]
-        grad_router = small[2 : 2 + n_experts].T
-        grad_table = small[8 : 8 + n_heads, :n_buckets].T
-    else:
-        sum_out = lax.psum_scatter(dw_out, "fsdp", scatter_dimension=0, tiled=True)
-        sum_in = lax.psum_scatter(dw_in, "fsdp", scatter_dimension=0, tiled=True)
-        sum_in = sum_in.reshape(n_seq, part_in, n_fsdp * part_out)
-        sum_in = lax.all_to_all(sum_in, "seq", split_axis=0, concat_axis=0, tiled=True)
-        sum_in = sum_in.reshape(n_seq, part_in, n_fsdp, part_out).transpose(1, 2, 0, 3)
-        sum_in = sum_in.reshape(part_in, hidden)
-        grad_out = lax.all_gather(sum_out, "rep", axis=0, tiled=False)
-        grad_in = lax.all_gather(sum_in, "rep", axis=0, tiled=False)
-        swap = [(0, 1), (1, 0)]
-        dh_one = dh_own + lax.ppermute(dh_other, "seq", swap).astype(f32)
-        dx, dgain_one = norm_back(tokens.astype(f32), gain_one, dh_one)
-        grad_tokens = (dx_mid + dx).astype(bf16)
-        attn_grads = jnp.stack([dwq, dwk, dwv, dwo])
-        attn_grads = attn_grads.reshape(n_rep, n_fsdp, n_seq, part_attn, width)
-        attn_grads = attn_grads.transpose(0, 2, 1, 3, 4)
-        attn_grads = attn_grads.reshape(n_rep * n_seq * n_fsdp * part_attn, width)
-        attn_sum = lax.psum_scatter(attn_grads, plane, scatter_dimension=0, tiled=True)
-        attn_sum = lax.psum_scatter(attn_sum, "fsdp", scatter_dimension=0, tiled=True)
-        attn_sum = lax.all_gather(attn_sum, "rep", axis=0, tiled=False)
-        ddist = ddist.reshape(n_heads, span)[:, : buckets.shape[0]]
-        table = lax.dot_general(
-            match,
-            ddist,
-            (((0,), (1,)), ((), ())),
-            precision=highest,
-            preferred_element_type=f32,
+        *wide, grad_one, grad_two, grad_table, grad_router = widen(
+            attn_sum, grad_in, grad_out, small, n_heads, n_buckets
         )
-        grad_one, grad_two, grad_table, grad_router = lax.psum(
-            (dgain_one[0], dgain_two[0], table, drouter[:n_experts].T), ("rep", "fsdp", "seq")
+        return (
+            out_rows,
+            grad_tokens,
+            *wide,
+            grad_one[0],
+            grad_two[0],
+            grad_table.T,
+            grad_router.T,
         )
+    sum_out = lax.psum_scatter(dw_out, "fsdp", scatter_dimension=0, tiled=True)
+    sum_in = lax.psum_scatter(dw_in, "fsdp", scatter_dimension=0, tiled=True)
+    sum_in = sum_in.reshape(n_seq, part_in, n_fsdp * part_out)
+    sum_in = lax.all_to_all(sum_in, "seq", split_axis=0, concat_axis=0, tiled=True)
+    sum_in = sum_in.reshape(n_seq, part_in, n_fsdp, part_out).transpose(1, 2, 0, 3)
+    sum_in = sum_in.reshape(part_in, hidden)
+    grad_out = lax.all_gather(sum_out, "rep", axis=0, tiled=False)
+    grad_in = lax.all_gather(sum_in, "rep", axis=0, tiled=False)
+    swap = [(0, 1), (1, 0)]
+    dh_one = dh_own + lax.ppermute(dh_other, "seq", swap).astype(f32)
+    dx, dgain_one = norm_back(tokens.astype(f32), gain_attn[None, :], dh_one)
+    grad_tokens = (dx_mid + dx).astype(bf16)
+    attn_grads = jnp.stack([dwq, dwk, dwv, dwo])
+    attn_grads = attn_grads.reshape(n_rep, n_fsdp, n_seq, part_attn, width)
+    attn_grads = attn_grads.transpose(0, 2, 1, 3, 4)
+    attn_grads = attn_grads.reshape(n_rep * n_seq * n_fsdp * part_attn, width)
+    attn_sum = lax.psum_scatter(attn_grads, plane, scatter_dimension=0, tiled=True)
+    attn_sum = lax.psum_scatter(attn_sum, "fsdp", scatter_dimension=0, tiled=True)
+    attn_sum = lax.all_gather(attn_sum, "rep", axis=0, tiled=False)
+    ddist = ddist[:n_heads, : buckets.shape[0]]
+    match = (buckets[:, None] == jnp.arange(n_buckets)[None, :]).astype(f32)
+    table = lax.dot_general(
+        match,
+        ddist,
+        (((0,), (1,)), ((), ())),
+        precision=highest,
+        preferred_element_type=f32,
+    )
+    grad_one, grad_two, grad_table, grad_router = lax.psum(
+        (dgain_one[0], dgain_two[0], table, drouter[:n_experts].T), ("rep", "fsdp", "seq")
+    )
     attn_sum = attn_sum.astype(f32)
     return (
         out_rows,

time: 366 us -> 345 us (0.943)
  Pallas kernels: 344 us -> 333 us
  local copies, waits for them, and re-layouts: 12 us -> 6.4 us
  other arithmetic: 8.23 us -> 3.96 us
    pallas_call x1, Pallas kernels: 90.1 us -> 67.1 us  [finish(): pl.pallas_call(functools.partial(finish_kernel, n_fsdp, n_experts, n_head...]
    pallas_call x2 -> x4, Pallas kernels: 148 us -> 165 us  [the longest x1 66.9 us: experts_down(): pl.pallas_call(functools.partial(experts_down_kernel, n_experts, 512, n_f...]
    convert_element_type x3 -> x2, other arithmetic: 7.25 us -> 1.39 us  [rows(): array = array.astype(f32)]
where the time goes in v3:
time: 345 us
  Pallas kernels  333 us (97%)
  local copies, waits for them, and re-layouts  6.4 us (2%)
  other arithmetic  3.96 us (1%)
    pallas_call x1, Pallas kernels, finish(): pl.pallas_call(functools.partial(finish_kernel, n_fsdp, n_experts, n_head...  67.1 us
    pallas_call x1, Pallas kernels, experts_down(): pl.pallas_call(functools.partial(experts_down_kernel, n_experts, 512, n_f...  66.9 us
    pallas_call x1, Pallas kernels, attention_backward(): pl.pallas_call(functools.partial(backward_kernel, background, n_experts,...  56.2 us
    pallas_call x1, Pallas kernels, gather(): pl.pallas_call(functools.partial(gather_kernel, n_fsdp, part_out), out_sh...  45.9 us
    pallas_call x1, Pallas kernels, experts_up(): pl.pallas_call(functools.partial(experts_up_kernel, n_experts, hidden, n_...  45.3 us
    pallas_call x1, Pallas kernels, attention_forward(): pl.pallas_call(functools.partial(forward_kernel, background, n_experts, h...  45 us
    pallas_call x1, Pallas kernels, widen(): pl.pallas_call(functools.partial(widen_kernel, n_experts, n_heads, n_buck...  7.08 us

profile of v3, /device:TPU:0, one launch (start us, length us, event | category | flops | bytes accessed | tf_op | source)
XLA Modules:
  0.0 344.6 jit_solution(3282903191294861341)
XLA Ops:
  0.6 0.7 convert_bitcast_fusion
  1.3 0.7 broadcast_in_dim.7
  2.0 0.7 broadcast_in_dim.8
  2.7 0.7 convert_element_type.23
  3.5 0.7 pad.23
  4.2 0.7 pad.27
  4.9 1.9 concatenate.3.pack_ref
  6.8 45.9 %gather_weights.1 = (bf16[4,4,2,96,768]{4,3,2,1,0:T(8,128)(2,1)}, bf16[2,384,768]{2,1,0:T(8,128)(2,1)}, bf16[4,192,1536]{2,1,0:T(8,128)(2,1)}) custom-call(bf16[96,768]{1,0:T(8,128)(2,1)} %attn_q.1, bf16[96,768]{1,0:T(8,128)(2,1)} %attn_k.1, bf16[96,768]{1,0:T(8,128)(2,1)} %attn_v.1, bf16[96,768]{1,0:T(8,128)(2,1)} %attn_o.1, bf16[384,768]{1,0:T(8,128)(2,1)} %tokens_ref.1, ...), custom_call_target="tpu_custom_call" | custom-call | tf_op jit(solution)/shard_map/gather_weights/pallas_call | solution.py:318
  52.8 45.0 %attention_forward.1 = (bf16[384,768]{1,0:T(8,128)(2,1)}, bf16[768,768]{1,0:T(8,128)(2,1)}, bf16[768,768]{1,0:T(8,128)(2,1)}, bf16[384,768]{1,0:T(8,128)(2,1)}, ...) custom-call(s32[2]{0:T(128)} %bitcast.38, ...), custom_call_target="tpu_custom_call", output_to_operand_aliasing={{10}: (8, {})} | custom-call | flops 20000000000 | bytes 20000000 | tf_op jit(solution)/shard_map/attention_forward/pallas_call | solution.py:577
  97.8 45.3 %experts_up.1 = (bf16[8,384,896]{2,1,0:T(8,128)(2,1)}, bf16[8,384,1536]{2,1,0:T(8,128)(2,1)}, bf16[8,384,1536]{2,1,0:T(8,128)(2,1)}, bf16[1536,768]{1,0:T(8,128)(2,1)}, bf16[4,384,768]{2,1,0:T(8,128)(2,1)}) custom-call(bf16[384,896]{1,0:T(8,128)(2,1)} %get-tuple-element.66.message_ref, ...), custom_call_target="tpu_custom_call", output_to_operand_aliasing={{4}: (3, {})} | custom-call | flops 20000000000 | bytes 30000000 | tf_op jit(solution)/shard_map/experts_up/pallas_call | solution.py:858
  143.1 66.9 %experts_down.1 = (f32[384,896]{1,0:T(8,128)}, bf16[8,192,768]{2,1,0:T(8,128)(2,1)}, bf16[768,1536]{1,0:T(8,128)(2,1)}, bf16[384,768]{1,0:T(8,128)(2,1)}) custom-call(bf16[8,384,896]{2,1,0:T(8,128)(2,1)} %get-tuple-element.70.message_ref, bf16[8,384,768]{2,1,0:T(8,128)(2,1)} %get-tuple-element.67.dy_ref, bf16[8,384,1536]{2,1,0:T(8,128)(2,1)} %get-tuple-element.71.act_ref, ...), custom_call_target="tpu_custom_call" | custom-call | flops 40000000000 | bytes 40000000 | tf_op jit(solution)/shard_map/experts_down/pallas_call | solution.py:1095
  210.0 56.2 %attention_backward.1 = (bf16[768,768]{1,0:T(8,128)(2,1)}, bf16[768,768]{1,0:T(8,128)(2,1)}, bf16[768,768]{1,0:T(8,128)(2,1)}, bf16[768,768]{1,0:T(8,128)(2,1)},...) custom-call(s32[2]{0:T(128)} %bitcast.39, ...), custom_call_target="tpu_custom_call" | custom-call | flops 40000000000 | bytes 30000000 | tf_op jit(solution)/shard_map/attention_backward/pallas_call | solution.py:1488
  266.2 67.1 %finish_gradients.1 = (bf16[4,96,768]{2,1,0:T(8,128)(2,1)}, bf16[4,96,3072]{2,1,0:T(8,128)(2,1)}, bf16[4,384,768]{2,1,0:T(8,128)(2,1)}, bf16[384,768]{1,0:T(8,128)(2,1)}, f32[8,768]{1,0:T(8,128)}) custom-call(bf16[4,2,96,768]{3,2,1,0:T(8,128)(2,1)} %bitcast.18, bf16[4,2,96,768]{3,2,1,0:T(8,128)(2,1)} %bitcast.19, bf16[4,2,96,768]{3,2,1,0:T(8,128)(2,1)} %bitcast.20, ...), custom_call_target="tpu_custom_call" | custom-call | tf_op jit(solution)/shard_map/finish_gradients/pallas_call | solution.py:1794
  333.2 0.0 copy-start
  333.2 0.0 copy-start.1
  333.3 7.1 %widen.1 = (f32[96,768]{1,0:T(8,128)}, f32[96,768]{1,0:T(8,128)}, f32[96,768]{1,0:T(8,128)}, f32[96,768]{1,0:T(8,128)}, f32[4,96,3072]{2,1,0:T(8,128)}, /*index=...) custom-call(bf16[4,96,768]{2,1,0:T(8,128)(2,1)} %get-tuple-element.100.attn, ...), custom_call_target="tpu_custom_call" | custom-call | tf_op jit(solution)/shard_map/widen/pallas_call | solution.py:1872
  340.3 1.3 reduce
  341.6 1.3 reduce.1
  342.9 0.0 copy-done
  342.9 0.8 copy.33
  343.7 0.0 copy-done.1
  343.7 0.8 copy.34
  (5 shorter events, 0.0 us)
Async XLA Ops:
  333.2 9.7 %copy-start = (bf16[384,768]{1,0:T(8,128)(2,1)S(1)}, bf16[384,768]{1,0:T(8,128)(2,1)}, u32[]{:S(2)}) copy-start(bf16[384,768]{1,0:T(8,128)(2,1)} %get-tuple-element.126) | copy-start | bytes 1769476
  333.2 10.5 %copy-start.1 = (bf16[384,768]{1,0:T(8,128)(2,1)S(1)}, bf16[384,768]{1,0:T(8,128)(2,1)}, u32[]{:S(2)}) copy-start(bf16[384,768]{1,0:T(8,128)(2,1)} %get-tuple-element.127) | copy-start | bytes 1769476

commit v4 on v3

--- a/solution.py
+++ b/solution.py
@@ -201,9 +201,16 @@
     attn_o,
     tokens,
     expert_in,
+    router,
+    gain_attn,
+    gain_ffn,
+    buckets,
+    rel_table,
+    routes,
     weights,
     x_all,
     w_in,
+    pack,
     attn_held,
     tokens_held,
     in_held,
@@ -275,16 +282,23 @@
     own_in = pltpu.make_async_copy(in_held, w_in.at[line, rows(seq)], local.at[n_fsdp + 3])
     own_in.start()
     x_own.turn()
+    pack[...] = jnp.zeros_like(pack)
+    pack[0 : router.shape[0], : router.shape[1]] = router[...]
+    pack[4, : gain_attn.shape[0]] = gain_attn[...]
+    pack[5, : gain_ffn.shape[0]] = gain_ffn[...]
+    pack[6, : buckets.shape[0]] = buckets[...].astype(f32)
+    pack[8 : 8 + rel_table.shape[0], : rel_table.shape[1]] = rel_table[...]
+    pack[24:26, : routes.shape[1]] = routes[...].astype(f32)
     for shift in shifts[1:]:
         z_copies[shift].wait_recv()
         spread_out(shift)
     for copy in in_x:
         copy.wait_recv()
     own_in.wait()
-    in_copies = [
-        start(wires.copy(("line", shift), w_in.at[line], w_in.at[line], me.along(shift)))
-        for shift in (1, -1)
-    ]
+    in_copies = []
+    for i, shift in enumerate((1, -1)):
+        half = w_in.at[line, pl.ds(i * part_in, part_in)]
+        in_copies.append(start(wires.copy(("line", shift), half, half, me.along(shift))))
     token_copy = start(wires.copy("tokens", tokens, x_all.at[seq], beside))
     for shift in shifts:
         z = at[shift]
@@ -310,20 +324,22 @@
         copy.wait_send()
 
 
-def gather(attn, tokens, expert_in, part_out, n_fsdp):
+def gather(attn, tokens, expert_in, part_out, n_fsdp, small, span):
     part_attn, width = attn[0].shape
     n_rows = tokens.shape[0]
     n_experts, part_in, hidden = expert_in.shape
     anywhere = pl.BlockSpec(memory_space=pl.ANY)
-    weights, x_all, w_in = pl.pallas_call(
+    inside = pl.BlockSpec(memory_space=pltpu.VMEM)
+    weights, x_all, w_in, pack = pl.pallas_call(
         functools.partial(gather_kernel, n_fsdp, part_out),
         out_shape=[
             jax.ShapeDtypeStruct((4, n_fsdp, 2, part_attn, width), bf16),
             jax.ShapeDtypeStruct((2, n_rows, width), bf16),
             jax.ShapeDtypeStruct((n_fsdp, 2 * part_in, n_fsdp * part_out), bf16),
+            jax.ShapeDtypeStruct((32, span), f32),
         ],
-        in_specs=[anywhere] * 6,
-        out_specs=[anywhere] * 3,
+        in_specs=[anywhere] * 6 + [inside] * 6,
+        out_specs=[anywhere] * 3 + [inside],
         scratch_shapes=[
             pltpu.VMEM((part_attn, width), bf16),
             pltpu.VMEM((n_rows, width), bf16),
@@ -334,11 +350,12 @@
         ],
         compiler_params=pltpu.CompilerParams(collective_id=0, has_side_effects=True),
         name="gather_weights",
-    )(*attn, tokens, expert_in)
+    )(*attn, tokens, expert_in, *small)
     return (
         weights.reshape(4, n_fsdp * 2 * part_attn, width),
         x_all.reshape(2 * n_rows, width),
         w_in,
+        pack,
     )
 
 
@@ -358,41 +375,43 @@
         self.store().wait()
 
 
-def relay_plan(me, pieces):
+def line_plan(me, own, pieces):
     rows = pieces.shape[1] // 2
     plan = {}
     for i, shift in enumerate((1, -1)):
-        piece = pieces.at[(me.line - shift) % me.n_fsdp, pl.ds(i * rows, rows)]
+        first, rest = pl.ds(i * rows, rows), pl.ds((1 - i) * rows, rows)
+        target = pieces.at[me.line]
+        piece = pieces.at[(me.line - shift) % me.n_fsdp, first]
+        plan["first", shift] = (own.at[first], target.at[first], me.along(shift))
+        plan["rest", shift] = (own.at[rest], target.at[rest], me.along(shift))
         plan["relay", shift] = (piece, piece, me.along(shift))
     return plan
 
 
 class Background:
-    n_in, n_out = 3, 3
+    n_in, n_out = 2, 2
 
     def __init__(self, n_fsdp):
         self.n_fsdp = n_fsdp
 
-    def out_shape(self, dy, w_in, expert_out):
+    def out_shape(self, dy, w_in):
         return [
             jax.ShapeDtypeStruct((8,) + dy.shape, bf16),
             jax.ShapeDtypeStruct(w_in.shape, bf16),
-            jax.ShapeDtypeStruct((self.n_fsdp,) + expert_out.shape[1:], bf16),
         ]
 
-    def scratch(self, dy, w_in, expert_out):
+    def scratch(self, dy, w_in):
         return [
             pltpu.SemaphoreType.DMA((16,)),
             pltpu.SemaphoreType.DMA((16,)),
-            pltpu.SemaphoreType.DMA((4,)),
+            pltpu.SemaphoreType.DMA((2,)),
             pltpu.VMEM(dy.shape, bf16),
-            pltpu.VMEM(expert_out.shape[1:], bf16),
         ]
 
     def run(self, step, before, ins, outs, scratch):
-        dy, _, expert_out = ins
-        dy_all, w_in, w_out = outs
-        send, recv, local, dy_held, out_held = scratch
+        dy, _ = ins
+        dy_all, w_in = outs
+        send, recv, local, dy_held = scratch
         me = Place(self.n_fsdp)
         half = dy.shape[0] // 2
         first, second = pl.ds(0, half), pl.ds(half, half)
@@ -409,26 +428,26 @@
             "c3": (slot[5 + core], slot[5 + core], mate),
             "xy": (slot[1 + core, first], slot[5 + core, first], across),
             "yx": (slot[3 + core, second], slot[5 + core, second], beside),
-            ("z", 1): (expert_out.at[me.rep], w_out.at[me.line], me.along(1)),
-            ("z", -1): (expert_out.at[me.rep], w_out.at[me.line], me.along(-1)),
-        } | relay_plan(me, w_in)
+        }
+        line = line_plan(me, w_in.at[me.line], w_in)
+        plan |= {name: line[name] for name in line if name[0] != "first"}
         copies = Planned(plan, send, recv)
         own_dy = Bounce(dy, dy_held, slot[own], local.at[pl.ds(0, 2)])
-        own_out = Bounce(expert_out.at[me.rep], out_held, w_out.at[me.line], local.at[pl.ds(2, 2)])
         if before:
 
             @pl.when(step == 0)
             def _():
                 meet([mate, across, beside, me.along(1), me.along(-1)])
-                for name in (("relay", 1), ("relay", -1), ("z", 1), ("z", -1), "x", "y", "c0"):
+                for name in line:
+                    if name[0] != "first":
+                        copies[name].start()
+                for name in ("x", "y", "c0"):
                     copies[name].start()
                 own_dy.start()
-                own_out.start()
 
             @pl.when(step == 3)
             def _():
                 own_dy.turn()
-                own_out.turn()
                 copies["x"].wait_recv()
                 copies["xy"].start()
                 copies["c1"].start()
@@ -447,7 +466,6 @@
                 if name not in ("x", "y", "xy", "yx"):
                     copies[name].wait_recv()
             own_dy.wait()
-            own_out.wait()
             for name in plan:
                 copies[name].wait_send()
 
@@ -744,6 +762,11 @@
     return (j + 1) // 2 % 4, (j + 1) % 2
 
 
+def down_order(step):
+    inner = (step % 7 + 6) // 7
+    return step + inner * ((step + 3) % 6 + 1 - step)
+
+
 def experts_up_kernel(
     n_experts,
     chunk,
@@ -751,7 +774,7 @@
     message_ref,
     dy_ref,
     w_in_ref,
-    _,
+    expert_out,
     h_out,
     act_out,
     slope_out,
@@ -759,8 +782,10 @@
     w_out,
     h_ref,
     dw_out_acc,
+    out_held,
     send,
     recv,
+    local,
 ):
     step = pl.program_id(0)
     last = pl.num_programs(0) - 1
@@ -782,19 +807,30 @@
         "c3": (slot[5 + core], slot[5 + core], mate),
         "xy": (slot[1 + core, first], slot[5 + core, first], across),
         "yx": (slot[3 + core, second], slot[5 + core, second], beside),
-    } | relay_plan(me, w_out)
+    } | line_plan(me, expert_out.at[me.rep], w_out)
     copies = Planned(plan, send, recv)
+    own_out = Bounce(expert_out.at[me.rep], out_held, w_out.at[me.line], local)
 
     @pl.when(step == 0)
     def _():
         meet([mate, across, beside, me.along(1), me.along(-1)])
-        for name in ("c0", "x", "y", ("relay", 1), ("relay", -1)):
+        for name in ("c0", "x", "y", ("first", 1), ("first", -1)):
             copies[name].start()
+        own_out.start()
         h_ref[own] = message_ref[...]
         dw_out_acc[...] = jnp.zeros_like(dw_out_acc)
 
+    @pl.when(step == 1)
+    def _():
+        own_out.turn()
+        for shift in (1, -1):
+            copies["rest", shift].start()
+
     @pl.when(step == 2)
     def _():
+        for shift in (1, -1):
+            copies["first", shift].wait_recv()
+            copies["relay", shift].start()
         copies["x"].wait_recv()
         copies["c1"].start()
         copies["xy"].start()
@@ -840,13 +876,15 @@
     @pl.when(step == last)
     def _():
         dw_out_ref[...] = dw_out_acc[...].astype(bf16)
+        own_out.wait()
         for shift in (1, -1):
+            copies["rest", shift].wait_recv()
             copies["relay", shift].wait_recv()
         for name in plan:
             copies[name].wait_send()
 
 
-def experts_up(message, dy_all, w_in, w_out, n_experts, n_fsdp):
+def experts_up(message, dy_all, w_in, expert_out, n_experts, n_fsdp):
     blocks, rows, width = dy_all.shape
     long = message.shape[1]
     hidden = w_in.shape[1]
@@ -862,7 +900,7 @@
             jax.ShapeDtypeStruct((blocks, rows, hidden), bf16),
             jax.ShapeDtypeStruct((blocks, rows, hidden), bf16),
             jax.ShapeDtypeStruct((hidden, width), bf16),
-            jax.ShapeDtypeStruct(w_out.shape, bf16),
+            jax.ShapeDtypeStruct((n_fsdp,) + expert_out.shape[1:], bf16),
         ],
         grid=(blocks,),
         in_specs=[whole((rows, long)), turn(width), whole((width, hidden)), anywhere],
@@ -870,10 +908,11 @@
         scratch_shapes=[
             pltpu.VMEM((blocks, rows, long), bf16),
             pltpu.VMEM((hidden, width), f32),
-            dma(12),
-            dma(12),
+            pltpu.VMEM(expert_out.shape[1:], bf16),
+            dma(16),
+            dma(16),
+            dma(2),
         ],
-        input_output_aliases={3: 4},
         compiler_params=pltpu.CompilerParams(
             vmem_limit_bytes=VMEM_LIMIT, collective_id=2, has_side_effects=True
         ),
@@ -881,7 +920,7 @@
             flops=20_000_000_000, transcendentals=0, bytes_accessed=30_000_000
         ),
         name="experts_up",
-    )(message, dy_all, w_in, w_out)
+    )(message, dy_all, w_in, expert_out)
 
 
 def experts_down_kernel(
@@ -941,7 +980,7 @@
         )
 
     def to_owner(j):
-        q, k = plane_slot(j)
+        q, k = plane_slot(down_order(j))
         return pltpu.make_async_remote_copy(
             src_ref=fin_ref.at[j % 2],
             dst_ref=land_ref.at[q, core],
@@ -952,10 +991,10 @@
         )
 
     def keep_out(j):
-        return pltpu.make_async_copy(fin_out_ref.at[j % 2], out_half.at[j], local.at[j])
+        return pltpu.make_async_copy(fin_out_ref.at[j % 2], out_half.at[down_order(j)], local.at[j])
 
     def stays(j):
-        q, k = plane_slot(j)
+        q, k = plane_slot(down_order(j))
         return (q == 0) & (k == core)
 
     def finish_block(j):
@@ -1023,7 +1062,7 @@
             part[:, :width] += dh_part
         dgate = dgate_part if dgate is None else dgate + dgate_part
         dw_in_acc[:, piece] += dot(h_turned, dup)
-        if start == 0:
+        if start == chunk:
 
             @pl.when(step >= 1)
             def _():
@@ -1088,7 +1127,9 @@
     half = rows // 2
     once = pl.Buffered(1)
     whole = lambda shape: pl.BlockSpec(shape, lambda i: (0,) * len(shape), pipeline_mode=once)
-    block = lambda columns: pl.BlockSpec((None, rows, columns), lambda i: (i, 0, 0))
+    block = lambda columns: pl.BlockSpec(
+        (None, rows, columns), lambda i: (down_order(i), 0, 0)
+    )
     anywhere = pl.BlockSpec(memory_space=pl.ANY)
     both = long + width
     dma = lambda *shape: pltpu.SemaphoreType.DMA(shape)
@@ -1202,7 +1243,7 @@
 
 
 class BackgroundBack:
-    n_in, n_out = 2, 2
+    n_in, n_out = 2, 3
 
     def __init__(self, n_fsdp):
         self.n_fsdp = n_fsdp
@@ -1212,6 +1253,7 @@
         return [
             jax.ShapeDtypeStruct((2 * half, width), bf16),
             jax.ShapeDtypeStruct(dw_in.shape[1:], bf16),
+            jax.ShapeDtypeStruct((self.n_fsdp, width // (2 * self.n_fsdp), width), bf16),
         ]
 
     def out_specs(self, shapes):
@@ -1220,17 +1262,85 @@
 
     def scratch(self, out_half, dw_in):
         half, width = out_half.shape[1:]
+        pairs = width // LANES
         return [
             pltpu.VMEM((4, 2, half, width), bf16),
             pltpu.SemaphoreType.DMA((8,)),
             pltpu.SemaphoreType.DMA((4, 2)),
+            pltpu.VMEM((2, 4) + self.split(width), bf16),
+            pltpu.VMEM((pairs, 2) + self.split(width), bf16),
+            pltpu.VMEM((pairs, 2) + self.split(width), bf16),
+            pltpu.VMEM((pairs, 3, self.n_fsdp) + self.split(width)[2:], bf16),
+            pltpu.SemaphoreType.DMA((pairs, 2)),
+            pltpu.SemaphoreType.DMA((pairs, 2)),
+            pltpu.SemaphoreType.DMA((pairs, 3)),
+            pltpu.SemaphoreType.DMA((pairs, 3)),
         ] + LineSum.scratch(*dw_in.shape[1:])
+
+    def split(self, width):
+        return (self.n_fsdp, 2, width // (2 * self.n_fsdp), LANES)
+
+    def to_mate(self, pair, i, scratch):
+        me = Place(self.n_fsdp)
+        own, given = scratch[3:5]
+        send, recv = scratch[7:9]
+        return pltpu.make_async_remote_copy(
+            src_ref=own.at[pair % 2, 2 * i + 1 - me.core],
+            dst_ref=given.at[pair, i],
+            send_sem=send.at[pair, i],
+            recv_sem=recv.at[pair, i],
+            device_id=me.mate(),
+            device_id_type=MESH,
+        )
+
+    def to_chip(self, pair, i, scratch):
+        me = Place(self.n_fsdp)
+        added, landed = scratch[5:7]
+        send, recv = scratch[9:11]
+        rows, columns = ((0, 1), (1, 0), (1, 1))[i]
+        row, column = (me.row + rows) % 2, (me.seq + columns) % 2
+        return pltpu.make_async_remote_copy(
+            src_ref=added.at[pair, row, :, column],
+            dst_ref=landed.at[pair, i],
+            send_sem=send.at[pair, i],
+            recv_sem=recv.at[pair, i],
+            device_id=me.chip(rows, columns),
+            device_id_type=MESH,
+        )
+
+    def give(self, pair, grads, scratch):
+        own = scratch[3]
+
+        @pl.when(pair >= 2)
+        def _():
+            for i in (0, 1):
+                self.to_mate(pair - 2, i, scratch).wait_send()
+
+        for i, grad in enumerate(grads):
+            own[pair % 2, i] = grad.reshape(own.shape[2:])
+        for i in (0, 1):
+            self.to_mate(pair, i, scratch).start()
+
+    def collect(self, pair, scratch):
+        core = Place(self.n_fsdp).core
+        own, given, added = scratch[3:6]
+        for i in (0, 1):
+            self.to_mate(pair, i, scratch).wait_recv()
+            total = own[pair % 2, 2 * i + core].astype(f32) + given[pair, i].astype(f32)
+            added[pair, i] = total.astype(bf16)
+        for i in range(3):
+            self.to_chip(pair, i, scratch).start()
+
+    def collect_before(self, pair, scratch):
+        @pl.when(pair >= 1)
+        def _():
+            self.collect(pair - 1, scratch)
 
     def run(self, step, before, ins, outs, scratch, x_mid):
         out_half, dw_in = ins
-        out_rows, sum_in = outs
+        out_rows, sum_in, plane_sum = outs
         land, send, recv = scratch[:3]
-        near, mid, far, mine, line_send, line_recv, line_local = scratch[3:]
+        near, mid, far, mine, line_send, line_recv, line_local = scratch[11:]
         me = Place(self.n_fsdp)
         core = me.core
         half = out_half.shape[1]
@@ -1282,6 +1392,10 @@
 
         @pl.when(step == pl.num_programs(0) - 1)
         def _():
+            added, landed = scratch[5:7]
+            pairs = landed.shape[0]
+            self.collect(pairs - 1, scratch)
+            sum_in[...] = line.total()
             for j in range(8):
                 if j in (0, 7):
 
@@ -1317,7 +1431,18 @@
                         arrived.wait_recv()
                     total = total + land[q, side].astype(f32)
                 out_rows[here, :] = total.astype(bf16)
-            sum_in[...] = line.total()
+            for pair in (pairs - 2, pairs - 1):
+                for i in (0, 1):
+                    self.to_mate(pair, i, scratch).wait_send()
+            for pair in range(pairs):
+                total = added[pair, me.row, :, me.seq].astype(f32)
+                for i in range(3):
+                    self.to_chip(pair, i, scratch).wait_recv()
+                    total = total + landed[pair, i].astype(f32)
+                plane_sum[:, :, pair * LANES : (pair + 1) * LANES] = total.astype(bf16)
+            for pair in range(pairs):
+                for i in range(3):
+                    self.to_chip(pair, i, scratch).wait_send()
 
 
 def backward_kernel(
@@ -1346,9 +1471,10 @@
     step = pl.program_id(0)
     n_in, n_out = (background.n_in, background.n_out) if background else (0, 0)
     behind_in, refs = refs[:n_in], refs[n_in:]
-    dwq_out, dwk_out, dwv_out, dwo_out, dh_own_out, dh_other_out = refs[:6]
-    dx_mid_out, gain_out, router_out, ddist_out = refs[6:10]
-    behind_out, refs = refs[10 : 10 + n_out], refs[10 + n_out :]
+    n_grads = 0 if background else 4
+    grad_outs, refs = refs[:n_grads], refs[n_grads:]
+    dh_own_out, dh_other_out, dx_mid_out, gain_out, router_out, ddist_out = refs[:6]
+    behind_out, refs = refs[6 : 6 + n_out], refs[6 + n_out :]
     da_ref, dh_all_ref, dh_mine_ref, mask_ref, bias_ref, dbias_ref, dq_ref, dist_ref = refs[:8]
     if background:
         background.run(step, True, behind_in, behind_out, refs[8:], x_mid_ref)
@@ -1393,7 +1519,6 @@
 
     da = da_ref[...]
     do = dot_t(da, wo_ref[...]).astype(bf16)
-    dwo_out[...] = t_dot(o_ref[...], da).astype(bf16)
     block = LANES
     span = pack_ref.shape[1]
     first_half = lax.broadcasted_iota(jnp.int32, (block, LANES), 1) < head_dim
@@ -1436,9 +1561,16 @@
     dk = dk.astype(bf16)
     dv = dv.astype(bf16)
     h_all = h_ref[...]
-    dwq_out[...] = t_dot(h_ref[own, :], dq).astype(bf16)
-    dwk_out[...] = t_dot(h_all, dk).astype(bf16)
-    dwv_out[...] = t_dot(h_all, dv).astype(bf16)
+    da_columns = da_ref[:, pl.ds(pl.multiple_of(step * LANES, LANES), LANES)]
+    if background:
+        background.collect_before(step, refs[8:])
+    factors = ((h_ref[own, :], dq), (h_all, dk), (h_all, dv), (o_ref[...], da_columns))
+    grads = [t_dot(left, right).astype(bf16) for left, right in factors]
+    if background:
+        background.give(step, grads, refs[8:])
+    else:
+        for target, grad in zip(grad_outs, grads):
+            target[...] = grad
     dh_all_ref[...] += dot_t(dk, wk_ref[...]) + dot_t(dv, wv_ref[...])
     dh_mine_ref[...] += dot_t(dq, wq_ref[...])
 
@@ -1477,6 +1609,7 @@
     pairs = width // LANES
     span = pack.shape[1]
     more_shapes, more_scratch, params = [], [], {}
+    n_grads = 0 if background else 4
     if background:
         more_shapes = background.out_shape(*behind)
         more_scratch = background.scratch(*behind)
@@ -1487,11 +1620,8 @@
     matrix = lambda i: pl.BlockSpec((None, width, LANES), lambda p, *_: (i, 0, p))
     return pl.pallas_call(
         functools.partial(backward_kernel, background, n_experts, head_dim),
-        out_shape=[
-            jax.ShapeDtypeStruct((width, width), bf16),
-            jax.ShapeDtypeStruct((width, width), bf16),
-            jax.ShapeDtypeStruct((width, width), bf16),
-            jax.ShapeDtypeStruct((width, width), bf16),
+        out_shape=[jax.ShapeDtypeStruct((width, width), bf16)] * n_grads
+        + [
             jax.ShapeDtypeStruct((n_rows, width), f32),
             jax.ShapeDtypeStruct((n_rows, width), bf16),
             jax.ShapeDtypeStruct((n_rows, width), f32),
@@ -1518,15 +1648,12 @@
                 columns(n_rows),
                 columns(length),
                 columns(length),
-                columns(n_rows),
+                whole((n_rows, width)),
                 columns(n_rows),
             ]
             + [anywhere] * len(behind),
-            out_specs=[
-                columns(width),
-                columns(width),
-                columns(width),
-                pl.BlockSpec((LANES, width), lambda p, *_: (p, 0)),
+            out_specs=[columns(width)] * n_grads
+            + [
                 whole((n_rows, width)),
                 whole((n_rows, width)),
                 whole((n_rows, width)),
@@ -1578,13 +1705,10 @@
     n_fsdp,
     n_experts,
     n_heads,
-    dwq,
-    dwk,
-    dwv,
-    dwo,
     sum_in,
     sum_out,
     dh_other,
+    line_ref,
     dh_own_ref,
     dx_mid_ref,
     tokens_ref,
@@ -1597,10 +1721,6 @@
     grad_out,
     tokens_out,
     small_out,
-    mine_ref,
-    rx_ref,
-    land_ref,
-    line_ref,
     line_land,
     dh_land,
     small_plane,
@@ -1624,15 +1744,10 @@
     peers += [me.chip(1, 0, 1 - core), me.chip(0, 1, 1 - core), me.chip(1, 1, 1 - core)]
     shifts = (1, -1, 2)
     plan = {
-        "pair0": (None, rx_ref.at[0], mate),
-        "pair1": (None, rx_ref.at[1], mate),
         "dh": (dh_other, dh_land, beside),
         "out_c": (sum_out, grad_out.at[rep], mate),
         "out_y": (sum_out, grad_out.at[rep], across),
         "out_f": (grad_out.at[far_rep], grad_out.at[far_rep], mate),
-        "to_y": (mine_ref.at[far_row, :, seq], land_ref.at[1], across),
-        "to_xy": (mine_ref.at[far_row, :, 1 - seq], land_ref.at[2], corner),
-        "to_x": (mine_ref.at[row, :, 1 - seq], land_ref.at[0], beside),
         "attn_c": (line_land.at[3], attn_out.at[rep], mate),
         "attn_y": (line_land.at[3], attn_out.at[rep], across),
         "attn_f": (attn_out.at[far_rep], attn_out.at[far_rep], mate),
@@ -1653,42 +1768,18 @@
     for i, peer in enumerate(peers):
         plan["small", i] = (small_plane.at[here], small_plane.at[here], peer)
     copies = Planned(plan, send, recv)
-    matrices = (dwq, dwk, dwv, dwo)
-
-    def pair(side, i):
-        plan[f"pair{i}"] = (matrices[2 * i + 1 - side], rx_ref.at[i], mate)
-        return copies[f"pair{i}"]
-
-    keep = lambda side, i: pltpu.make_async_copy(
-        matrices[2 * i + side], mine_ref.at[i], local.at[i]
-    )
-
     meet(peers + [me.along(shift) for shift in shifts])
-    for side in (0, 1):
-
-        @pl.when(core == side)
-        def _():
-            for i in (0, 1):
-                pair(side, i).start()
-                keep(side, i).start()
-
+    for i in range(3):
+        copies["line", i].start()
     for z in range(n_fsdp):
         copies["in_x", z].start()
     copies["out_y"].start()
+    copies["dh"].start()
+    copies["out_c"].start()
     own_in = pltpu.make_async_copy(sum_in.at[seq], in_held, local.at[2])
     own_in.start()
     own_out = Bounce(sum_out, out_held, grad_out.at[rep], local.at[pl.ds(8, 2)])
     own_out.start()
-    for i in (0, 1):
-        keep(0, i).wait()
-        pair(0, i).wait_recv()
-    for i, names in ((far_row, ("to_y", "to_xy")), (row, ("to_x",))):
-        total = mine_ref[i].astype(f32) + rx_ref[i].astype(f32)
-        mine_ref[i] = total.astype(bf16)
-        for name in names:
-            copies[name].start()
-    copies["out_c"].start()
-    own_out.turn()
     own_in.wait()
     kept = []
     for z in range(n_fsdp):
@@ -1696,6 +1787,7 @@
         target = grad_in.at[rep, :, columns(z, seq)]
         kept.append(pltpu.make_async_copy(source, target, local.at[4 + z]))
         kept[-1].start()
+    own_out.turn()
     table = exact_dot_t(ddist_ref[...], bucket_match(pack_ref))
     small = small_plane.at[here]
     small[...] = jnp.zeros_like(small_out)
@@ -1708,29 +1800,8 @@
         copy.wait()
     for z in range(n_fsdp):
         copies["in_x", z].wait_recv()
+    copies["in_y"].start()
     copies["in_c"].start()
-    copies["out_y"].wait_recv()
-    copies["out_f"].start()
-    copies["to_x"].wait_recv()
-    copies["dh"].start()
-    copies["to_y"].wait_recv()
-    copies["in_y"].start()
-    copies["to_xy"].wait_recv()
-    for z in range(n_fsdp):
-        total = mine_ref[row, z, seq].astype(f32)
-        for i in range(3):
-            total = total + land_ref[i, z].astype(f32)
-        line_ref[z] = total.astype(bf16)
-    for i in range(3):
-        copies["line", i].start()
-    copies["dh"].wait_recv()
-    dh_one = dh_own_ref[...] + dh_land[...].astype(f32)
-    gain_one = pack_ref[4:5, :width]
-    dx, dgain_one = norm_back(tokens_ref[...].astype(f32), gain_one, dh_one)
-    small[0:1, :] = dgain_one
-    for i in range(len(peers)):
-        copies["small", i].start()
-    tokens_out[...] = (dx_mid_ref[...] + dx).astype(bf16)
     total = line_ref[line].astype(f32)
     for i in range(3):
         copies["line", i].wait_recv()
@@ -1740,6 +1811,18 @@
     copies["attn_c"].start()
     own_attn = pltpu.make_async_copy(line_land.at[3], attn_out.at[rep], local.at[3])
     own_attn.start()
+    copies["out_y"].wait_recv()
+    copies["out_f"].start()
+    copies["dh"].wait_recv()
+    dh_one = dh_own_ref[...] + dh_land[...].astype(f32)
+    gain_one = pack_ref[4:5, :width]
+    dx, dgain_one = norm_back(tokens_ref[...].astype(f32), gain_one, dh_one)
+    small[0:1, :] = dgain_one
+    for i in range(len(peers)):
+        copies["small", i].start()
+    tokens_out[...] = (dx_mid_ref[...] + dx).astype(bf16)
+    copies["attn_y"].wait_recv()
+    copies["attn_f"].start()
     for i in range(len(peers)):
         copies["small", i].wait_recv()
     total = small_plane[0]
@@ -1750,8 +1833,6 @@
         copies["small_z", i].start()
     copies["in_y"].wait_recv()
     copies["in_f"].start()
-    copies["attn_y"].wait_recv()
-    copies["attn_f"].start()
     for i in range(3):
         copies["small_z", i].wait_recv()
     total = small_line[0]
@@ -1767,7 +1848,7 @@
 
 
 def finish(
-    attn_grads,
+    plane_sum,
     sum_in,
     sum_out,
     dh_other,
@@ -1784,13 +1865,11 @@
     hidden,
 ):
     n_rows, width = tokens.shape
-    part_attn = width // (2 * n_fsdp)
+    part_attn = plane_sum.shape[1]
     part_in = sum_in.shape[1]
     anywhere = pl.BlockSpec(memory_space=pl.ANY)
     inside = pl.BlockSpec(memory_space=pltpu.VMEM)
     dma = lambda n: pltpu.SemaphoreType.DMA((n,))
-    split = (n_fsdp, 2, part_attn, width)
-    attn_grads = [g.reshape(split) for g in attn_grads]
     return pl.pallas_call(
         functools.partial(finish_kernel, n_fsdp, n_experts, n_heads),
         out_shape=[
@@ -1800,13 +1879,9 @@
             jax.ShapeDtypeStruct((n_rows, width), bf16),
             jax.ShapeDtypeStruct((8, width), f32),
         ],
-        in_specs=[anywhere] * 7 + [inside] * 7,
+        in_specs=[anywhere] * 3 + [inside] * 8,
         out_specs=[anywhere] * 3 + [inside] * 2,
         scratch_shapes=[
-            pltpu.VMEM((2,) + split, bf16),
-            pltpu.VMEM((2,) + split, bf16),
-            pltpu.VMEM((3, n_fsdp, part_attn, width), bf16),
-            pltpu.VMEM((n_fsdp, part_attn, width), bf16),
             pltpu.VMEM((4, part_attn, width), bf16),
             pltpu.VMEM((n_rows, width), bf16),
             pltpu.VMEM((8, 8, width), f32),
@@ -1822,10 +1897,10 @@
         ),
         name="finish_gradients",
     )(
-        *attn_grads,
         sum_in,
         sum_out,
         dh_other,
+        plane_sum,
         dh_own,
         dx_mid,
         tokens,
@@ -1852,8 +1927,8 @@
 
     @pl.when(step == 0)
     def _():
-        gain_one[...] = small[0:1, :]
-        gain_two[...] = small[1:2, :]
+        gain_one[...] = small[0, :]
+        gain_two[...] = small[1, :]
         router[...] = small[2 : 2 + n_experts, :]
         for head in range(n_heads):
             at = head % 6 * LANES
@@ -1867,7 +1942,7 @@
     width = small.shape[1]
     own = lambda a: pl.BlockSpec((None,) + a.shape[1:], lambda i: (i, 0, 0))
     whole = lambda shape: pl.BlockSpec(shape, lambda i: (0,) * len(shape))
-    small_shapes = [(1, width), (1, width), (n_heads, n_buckets), (n_experts, width)]
+    small_shapes = [(width,), (width,), (n_heads, n_buckets), (n_experts, width)]
     wide = [attn.shape[1:]] * 4
     return pl.pallas_call(
         functools.partial(widen_kernel, n_experts, n_heads, n_buckets),
@@ -1918,9 +1993,16 @@
     place = piece_starts[0]
     near = n_fsdp == 4 and part_attn % 16 == 0
     pick = lambda array: lax.dynamic_index_in_dim(array, rep, 0, keepdims=False)
+    span = -(-buckets.shape[0] // LANES) * LANES
     if near:
-        weights, x_all, w_in = gather(
-            (attn_q, attn_k, attn_v, attn_o), tokens, expert_in, part_out, n_fsdp
+        weights, x_all, w_in, pack = gather(
+            (attn_q, attn_k, attn_v, attn_o),
+            tokens,
+            expert_in,
+            part_out,
+            n_fsdp,
+            (router.T, gain_attn, gain_ffn, buckets, rel_table.T, routes.T),
+            span,
         )
     else:
         attn_own = pick(jnp.stack([attn_q, attn_k, attn_v, attn_o]))
@@ -1936,9 +2018,7 @@
         w_in = lax.all_gather(in_pair, "fsdp", axis=0, tiled=True)
         w_out = lax.all_gather(pick(expert_out), "fsdp", axis=0, tiled=True)
         dy_all = lax.all_gather(cotangent, plane, axis=0, tiled=True)
-
-    span = -(-buckets.shape[0] // LANES) * LANES
-    pack = pack_small(router, gain_attn, gain_ffn, buckets, rel_table, routes, span)
+        pack = pack_small(router, gain_attn, gain_ffn, buckets, rel_table, routes, span)
 
     q, k, v, o, lse, x_mid, message, probs, h_all, *gathered = attention_forward(
         place,
@@ -1949,14 +2029,14 @@
         n_experts,
         head_dim,
         Background(n_fsdp) if near else None,
-        (cotangent, w_in, expert_out) if near else (),
+        (cotangent, w_in) if near else (),
     )
     behind = ()
     if near:
-        dy_all, w_in, w_out = gathered
+        dy_all, w_in = gathered
         w_in = w_in.reshape(width, n_fsdp * part_out)
         message_all, act, slope, dw_out, w_out = experts_up(
-            message, dy_all, w_in, w_out, n_experts, n_fsdp
+            message, dy_all, w_in, expert_out, n_experts, n_fsdp
         )
         back, out_half, dw_in, sum_out = experts_down(
             message_all,
@@ -1999,11 +2079,10 @@
         BackgroundBack(n_fsdp) if near else None,
         behind,
     )
-    dwq, dwk, dwv, dwo, dh_own, dh_other, dx_mid, dgain_two, drouter, ddist = grads[:10]
     if near:
-        out_rows, sum_in = grads[10:]
+        dh_own, dh_other, dx_mid, dgain_two, drouter, ddist, out_rows, sum_in, plane_sum = grads
         attn_sum, grad_in, grad_out, grad_tokens, small = finish(
-            (dwq, dwk, dwv, dwo),
+            plane_sum,
             sum_in.reshape(n_seq, part_in, n_fsdp * part_out),
             sum_out,
             dh_other,
@@ -2026,11 +2105,12 @@
             out_rows,
             grad_tokens,
             *wide,
-            grad_one[0],
-            grad_two[0],
+            grad_one,
+            grad_two,
             grad_table.T,
             grad_router.T,
         )
+    dwq, dwk, dwv, dwo, dh_own, dh_other, dx_mid, dgain_two, drouter, ddist = grads
     sum_out = lax.psum_scatter(dw_out, "fsdp", scatter_dimension=0, tiled=True)
     sum_in = lax.psum_scatter(dw_in, "fsdp", scatter_dimension=0, tiled=True)
     sum_in = sum_in.reshape(n_seq, part_in, n_fsdp * part_out)

time: 345 us -> 300 us (0.87)
  Pallas kernels: 333 us -> 298 us
  local copies, waits for them, and re-layouts: 6.4 us -> 1.64 us
  other arithmetic: 3.96 us -> 0 us
    pallas_call x1, Pallas kernels: 67.1 us -> 41.7 us  [finish(): pl.pallas_call(functools.partial(finish_kernel, n_fsdp, n_experts, n_head...]
    pallas_call x1, Pallas kernels: 45 us -> 36.4 us  [attention_forward(): pl.pallas_call(functools.partial(forward_kernel, background, n_experts, h...]
    pallas_call x1, Pallas kernels: 56.2 us -> 64.6 us  [attention_backward(): pl.pallas_call(functools.partial(backward_kernel, background, n_experts,...]
    pallas_call x1, Pallas kernels: 66.9 us -> 59.7 us  [experts_down(): pl.pallas_call(functools.partial(experts_down_kernel, n_experts, 512, n_f...]
    pallas_call x1, Pallas kernels: 45.9 us -> 42 us  [gather(): pl.pallas_call(functools.partial(gather_kernel, n_fsdp, part_out), out_sh...]
where the time goes in v4:
time: 300 us
  Pallas kernels  298 us (99%)
    pallas_call x1, Pallas kernels, attention_backward(): pl.pallas_call(functools.partial(backward_kernel, background, n_experts,...  64.6 us
    pallas_call x1, Pallas kernels, experts_down(): pl.pallas_call(functools.partial(experts_down_kernel, n_experts, 512, n_f...  59.7 us
    pallas_call x1, Pallas kernels, experts_up(): pl.pallas_call(functools.partial(experts_up_kernel, n_experts, hidden, n_...  46.1 us
    pallas_call x1, Pallas kernels, gather(): pl.pallas_call(functools.partial(gather_kernel, n_fsdp, part_out), out_sh...  42 us
    pallas_call x1, Pallas kernels, finish(): pl.pallas_call(functools.partial(finish_kernel, n_fsdp, n_experts, n_head...  41.7 us
    pallas_call x1, Pallas kernels, attention_forward(): pl.pallas_call(functools.partial(forward_kernel, background, n_experts, h...  36.4 us
    pallas_call x1, Pallas kernels, widen(): pl.pallas_call(functools.partial(widen_kernel, n_experts, n_heads, n_buck...  7.08 us

profile of v4, /device:TPU:0, one launch (start us, length us, event | category | flops | bytes accessed | tf_op | source)
XLA Modules:
  0.0 299.9 jit_solution(15601550196883043321)
XLA Ops:
  0.6 42.0 %gather_weights.1 = (bf16[4,4,2,96,768]{4,3,2,1,0:T(8,128)(2,1)}, bf16[2,384,768]{2,1,0:T(8,128)(2,1)}, bf16[4,192,1536]{2,1,0:T(8,128)(2,1)}, f32[32,1536]{1,0:T(8,128)}) custom-call(bf16[96,768]{1,0:T(8,128)(2,1)} %attn_q.1, bf16[96,768]{1,0:T(8,128)(2,1)} %attn_k.1, bf16[96,768]{1,0:T(8,128)(2,1)} %attn_v.1, bf16[96,768]{1,0:T(8,128)(2,1)} %attn_o.1, ...), custom_call_target="tpu_custom_call" | custom-call | tf_op jit(solution)/shard_map/gather_weights/pallas_call | solution.py:333
  42.7 36.4 %attention_forward.1 = (bf16[384,768]{1,0:T(8,128)(2,1)}, bf16[768,768]{1,0:T(8,128)(2,1)}, bf16[768,768]{1,0:T(8,128)(2,1)}, bf16[384,768]{1,0:T(8,128)(2,1)}, ...) custom-call(s32[2]{0:T(128)} %bitcast.30, ...), custom_call_target="tpu_custom_call", output_to_operand_aliasing={{10}: (8, {})} | custom-call | flops 20000000000 | bytes 20000000 | tf_op jit(solution)/shard_map/attention_forward/pallas_call | solution.py:595
  79.1 46.1 %experts_up.1 = (bf16[8,384,896]{2,1,0:T(8,128)(2,1)}, bf16[8,384,1536]{2,1,0:T(8,128)(2,1)}, bf16[8,384,1536]{2,1,0:T(8,128)(2,1)}, bf16[1536,768]{1,0:T(8,128)(2,1)}, bf16[4,384,768]{2,1,0:T(8,128)(2,1)}) custom-call(bf16[384,896]{1,0:T(8,128)(2,1)} %get-tuple-element.64.message_ref, bf16[8,384,768]{2,1,0:T(8,128)(2,1)} %get-tuple-element.65.dy_ref, ...), custom_call_target="tpu_custom_call" | custom-call | flops 20000000000 | bytes 30000000 | tf_op jit(solution)/shard_map/experts_up/pallas_call | solution.py:896
  125.2 59.7 %experts_down.1 = (f32[384,896]{1,0:T(8,128)}, bf16[8,192,768]{2,1,0:T(8,128)(2,1)}, bf16[768,1536]{1,0:T(8,128)(2,1)}, bf16[384,768]{1,0:T(8,128)(2,1)}) custom-call(bf16[8,384,896]{2,1,0:T(8,128)(2,1)} %get-tuple-element.67.message_ref, bf16[8,384,768]{2,1,0:T(8,128)(2,1)} %get-tuple-element.65.dy_ref, bf16[8,384,1536]{2,1,0:T(8,128)(2,1)} %get-tuple-element.68.act_ref, ...), custom_call_target="tpu_custom_call" | custom-call | flops 40000000000 | bytes 40000000 | tf_op jit(solution)/shard_map/experts_down/pallas_call | solution.py:1136
  184.9 64.6 %attention_backward.1 = (f32[384,768]{1,0:T(8,128)}, bf16[384,768]{1,0:T(8,128)(2,1)}, f32[384,768]{1,0:T(8,128)}, f32[1,768]{1,0:T(1,128)}, f32[128,768]{1,0:T(...) custom-call(s32[2]{0:T(128)} %bitcast.31, ...), custom_call_target="tpu_custom_call" | custom-call | flops 40000000000 | bytes 30000000 | tf_op jit(solution)/shard_map/attention_backward/pallas_call | solution.py:1621
  249.5 41.7 %finish_gradients.1 = (bf16[4,96,768]{2,1,0:T(8,128)(2,1)}, bf16[4,96,3072]{2,1,0:T(8,128)(2,1)}, bf16[4,384,768]{2,1,0:T(8,128)(2,1)}, bf16[384,768]{1,0:T(8,128)(2,1)}, f32[8,768]{1,0:T(8,128)}) custom-call(bf16[2,96,1536]{2,1,0:T(8,128)(2,1)} %bitcast.13, bf16[384,768]{1,0:T(8,128)(2,1)} %get-tuple-element.85.sum_out, ...), custom_call_target="tpu_custom_call" | custom-call | tf_op jit(solution)/shard_map/finish_gradients/pallas_call | solution.py:1873
  291.2 0.0 copy-start
  291.2 0.0 copy-start.1
  291.2 7.1 %widen.1 = (f32[96,768]{1,0:T(8,128)}, f32[96,768]{1,0:T(8,128)}, f32[96,768]{1,0:T(8,128)}, f32[96,768]{1,0:T(8,128)}, f32[4,96,3072]{2,1,0:T(8,128)}, /*index=...) custom-call(bf16[4,96,768]{2,1,0:T(8,128)(2,1)} %get-tuple-element.94.attn, ...), custom_call_target="tpu_custom_call" | custom-call | tf_op jit(solution)/shard_map/widen/pallas_call | solution.py:1947
  298.3 0.0 copy-done
  298.3 0.8 copy.31
  299.1 0.0 copy-done.1
  299.1 0.8 copy.32
Async XLA Ops:
  291.2 7.1 %copy-start = (bf16[384,768]{1,0:T(8,128)(2,1)S(1)}, bf16[384,768]{1,0:T(8,128)(2,1)}, u32[]{:S(2)}) copy-start(bf16[384,768]{1,0:T(8,128)(2,1)} %get-tuple-element.120) | copy-start | bytes 1769476
  291.2 7.9 %copy-start.1 = (bf16[384,768]{1,0:T(8,128)(2,1)S(1)}, bf16[384,768]{1,0:T(8,128)(2,1)}, u32[]{:S(2)}) copy-start(bf16[384,768]{1,0:T(8,128)(2,1)} %get-tuple-element.121) | copy-start | bytes 1769476

commit v5 on v4

--- a/solution.py
+++ b/solution.py
@@ -75,6 +75,18 @@
     return pltpu.roll(
         jnp.broadcast_to(row, (block, width)), width - (block - 1), 1, stride=1, stride_axis=0
     )
+
+
+def by_head(values, first_half):
+    zero = jnp.zeros((), values.dtype)
+    return jnp.concatenate(
+        [jnp.where(first_half, values, zero), jnp.where(first_half, zero, values)]
+    )
+
+
+def of_head(stacked, first_half):
+    block = stacked.shape[0] // 2
+    return jnp.where(first_half, stacked[:block], stacked[block:])
 
 
 def gather_diagonals(sums):
@@ -486,7 +498,7 @@
     step = pl.program_id(0)
     n_in, n_out = (background.n_in, background.n_out) if background else (0, 0)
     behind_in, refs = refs[:n_in], refs[n_in:]
-    q_out, k_out, v_out, o_out, lse_out, x_mid_out, message_out, probs_out, h_out = refs[:9]
+    q_out, k_out, v_out, o_out, p_out, x_mid_out, message_out, probs_out, h_out = refs[:9]
     behind_out, refs = refs[9 : 9 + n_out], refs[9 + n_out :]
     total_ref, mask_ref, bias_ref, dist_ref = refs[:4]
     if background:
@@ -506,8 +518,8 @@
 
     h_all = h_out[...]
     q_low = dot(h_out[own, :], wq_ref[...]).astype(bf16) * (head_dim**-0.5)
-    k_low = dot(h_all, wk_ref[...]).astype(bf16)
-    v_low = dot(h_all, wv_ref[...]).astype(bf16)
+    kv_low = dot(h_all, jnp.concatenate([wk_ref[...], wv_ref[...]], 1)).astype(bf16)
+    k_low, v_low = kv_low[:, :LANES], kv_low[:, LANES:]
     q_out[...] = q_low
     k_out[...] = k_low
     v_out[...] = v_low
@@ -519,21 +531,15 @@
     for b in range(rows // block):
         here = slice(b * block, (b + 1) * block)
         offset = pl.multiple_of(length - LANES - block * b - first_row(rows), LANES)
-        halves = []
-        tops = []
-        for head in range(2):
-            mine = first_half if head == 0 else ~first_half
-            q_head = jnp.where(mine, q_low[here], jnp.zeros((), bf16))
-            scores = dot_t(q_head, k_low)
-            scores = scores + bias_ref[head, :, pl.ds(offset, length)] + mask_ref[here, :]
-            top = jnp.max(scores, -1, keepdims=True)
-            exp_scores = jnp.exp(scores - top)
-            total = jnp.sum(exp_scores, -1, keepdims=True)
-            probs = (exp_scores * (1.0 / total)).astype(bf16)
-            halves.append(dot(probs, v_low))
-            tops.append(top + jnp.log(total))
-        o_out[here, :] = jnp.where(first_half, halves[0], halves[1]).astype(bf16)
-        lse_out[here, :] = jnp.where(first_half, tops[0], tops[1])
+        scores = dot_t(by_head(q_low[here], first_half), k_low).reshape(2, block, length)
+        scores = scores + bias_ref[:, :, pl.ds(offset, length)] + mask_ref[here, :]
+        top = jnp.max(scores, -1, keepdims=True)
+        exp_scores = jnp.exp(scores - top)
+        total = jnp.sum(exp_scores, -1, keepdims=True)
+        probs = (exp_scores * (1.0 / total)).astype(bf16)
+        p_out[:, here, :] = probs
+        heads = dot(probs.reshape(2 * block, length), v_low)
+        o_out[here, :] = of_head(heads, first_half).astype(bf16)
     total_ref[...] += dot(o_out[...], wo_ref[...])
 
     @pl.when(step == pl.num_programs(0) - 1)
@@ -580,7 +586,7 @@
         jax.ShapeDtypeStruct((length, width), bf16),
         jax.ShapeDtypeStruct((length, width), bf16),
         jax.ShapeDtypeStruct((n_rows, width), bf16),
-        jax.ShapeDtypeStruct((n_rows, width), f32),
+        jax.ShapeDtypeStruct((pairs, 2, n_rows, length), bf16),
         jax.ShapeDtypeStruct((n_rows, width), f32),
         jax.ShapeDtypeStruct((n_rows, width + LANES), bf16),
         jax.ShapeDtypeStruct((n_rows, LANES), f32),
@@ -612,7 +618,7 @@
                 columns(length),
                 columns(length),
                 columns(n_rows),
-                columns(n_rows),
+                pl.BlockSpec((None, 2, n_rows, length), lambda p, *_: (p, 0, 0, 0)),
                 whole((n_rows, width)),
                 whole((n_rows, width + LANES)),
                 whole((n_rows, LANES)),
@@ -763,8 +769,8 @@
 
 
 def down_order(step):
-    inner = (step % 7 + 6) // 7
-    return step + inner * ((step + 3) % 6 + 1 - step)
+    inner = (13 - step) // 8
+    return inner * ((step + 4) % 6 + 1) + (1 - inner) * (step - 6) * 7
 
 
 def experts_up_kernel(
@@ -773,7 +779,7 @@
     n_fsdp,
     message_ref,
     dy_ref,
-    w_in_ref,
+    w_in,
     expert_out,
     h_out,
     act_out,
@@ -782,6 +788,9 @@
     w_out,
     h_ref,
     dw_out_acc,
+    w_in_ref,
+    gated_ref,
+    dy_pair_ref,
     out_held,
     send,
     recv,
@@ -809,16 +818,19 @@
         "yx": (slot[3 + core, second], slot[5 + core, second], beside),
     } | line_plan(me, expert_out.at[me.rep], w_out)
     copies = Planned(plan, send, recv)
-    own_out = Bounce(expert_out.at[me.rep], out_held, w_out.at[me.line], local)
+    own_out = Bounce(expert_out.at[me.rep], out_held, w_out.at[me.line], local.at[pl.ds(0, 2)])
 
     @pl.when(step == 0)
     def _():
+        load = pltpu.make_async_copy(w_in, w_in_ref, local.at[2])
+        load.start()
         meet([mate, across, beside, me.along(1), me.along(-1)])
         for name in ("c0", "x", "y", ("first", 1), ("first", -1)):
             copies[name].start()
         own_out.start()
         h_ref[own] = message_ref[...]
         dw_out_acc[...] = jnp.zeros_like(dw_out_acc)
+        load.wait()
 
     @pl.when(step == 1)
     def _():
@@ -858,7 +870,8 @@
     lane = lax.broadcasted_iota(jnp.int32, extra.shape, 1)
     mine = (lane == expert) | (lane == expert + n_experts)
     gate = jnp.sum(jnp.where(mine, extra, 0.0), -1, keepdims=True)
-    dy = dy_ref[...]
+    place = pl.ds(pl.multiple_of(step % 2 * rows, rows), rows)
+    dy_pair_ref[place, :] = dy_ref[...]
     for start in range(0, hidden, chunk):
         piece = slice(start, start + chunk)
         up = dot(h, w_in_ref[:, piece])
@@ -870,8 +883,11 @@
         slope = 0.5 * more + halved * (1.0 - tanh * tanh) * (GELU_A + 3.0 * GELU_B * square)
         act_out[:, piece] = act
         slope_out[:, piece] = slope.astype(bf16)
-        gated = (gate * act.astype(f32)).astype(bf16)
-        dw_out_acc[piece, :] += t_dot(gated, dy)
+        gated_ref[place, piece] = (gate * act.astype(f32)).astype(bf16)
+
+    @pl.when(step % 2 == 1)
+    def _():
+        dw_out_acc[...] += t_dot(gated_ref[...], dy_pair_ref[...])
 
     @pl.when(step == last)
     def _():
@@ -894,7 +910,7 @@
     anywhere = pl.BlockSpec(memory_space=pl.ANY)
     dma = lambda *shape: pltpu.SemaphoreType.DMA(shape)
     return pl.pallas_call(
-        functools.partial(experts_up_kernel, n_experts, hidden, n_fsdp),
+        functools.partial(experts_up_kernel, n_experts, hidden // 2, n_fsdp),
         out_shape=[
             jax.ShapeDtypeStruct((blocks, rows, long), bf16),
             jax.ShapeDtypeStruct((blocks, rows, hidden), bf16),
@@ -903,15 +919,18 @@
             jax.ShapeDtypeStruct((n_fsdp,) + expert_out.shape[1:], bf16),
         ],
         grid=(blocks,),
-        in_specs=[whole((rows, long)), turn(width), whole((width, hidden)), anywhere],
+        in_specs=[whole((rows, long)), turn(width), anywhere, anywhere],
         out_specs=[turn(long), turn(hidden), turn(hidden), whole((hidden, width)), anywhere],
         scratch_shapes=[
             pltpu.VMEM((blocks, rows, long), bf16),
             pltpu.VMEM((hidden, width), f32),
+            pltpu.VMEM((width, hidden), bf16),
+            pltpu.VMEM((2 * rows, hidden), bf16),
+            pltpu.VMEM((2 * rows, width), bf16),
             pltpu.VMEM(expert_out.shape[1:], bf16),
             dma(16),
             dma(16),
-            dma(2),
+            dma(3),
         ],
         compiler_params=pltpu.CompilerParams(
             vmem_limit_bytes=VMEM_LIMIT, collective_id=2, has_side_effects=True
@@ -931,8 +950,8 @@
     dy_ref,
     act_ref,
     slope_ref,
-    w_in_ref,
-    w_out_ref,
+    w_in,
+    w_out,
     dw_out,
     back_ref,
     out_half,
@@ -945,6 +964,10 @@
     fin_out_ref,
     land_ref,
     dw_in_acc,
+    w_in_ref,
+    w_out_ref,
+    h_pair_ref,
+    dup_ref,
     tx_send,
     tx_recv,
     fin_sem,
@@ -1024,6 +1047,12 @@
 
     @pl.when(step == 0)
     def _():
+        loads = [
+            pltpu.make_async_copy(w_in, w_in_ref, local.at[0]),
+            pltpu.make_async_copy(w_out, w_out_ref, local.at[1]),
+        ]
+        for load in loads:
+            load.start()
         partners = [mate, me.along(1), me.along(-1)]
         for q in (1, 2, 3):
             for k in (0, 1):
@@ -1031,13 +1060,16 @@
         meet(partners)
         adds.start()
         dw_in_acc[...] = jnp.zeros_like(dw_in_acc)
+        for load in loads:
+            load.wait()
 
     @pl.when(step == 3)
     def _():
         adds.turn()
 
     expert = me.rep
-    h_turned = message_ref[:, :width].T
+    place = pl.ds(pl.multiple_of(step % 2 * rows, rows), rows)
+    h_pair_ref[:, place] = message_ref[:, :width].T
     extra = message_ref[:, width:].astype(f32)
     lane = lax.broadcasted_iota(jnp.int32, extra.shape, 1)
     mine = (lane == expert) | (lane == expert + n_experts)
@@ -1061,12 +1093,16 @@
             part[:, long:] += out_part
             part[:, :width] += dh_part
         dgate = dgate_part if dgate is None else dgate + dgate_part
-        dw_in_acc[:, piece] += dot(h_turned, dup)
+        dup_ref[place, piece] = dup
         if start == chunk:
 
             @pl.when(step >= 1)
             def _():
                 finish_block(step - 1)
+
+    @pl.when(step % 2 == 1)
+    def _():
+        dw_in_acc[...] += dot(h_pair_ref[...], dup_ref[...])
 
     high = dgate.astype(bf16).astype(f32)
     low = dgate - high
@@ -1090,11 +1126,11 @@
         to_mate(last).wait_send()
         keep_out(last - 1).wait()
         keep_out(last).wait()
-        to_owner(last - 1).wait_send()
-
-        @pl.when(~stays(last))
-        def _():
-            to_owner(last).wait_send()
+        for j in (last - 1, last):
+
+            @pl.when(~stays(j))
+            def _():
+                to_owner(j).wait_send()
 
         for side in range(2):
             total = None
@@ -1134,7 +1170,7 @@
     both = long + width
     dma = lambda *shape: pltpu.SemaphoreType.DMA(shape)
     return pl.pallas_call(
-        functools.partial(experts_down_kernel, n_experts, 512, n_fsdp),
+        functools.partial(experts_down_kernel, n_experts, hidden // 2, n_fsdp),
         out_shape=[
             jax.ShapeDtypeStruct((rows, long), f32),
             jax.ShapeDtypeStruct((blocks, half, width), bf16),
@@ -1147,8 +1183,8 @@
             block(width),
             block(hidden),
             block(hidden),
-            whole((width, hidden)),
-            whole((hidden, width)),
+            anywhere,
+            anywhere,
             anywhere,
         ],
         out_specs=[
@@ -1165,6 +1201,10 @@
             pltpu.VMEM((2, half, width), bf16),
             pltpu.VMEM((4, 2, half, long), bf16),
             pltpu.VMEM((width, hidden), f32),
+            pltpu.VMEM((width, hidden), bf16),
+            pltpu.VMEM((hidden, width), bf16),
+            pltpu.VMEM((width, 2 * rows), bf16),
+            pltpu.VMEM((2 * rows, hidden), bf16),
             dma(8),
             dma(8),
             dma(8),
@@ -1243,7 +1283,7 @@
 
 
 class BackgroundBack:
-    n_in, n_out = 2, 3
+    n_in, n_out = 2, 4
 
     def __init__(self, n_fsdp):
         self.n_fsdp = n_fsdp
@@ -1253,7 +1293,10 @@
         return [
             jax.ShapeDtypeStruct((2 * half, width), bf16),
             jax.ShapeDtypeStruct(dw_in.shape[1:], bf16),
-            jax.ShapeDtypeStruct((self.n_fsdp, width // (2 * self.n_fsdp), width), bf16),
+            jax.ShapeDtypeStruct(
+                (self.n_fsdp, width // (2 * self.n_fsdp), width - LANES), bf16
+            ),
+            jax.ShapeDtypeStruct((4,) + self.split(width), bf16),
         ]
 
     def out_specs(self, shapes):
@@ -1262,7 +1305,7 @@
 
     def scratch(self, out_half, dw_in):
         half, width = out_half.shape[1:]
-        pairs = width // LANES
+        pairs = width // LANES - 1
         return [
             pltpu.VMEM((4, 2, half, width), bf16),
             pltpu.SemaphoreType.DMA((8,)),
@@ -1308,18 +1351,26 @@
             device_id_type=MESH,
         )
 
-    def give(self, pair, grads, scratch):
+    def give(self, pair, grads, scratch, last_out):
         own = scratch[3]
+        last = pl.num_programs(0) - 1
 
         @pl.when(pair >= 2)
         def _():
             for i in (0, 1):
                 self.to_mate(pair - 2, i, scratch).wait_send()
 
-        for i, grad in enumerate(grads):
-            own[pair % 2, i] = grad.reshape(own.shape[2:])
-        for i in (0, 1):
-            self.to_mate(pair, i, scratch).start()
+        @pl.when(pair < last)
+        def _():
+            for i, grad in enumerate(grads):
+                own[pair % 2, i] = grad.reshape(own.shape[2:])
+            for i in (0, 1):
+                self.to_mate(pair, i, scratch).start()
+
+        @pl.when(pair == last)
+        def _():
+            for i, grad in enumerate(grads):
+                last_out[i] = grad.reshape(own.shape[2:])
 
     def collect(self, pair, scratch):
         core = Place(self.n_fsdp).core
@@ -1338,7 +1389,7 @@
 
     def run(self, step, before, ins, outs, scratch, x_mid):
         out_half, dw_in = ins
-        out_rows, sum_in, plane_sum = outs
+        out_rows, sum_in, plane_sum, _ = outs
         land, send, recv = scratch[:3]
         near, mid, far, mine, line_send, line_recv, line_local = scratch[11:]
         me = Place(self.n_fsdp)
@@ -1394,7 +1445,6 @@
         def _():
             added, landed = scratch[5:7]
             pairs = landed.shape[0]
-            self.collect(pairs - 1, scratch)
             sum_in[...] = line.total()
             for j in range(8):
                 if j in (0, 7):
@@ -1431,9 +1481,8 @@
                         arrived.wait_recv()
                     total = total + land[q, side].astype(f32)
                 out_rows[here, :] = total.astype(bf16)
-            for pair in (pairs - 2, pairs - 1):
-                for i in (0, 1):
-                    self.to_mate(pair, i, scratch).wait_send()
+            for i in (0, 1):
+                self.to_mate(pairs - 1, i, scratch).wait_send()
             for pair in range(pairs):
                 total = added[pair, me.row, :, me.seq].astype(f32)
                 for i in range(3):
@@ -1449,7 +1498,6 @@
     background,
     n_experts,
     head_dim,
-    place_ref,
     back_ref,
     dy_ref,
     x_mid_ref,
@@ -1465,7 +1513,7 @@
     k_ref,
     v_ref,
     o_ref,
-    lse_ref,
+    p_ref,
     *refs,
 ):
     step = pl.program_id(0)
@@ -1475,9 +1523,9 @@
     grad_outs, refs = refs[:n_grads], refs[n_grads:]
     dh_own_out, dh_other_out, dx_mid_out, gain_out, router_out, ddist_out = refs[:6]
     behind_out, refs = refs[6 : 6 + n_out], refs[6 + n_out :]
-    da_ref, dh_all_ref, dh_mine_ref, mask_ref, bias_ref, dbias_ref, dq_ref, dist_ref = refs[:8]
+    da_ref, dh_all_ref, dh_mine_ref, dbias_ref, dq_ref, h_turned_ref, o_turned_ref = refs[:7]
     if background:
-        background.run(step, True, behind_in, behind_out, refs[8:], x_mid_ref)
+        background.run(step, True, behind_in, behind_out, refs[7:], x_mid_ref)
     rows, width = x_mid_ref.shape
     length = h_ref.shape[0]
     own = pl.ds(pl.multiple_of(first_row(rows), rows), rows)
@@ -1514,13 +1562,12 @@
         dh_all_ref[...] = jnp.zeros_like(dh_all_ref)
         dh_mine_ref[...] = jnp.zeros_like(dh_mine_ref)
         ddist_out[...] = jnp.zeros_like(ddist_out)
-        dist_ref[...] = distances(pack_ref)
-        make_mask(place_ref, mask_ref)
+        h_turned_ref[...] = h_ref[...].T
+        o_turned_ref[...] = o_ref[...].T
 
     da = da_ref[...]
     do = dot_t(da, wo_ref[...]).astype(bf16)
     block = LANES
-    span = pack_ref.shape[1]
     first_half = lax.broadcasted_iota(jnp.int32, (block, LANES), 1) < head_dim
     zero = jnp.zeros((), bf16)
     k_low = k_ref[...]
@@ -1528,50 +1575,47 @@
     dk = None
     dv = None
     for head in range(2):
-        bias_ref[head] = spread(dist_ref[pl.ds(2 * step + head, 1), :], block, span)
         dbias_ref[head] = jnp.zeros_like(dbias_ref[head])
     for b in range(rows // block):
         here = slice(b * block, (b + 1) * block)
         offset = pl.multiple_of(length - LANES - block * b - first_row(rows), LANES)
-        halves = []
-        for head in range(2):
-            mine = first_half if head == 0 else ~first_half
-            q_head = jnp.where(mine, q_ref[here, :], zero)
-            do_head = jnp.where(mine, do[here], zero)
-            scores = dot_t(q_head, k_low)
-            scores = scores + bias_ref[head, :, pl.ds(offset, length)] + mask_ref[here, :]
-            at = head * head_dim
-            probs = jnp.exp(scores - lse_ref[here, at : at + 1])
-            dprobs = dot_t(do_head, v_low)
-            weighted = probs * dprobs
-            ds = weighted - probs * jnp.sum(weighted, -1, keepdims=True)
-            ds_low = ds.astype(bf16)
-            dbias_ref[head, :, pl.ds(offset, length)] += ds
-            halves.append(dot(ds_low, k_low))
-            dk_part = t_dot(ds_low, q_head)
-            dv_part = t_dot(probs.astype(bf16), do_head)
-            dk = dk_part if dk is None else dk + dk_part
-            dv = dv_part if dv is None else dv + dv_part
-        dq_ref[here, :] = (
-            jnp.where(first_half, halves[0], halves[1]) * (head_dim**-0.5)
-        ).astype(bf16)
+        q_heads = by_head(q_ref[here, :], first_half)
+        do_heads = by_head(do[here], first_half)
+        probs_low = p_ref[:, here, :]
+        probs = probs_low.astype(f32)
+        dprobs = dot_t(do_heads, v_low).reshape(2, block, length)
+        weighted = probs * dprobs
+        ds = weighted - probs * jnp.sum(weighted, -1, keepdims=True)
+        dbias_ref[:, :, pl.ds(offset, length)] += ds
+        ds_low = ds.astype(bf16).reshape(2 * block, length)
+        probs_low = probs_low.reshape(2 * block, length)
+        dq_heads = dot(ds_low, k_low)
+        dk_part = t_dot(ds_low, q_heads)
+        dv_part = t_dot(probs_low, do_heads)
+        dk = dk_part if dk is None else dk + dk_part
+        dv = dv_part if dv is None else dv + dv_part
+        dq_ref[here, :] = (of_head(dq_heads, first_half) * (head_dim**-0.5)).astype(bf16)
     for head in range(2):
         ddist_out[pl.ds(2 * step + head, 1), :] = gather_diagonals(dbias_ref[head])
     dq = dq_ref[...]
-    dk = dk.astype(bf16)
-    dv = dv.astype(bf16)
-    h_all = h_ref[...]
+    dkv = jnp.concatenate([dk, dv], 1).astype(bf16)
     da_columns = da_ref[:, pl.ds(pl.multiple_of(step * LANES, LANES), LANES)]
     if background:
-        background.collect_before(step, refs[8:])
-    factors = ((h_ref[own, :], dq), (h_all, dk), (h_all, dv), (o_ref[...], da_columns))
-    grads = [t_dot(left, right).astype(bf16) for left, right in factors]
+        background.collect_before(step, refs[7:])
+    mine = pl.ds(pl.multiple_of(first_row(rows), rows), rows)
+    grads_kv = dot(h_turned_ref[...], dkv).astype(bf16)
+    grads = [
+        dot(h_turned_ref[:, mine], dq).astype(bf16),
+        grads_kv[:, :LANES],
+        grads_kv[:, LANES:],
+        dot(o_turned_ref[...], da_columns).astype(bf16),
+    ]
     if background:
-        background.give(step, grads, refs[8:])
+        background.give(step, grads, refs[7:], behind_out[3])
     else:
         for target, grad in zip(grad_outs, grads):
             target[...] = grad
-    dh_all_ref[...] += dot_t(dk, wk_ref[...]) + dot_t(dv, wv_ref[...])
+    dh_all_ref[...] += dot_t(dkv, jnp.concatenate([wk_ref[...], wv_ref[...]], 1))
     dh_mine_ref[...] += dot_t(dq, wq_ref[...])
 
     @pl.when(step == pl.num_programs(0) - 1)
@@ -1581,11 +1625,10 @@
         dh_other_out[...] = dh_all_ref[other, :].astype(bf16)
 
     if background:
-        background.run(step, False, behind_in, behind_out, refs[8:], x_mid_ref)
+        background.run(step, False, behind_in, behind_out, refs[7:], x_mid_ref)
 
 
 def attention_backward(
-    place,
     back,
     dy,
     x_mid,
@@ -1598,7 +1641,7 @@
     k,
     v,
     o,
-    lse,
+    p,
     n_experts,
     head_dim,
     background=None,
@@ -1631,7 +1674,7 @@
         ]
         + more_shapes,
         grid_spec=pltpu.PrefetchScalarGridSpec(
-            num_scalar_prefetch=1,
+            num_scalar_prefetch=0,
             grid=(pairs,),
             in_specs=[
                 whole((n_rows, width + LANES)),
@@ -1649,7 +1692,7 @@
                 columns(length),
                 columns(length),
                 whole((n_rows, width)),
-                columns(n_rows),
+                pl.BlockSpec((None, 2, n_rows, length), lambda p, *_: (p, 0, 0, 0)),
             ]
             + [anywhere] * len(behind),
             out_specs=[columns(width)] * n_grads
@@ -1666,11 +1709,10 @@
                 pltpu.VMEM((n_rows, width), bf16),
                 pltpu.VMEM((length, width), f32),
                 pltpu.VMEM((n_rows, width), f32),
-                pltpu.VMEM((n_rows, length), f32),
-                pltpu.VMEM((2, LANES, span), f32),
                 pltpu.VMEM((2, LANES, span), f32),
                 pltpu.VMEM((n_rows, LANES), bf16),
-                pltpu.VMEM((16, span), f32),
+                pltpu.VMEM((width, length), bf16),
+                pltpu.VMEM((width, n_rows), bf16),
             ]
             + more_scratch,
         ),
@@ -1680,7 +1722,6 @@
         ),
         name="attention_backward",
     )(
-        place,
         back,
         dy,
         x_mid,
@@ -1696,7 +1737,7 @@
         k,
         v,
         o,
-        lse,
+        p,
         *behind,
     )
 
@@ -1709,6 +1750,7 @@
     sum_out,
     dh_other,
     line_ref,
+    last_ref,
     dh_own_ref,
     dx_mid_ref,
     tokens_ref,
@@ -1722,6 +1764,12 @@
     tokens_out,
     small_out,
     line_land,
+    last_given,
+    last_added,
+    last_land,
+    last_line,
+    last_line_land,
+    attn_held,
     dh_land,
     small_plane,
     small_line,
@@ -1748,8 +1796,8 @@
         "out_c": (sum_out, grad_out.at[rep], mate),
         "out_y": (sum_out, grad_out.at[rep], across),
         "out_f": (grad_out.at[far_rep], grad_out.at[far_rep], mate),
-        "attn_c": (line_land.at[3], attn_out.at[rep], mate),
-        "attn_y": (line_land.at[3], attn_out.at[rep], across),
+        "attn_c": (attn_held, attn_out.at[rep], mate),
+        "attn_y": (attn_held, attn_out.at[rep], across),
         "attn_f": (attn_out.at[far_rep], attn_out.at[far_rep], mate),
         "in_c": (grad_in.at[rep], grad_in.at[rep], mate),
         "in_y": (grad_in.at[rep], grad_in.at[rep], across),
@@ -1758,6 +1806,7 @@
     for i, shift in enumerate(shifts):
         target = (line + shift) % n_fsdp
         plan["line", i] = (line_ref.at[target], line_land.at[i], me.along(shift))
+        plan["last_z", i] = (last_line.at[target], last_line_land.at[i], me.along(shift))
         plan["small_z", i] = (small_line.at[line], small_line.at[line], me.along(shift))
     for z in range(n_fsdp):
         plan["in_x", z] = (
@@ -1767,8 +1816,15 @@
         )
     for i, peer in enumerate(peers):
         plan["small", i] = (small_plane.at[here], small_plane.at[here], peer)
+    for i in (0, 1):
+        plan["last_c", i] = (last_ref.at[2 * i + 1 - core], last_given.at[i], mate)
+    chips = ((row, 1 - seq, beside), (far_row, seq, across), (far_row, 1 - seq, corner))
+    for i, (to_row, to_column, chip) in enumerate(chips):
+        plan["last", i] = (last_added.at[to_row, :, to_column], last_land.at[i], chip)
     copies = Planned(plan, send, recv)
     meet(peers + [me.along(shift) for shift in shifts])
+    for i in (0, 1):
+        copies["last_c", i].start()
     for i in range(3):
         copies["line", i].start()
     for z in range(n_fsdp):
@@ -1788,6 +1844,12 @@
         kept.append(pltpu.make_async_copy(source, target, local.at[4 + z]))
         kept[-1].start()
     own_out.turn()
+    for i in (0, 1):
+        copies["last_c", i].wait_recv()
+        total = last_ref[2 * i + core].astype(f32) + last_given[i].astype(f32)
+        last_added[i] = total.astype(bf16)
+    for i in range(3):
+        copies["last", i].start()
     table = exact_dot_t(ddist_ref[...], bucket_match(pack_ref))
     small = small_plane.at[here]
     small[...] = jnp.zeros_like(small_out)
@@ -1802,15 +1864,19 @@
         copies["in_x", z].wait_recv()
     copies["in_y"].start()
     copies["in_c"].start()
+    total = last_added[row, :, seq].astype(f32)
+    for i in range(3):
+        copies["last", i].wait_recv()
+        total = total + last_land[i].astype(f32)
+    last_line[...] = total.astype(bf16)
+    for i in range(3):
+        copies["last_z", i].start()
     total = line_ref[line].astype(f32)
     for i in range(3):
         copies["line", i].wait_recv()
         total = total + line_land[i].astype(f32)
-    line_land[3] = total.astype(bf16)
-    copies["attn_y"].start()
-    copies["attn_c"].start()
-    own_attn = pltpu.make_async_copy(line_land.at[3], attn_out.at[rep], local.at[3])
-    own_attn.start()
+    early = total.shape[1]
+    attn_held[:, :early] = total.astype(bf16)
     copies["out_y"].wait_recv()
     copies["out_f"].start()
     copies["dh"].wait_recv()
@@ -1820,6 +1886,15 @@
     small[0:1, :] = dgain_one
     for i in range(len(peers)):
         copies["small", i].start()
+    total = last_line[line].astype(f32)
+    for i in range(3):
+        copies["last_z", i].wait_recv()
+        total = total + last_line_land[i].astype(f32)
+    attn_held[:, early:] = total.astype(bf16)
+    copies["attn_y"].start()
+    copies["attn_c"].start()
+    own_attn = pltpu.make_async_copy(attn_held, attn_out.at[rep], local.at[3])
+    own_attn.start()
     tokens_out[...] = (dx_mid_ref[...] + dx).astype(bf16)
     copies["attn_y"].wait_recv()
     copies["attn_f"].start()
@@ -1849,6 +1924,7 @@
 
 def finish(
     plane_sum,
+    last_grads,
     sum_in,
     sum_out,
     dh_other,
@@ -1866,6 +1942,7 @@
 ):
     n_rows, width = tokens.shape
     part_attn = plane_sum.shape[1]
+    split = last_grads.shape[1:]
     part_in = sum_in.shape[1]
     anywhere = pl.BlockSpec(memory_space=pl.ANY)
     inside = pl.BlockSpec(memory_space=pltpu.VMEM)
@@ -1879,10 +1956,16 @@
             jax.ShapeDtypeStruct((n_rows, width), bf16),
             jax.ShapeDtypeStruct((8, width), f32),
         ],
-        in_specs=[anywhere] * 3 + [inside] * 8,
+        in_specs=[anywhere] * 3 + [inside] * 9,
         out_specs=[anywhere] * 3 + [inside] * 2,
         scratch_shapes=[
-            pltpu.VMEM((4, part_attn, width), bf16),
+            pltpu.VMEM((3,) + plane_sum.shape[1:], bf16),
+            pltpu.VMEM((2,) + split, bf16),
+            pltpu.VMEM((2,) + split, bf16),
+            pltpu.VMEM((3, n_fsdp) + split[2:], bf16),
+            pltpu.VMEM((n_fsdp,) + split[2:], bf16),
+            pltpu.VMEM((3,) + split[2:], bf16),
+            pltpu.VMEM((part_attn, width), bf16),
             pltpu.VMEM((n_rows, width), bf16),
             pltpu.VMEM((8, 8, width), f32),
             pltpu.VMEM((n_fsdp, 8, width), f32),
@@ -1901,6 +1984,7 @@
         sum_out,
         dh_other,
         plane_sum,
+        last_grads,
         dh_own,
         dx_mid,
         tokens,
@@ -2020,7 +2104,7 @@
         dy_all = lax.all_gather(cotangent, plane, axis=0, tiled=True)
         pack = pack_small(router, gain_attn, gain_ffn, buckets, rel_table, routes, span)
 
-    q, k, v, o, lse, x_mid, message, probs, h_all, *gathered = attention_forward(
+    q, k, v, o, p, x_mid, message, probs, h_all, *gathered = attention_forward(
         place,
         x_all,
         weights,
@@ -2060,7 +2144,6 @@
         out_rows = (x_mid + out_sum.astype(f32)).astype(bf16)
 
     grads = attention_backward(
-        place,
         back,
         cotangent,
         x_mid,
@@ -2073,16 +2156,18 @@
         k,
         v,
         o,
-        lse,
+        p,
         n_experts,
         head_dim,
         BackgroundBack(n_fsdp) if near else None,
         behind,
     )
     if near:
-        dh_own, dh_other, dx_mid, dgain_two, drouter, ddist, out_rows, sum_in, plane_sum = grads
+        dh_own, dh_other, dx_mid, dgain_two, drouter, ddist = grads[:6]
+        out_rows, sum_in, plane_sum, last_grads = grads[6:]
         attn_sum, grad_in, grad_out, grad_tokens, small = finish(
             plane_sum,
+            last_grads,
             sum_in.reshape(n_seq, part_in, n_fsdp * part_out),
             sum_out,
             dh_other,

time: 300 us -> 290 us (0.967)
  Pallas kernels: 298 us -> 287 us
    pallas_call x2, Pallas kernels: 106 us -> 99.4 us  [the longest x1 54.2 us: experts_down(): pl.pallas_call(functools.partial(experts_down_kernel, n_experts, hidden /...]
    pallas_call x1, Pallas kernels: 64.6 us -> 59.1 us  [attention_backward(): pl.pallas_call(functools.partial(backward_kernel, background, n_experts,...]
    pallas_call x1, Pallas kernels: 41.7 us -> 45.5 us  [finish(): pl.pallas_call(functools.partial(finish_kernel, n_fsdp, n_experts, n_head...]
where the time goes in v5:
time: 290 us
  Pallas kernels  287 us (99%)
    pallas_call x1, Pallas kernels, attention_backward(): pl.pallas_call(functools.partial(backward_kernel, background, n_experts,...  59.1 us
    pallas_call x1, Pallas kernels, experts_down(): pl.pallas_call(functools.partial(experts_down_kernel, n_experts, hidden /...  54.2 us
    pallas_call x1, Pallas kernels, finish(): pl.pallas_call(functools.partial(finish_kernel, n_fsdp, n_experts, n_head...  45.5 us
    pallas_call x1, Pallas kernels, experts_up(): pl.pallas_call(functools.partial(experts_up_kernel, n_experts, hidden //...  45.3 us
    pallas_call x1, Pallas kernels, gather(): pl.pallas_call(functools.partial(gather_kernel, n_fsdp, part_out), out_sh...  42 us
    pallas_call x1, Pallas kernels, attention_forward(): pl.pallas_call(functools.partial(forward_kernel, background, n_experts, h...  34.3 us
    pallas_call x1, Pallas kernels, widen(): pl.pallas_call(functools.partial(widen_kernel, n_experts, n_heads, n_buck...  7.08 us

profile of v5, /device:TPU:0, one launch (start us, length us, event | category | flops | bytes accessed | tf_op | source)
XLA Modules:
  0.0 289.8 jit_solution(3250787312197251250)
XLA Ops:
  0.6 42.0 %gather_weights.1 = (bf16[4,4,2,96,768]{4,3,2,1,0:T(8,128)(2,1)}, bf16[2,384,768]{2,1,0:T(8,128)(2,1)}, bf16[4,192,1536]{2,1,0:T(8,128)(2,1)}, f32[32,1536]{1,0:T(8,128)}) custom-call(bf16[96,768]{1,0:T(8,128)(2,1)} %attn_q.1, bf16[96,768]{1,0:T(8,128)(2,1)} %attn_k.1, bf16[96,768]{1,0:T(8,128)(2,1)} %attn_v.1, bf16[96,768]{1,0:T(8,128)(2,1)} %attn_o.1, ...), custom_call_target="tpu_custom_call" | custom-call | tf_op jit(solution)/shard_map/gather_weights/pallas_call | solution.py:345
  42.7 34.3 %attention_forward.1 = (bf16[384,768]{1,0:T(8,128)(2,1)}, bf16[768,768]{1,0:T(8,128)(2,1)}, bf16[768,768]{1,0:T(8,128)(2,1)}, bf16[384,768]{1,0:T(8,128)(2,1)}, ...) custom-call(s32[2]{0:T(128)} %bitcast.30, ...), custom_call_target="tpu_custom_call", output_to_operand_aliasing={{10}: (8, {})} | custom-call | flops 20000000000 | bytes 20000000 | tf_op jit(solution)/shard_map/attention_forward/pallas_call | solution.py:601
  77.0 45.3 %experts_up.1 = (bf16[8,384,896]{2,1,0:T(8,128)(2,1)}, bf16[8,384,1536]{2,1,0:T(8,128)(2,1)}, bf16[8,384,1536]{2,1,0:T(8,128)(2,1)}, bf16[1536,768]{1,0:T(8,128)(2,1)}, bf16[4,384,768]{2,1,0:T(8,128)(2,1)}) custom-call(bf16[384,896]{1,0:T(8,128)(2,1)} %get-tuple-element.65.message_ref, bf16[8,384,768]{2,1,0:T(8,128)(2,1)} %get-tuple-element.66.dy_ref, ...), custom_call_target="tpu_custom_call" | custom-call | flops 20000000000 | bytes 30000000 | tf_op jit(solution)/shard_map/experts_up/pallas_call | solution.py:912
  122.3 54.2 %experts_down.1 = (f32[384,896]{1,0:T(8,128)}, bf16[8,192,768]{2,1,0:T(8,128)(2,1)}, bf16[768,1536]{1,0:T(8,128)(2,1)}, bf16[384,768]{1,0:T(8,128)(2,1)}) custom-call(bf16[8,384,896]{2,1,0:T(8,128)(2,1)} %get-tuple-element.68.message_ref, bf16[8,384,768]{2,1,0:T(8,128)(2,1)} %get-tuple-element.66.dy_ref, bf16[8,384,1536]{2,1,0:T(8,128)(2,1)} %get-tuple-element.69.act_ref, ...), custom_call_target="tpu_custom_call" | custom-call | flops 40000000000 | bytes 40000000 | tf_op jit(solution)/shard_map/experts_down/pallas_call | solution.py:1172
  176.4 59.1 %attention_backward.1 = (f32[384,768]{1,0:T(8,128)}, bf16[384,768]{1,0:T(8,128)(2,1)}, f32[384,768]{1,0:T(8,128)}, f32[1,768]{1,0:T(1,128)}, f32[128,768]{1,0:T(...) custom-call(f32[384,896]{1,0:T(8,128)} %get-tuple-element.73.back_re, ...), custom_call_target="tpu_custom_call" | custom-call | flops 40000000000 | bytes 30000000 | tf_op jit(solution)/shard_map/attention_backward/pallas_call | solution.py:1664
  235.5 45.5 %finish_gradients.1 = (bf16[4,96,768]{2,1,0:T(8,128)(2,1)}, bf16[4,96,3072]{2,1,0:T(8,128)(2,1)}, bf16[4,384,768]{2,1,0:T(8,128)(2,1)}, bf16[384,768]{1,0:T(8,128)(2,1)}, f32[8,768]{1,0:T(8,128)}) custom-call(bf16[2,96,1536]{2,1,0:T(8,128)(2,1)} %bitcast.13, bf16[384,768]{1,0:T(8,128)(2,1)} %get-tuple-element.86.sum_out, ...), custom_call_target="tpu_custom_call" | custom-call | tf_op jit(solution)/shard_map/finish_gradients/pallas_call | solution.py:1950
  281.0 0.0 copy-start
  281.0 0.0 copy-start.1
  281.0 7.1 %widen.1 = (f32[96,768]{1,0:T(8,128)}, f32[96,768]{1,0:T(8,128)}, f32[96,768]{1,0:T(8,128)}, f32[96,768]{1,0:T(8,128)}, f32[4,96,3072]{2,1,0:T(8,128)}, /*index=...) custom-call(bf16[4,96,768]{2,1,0:T(8,128)(2,1)} %get-tuple-element.96.attn, ...), custom_call_target="tpu_custom_call" | custom-call | tf_op jit(solution)/shard_map/widen/pallas_call | solution.py:2031
  288.1 0.0 copy-done
  288.1 0.8 copy.31
  288.9 0.0 copy-done.1
  288.9 0.8 copy.32
Async XLA Ops:
  281.0 7.1 %copy-start = (bf16[384,768]{1,0:T(8,128)(2,1)S(1)}, bf16[384,768]{1,0:T(8,128)(2,1)}, u32[]{:S(2)}) copy-start(bf16[384,768]{1,0:T(8,128)(2,1)} %get-tuple-element.122) | copy-start | bytes 1769476
  281.0 7.9 %copy-start.1 = (bf16[384,768]{1,0:T(8,128)(2,1)S(1)}, bf16[384,768]{1,0:T(8,128)(2,1)}, u32[]{:S(2)}) copy-start(bf16[384,768]{1,0:T(8,128)(2,1)} %get-tuple-element.123) | copy-start | bytes 1769476

commit v6 on v5

--- a/solution.py
+++ b/solution.py
@@ -1307,9 +1307,9 @@
         half, width = out_half.shape[1:]
         pairs = width // LANES - 1
         return [
-            pltpu.VMEM((4, 2, half, width), bf16),
+            pltpu.VMEM((3, 2, half, width), bf16),
             pltpu.SemaphoreType.DMA((8,)),
-            pltpu.SemaphoreType.DMA((4, 2)),
+            pltpu.SemaphoreType.DMA((3, 2)),
             pltpu.VMEM((2, 4) + self.split(width), bf16),
             pltpu.VMEM((pairs, 2) + self.split(width), bf16),
             pltpu.VMEM((pairs, 2) + self.split(width), bf16),
@@ -1318,6 +1318,10 @@
             pltpu.SemaphoreType.DMA((pairs, 2)),
             pltpu.SemaphoreType.DMA((pairs, 3)),
             pltpu.SemaphoreType.DMA((pairs, 3)),
+            pltpu.VMEM((2, half, width), bf16),
+            pltpu.VMEM((2, half, width), bf16),
+            pltpu.SemaphoreType.DMA((2,)),
+            pltpu.SemaphoreType.DMA((2,)),
         ] + LineSum.scratch(*dw_in.shape[1:])
 
     def split(self, width):
@@ -1391,25 +1395,42 @@
         out_half, dw_in = ins
         out_rows, sum_in, plane_sum, _ = outs
         land, send, recv = scratch[:3]
-        near, mid, far, mine, line_send, line_recv, line_local = scratch[11:]
+        relay, hop, relay_recv, hop_sem = scratch[11:15]
+        near, mid, far, mine, line_send, line_recv, line_local = scratch[15:]
         me = Place(self.n_fsdp)
         core = me.core
         half = out_half.shape[1]
         line = LineSum(me, dw_in, near, mid, far, mine, line_send, line_recv, line_local)
 
-        def to_owner(j):
-            q, k = plane_slot(j)
+        across, beside = (lambda k: me.chip(1, 0, k)), (lambda k: me.chip(0, 1, k))
+        plan = {
+            "mate": (out_half.at[7 * core], land.at[0, core], me.mate(), recv.at[0, core]),
+            "direct0": (out_half.at[3], land.at[2, core], across(0), recv.at[2, core]),
+            "direct1": (out_half.at[2], land.at[1, core], beside(1), recv.at[1, core]),
+            "hop0": (out_half.at[5], relay.at[0], across(core), relay_recv.at[0]),
+            "hop1": (out_half.at[6], relay.at[1], beside(core), relay_recv.at[1]),
+            "sum0": (hop.at[0], land.at[1, core], beside(0), recv.at[1, core]),
+            "sum1": (hop.at[1], land.at[2, core], across(1), recv.at[2, core]),
+        }
+
+        def result(name):
+            source, target, device, arrival = plan[name]
             return pltpu.make_async_remote_copy(
-                src_ref=out_half.at[j],
-                dst_ref=land.at[q, core],
-                send_sem=send.at[j],
-                recv_sem=recv.at[q, core],
-                device_id=me.chip(q // 2, q % 2, k),
+                src_ref=source,
+                dst_ref=target,
+                send_sem=send.at[list(plan).index(name)],
+                recv_sem=arrival,
+                device_id=device,
                 device_id_type=MESH,
             )
 
-        def stay(j):
-            return pltpu.make_async_copy(out_half.at[j], land.at[0, core], send.at[j])
+        def own_parts():
+            yield pltpu.make_async_copy(out_half.at[1], hop.at[0], hop_sem.at[0])
+            yield pltpu.make_async_copy(out_half.at[4], hop.at[1], hop_sem.at[1])
+
+        stay = lambda: pltpu.make_async_copy(
+            out_half.at[7 * (1 - core)], land.at[0, core], send.at[7]
+        )
 
         if before:
 
@@ -1421,23 +1442,24 @@
                         partners.append(me.chip(q // 2, q % 2, (core + k) % 2))
                 meet(partners)
                 line.start()
-                for j in range(8):
-                    if j in (0, 7):
-
-                        @pl.when(core == (j + 1) % 2)
-                        def _():
-                            stay(j).start()
-
-                        @pl.when(core != (j + 1) % 2)
-                        def _():
-                            to_owner(j).start()
-
-                    else:
-                        to_owner(j).start()
+                for name in ("hop0", "hop1", "direct0", "direct1", "mate"):
+                    result(name).start()
+                stay().start()
+                for part in own_parts():
+                    part.start()
 
             @pl.when(step == 2)
             def _():
                 line.turn()
+
+            @pl.when(step == 3)
+            def _():
+                for part in own_parts():
+                    part.wait()
+                for k in (0, 1):
+                    result(f"hop{k}").wait_recv()
+                    hop[k] = (hop[k].astype(f32) + relay[k].astype(f32)).astype(bf16)
+                    result(f"sum{k}").start()
 
             return
 
@@ -1446,23 +1468,13 @@
             added, landed = scratch[5:7]
             pairs = landed.shape[0]
             sum_in[...] = line.total()
-            for j in range(8):
-                if j in (0, 7):
-
-                    @pl.when(core == (j + 1) % 2)
-                    def _():
-                        stay(j).wait()
-
-                    @pl.when(core != (j + 1) % 2)
-                    def _():
-                        to_owner(j).wait_send()
-
-                else:
-                    to_owner(j).wait_send()
+            for name in plan:
+                result(name).wait_send()
+            stay().wait()
             for side in range(2):
                 here = slice(side * half, (side + 1) * half)
                 total = x_mid[here, :]
-                for q in range(4):
+                for q in range(3):
                     arrived = pltpu.make_async_remote_copy(
                         src_ref=out_half.at[0],
                         dst_ref=land.at[q, side],
@@ -1514,6 +1526,7 @@
     v_ref,
     o_ref,
     p_ref,
+    x_ref,
     *refs,
 ):
     step = pl.program_id(0)
@@ -1522,7 +1535,8 @@
     n_grads = 0 if background else 4
     grad_outs, refs = refs[:n_grads], refs[n_grads:]
     dh_own_out, dh_other_out, dx_mid_out, gain_out, router_out, ddist_out = refs[:6]
-    behind_out, refs = refs[6 : 6 + n_out], refs[6 + n_out :]
+    gain_one_out, refs = refs[6], refs[7:]
+    behind_out, refs = refs[:n_out], refs[n_out:]
     da_ref, dh_all_ref, dh_mine_ref, dbias_ref, dq_ref, h_turned_ref, o_turned_ref = refs[:7]
     if background:
         background.run(step, True, behind_in, behind_out, refs[7:], x_mid_ref)
@@ -1623,6 +1637,14 @@
         other = pl.ds(pl.multiple_of(length - rows - first_row(rows), rows), rows)
         dh_own_out[...] = dh_mine_ref[...] + dh_all_ref[own, :]
         dh_other_out[...] = dh_all_ref[other, :].astype(bf16)
+        for start in range(0, length, rows):
+            here = slice(start, start + rows)
+            values = x_ref[here, :].astype(f32)
+            part = jnp.sum(dh_all_ref[here, :] * (values * inverse_rms(values)), 0, keepdims=True)
+            gain_one_out[...] = part if start == 0 else gain_one_out[...] + part
+        values = x_ref[own, :].astype(f32)
+        scaled = values * inverse_rms(values)
+        gain_one_out[...] += jnp.sum(dh_mine_ref[...] * scaled, 0, keepdims=True)
 
     if background:
         background.run(step, False, behind_in, behind_out, refs[7:], x_mid_ref)
@@ -1642,6 +1664,7 @@
     v,
     o,
     p,
+    x_all,
     n_experts,
     head_dim,
     background=None,
@@ -1671,6 +1694,7 @@
             jax.ShapeDtypeStruct((1, width), f32),
             jax.ShapeDtypeStruct((LANES, width), f32),
             jax.ShapeDtypeStruct((16, span), f32),
+            jax.ShapeDtypeStruct((1, width), f32),
         ]
         + more_shapes,
         grid_spec=pltpu.PrefetchScalarGridSpec(
@@ -1693,6 +1717,7 @@
                 columns(length),
                 whole((n_rows, width)),
                 pl.BlockSpec((None, 2, n_rows, length), lambda p, *_: (p, 0, 0, 0)),
+                whole((length, width)),
             ]
             + [anywhere] * len(behind),
             out_specs=[columns(width)] * n_grads
@@ -1703,6 +1728,7 @@
                 whole((1, width)),
                 whole((LANES, width)),
                 whole((16, span)),
+                whole((1, width)),
             ]
             + (background.out_specs(more_shapes) if background else []),
             scratch_shapes=[
@@ -1738,6 +1764,7 @@
         v,
         o,
         p,
+        x_all,
         *behind,
     )
 
@@ -1755,6 +1782,7 @@
     dx_mid_ref,
     tokens_ref,
     pack_ref,
+    dgain_one_ref,
     dgain_two_ref,
     drouter_ref,
     ddist_ref,
@@ -1853,11 +1881,14 @@
     table = exact_dot_t(ddist_ref[...], bucket_match(pack_ref))
     small = small_plane.at[here]
     small[...] = jnp.zeros_like(small_out)
+    small[0:1, :] = dgain_one_ref[...]
     small[1:2, :] = dgain_two_ref[...]
     small[2 : 2 + n_experts, :] = drouter_ref[:n_experts, :]
     for head in range(n_heads):
         at = head % 6 * LANES
         small[6 + head // 6, at : at + LANES] = table[head]
+    for i in range(len(peers)):
+        copies["small", i].start()
     for copy in kept:
         copy.wait()
     for z in range(n_fsdp):
@@ -1871,6 +1902,14 @@
     last_line[...] = total.astype(bf16)
     for i in range(3):
         copies["last_z", i].start()
+    for i in range(len(peers)):
+        copies["small", i].wait_recv()
+    total = small_plane[0]
+    for i in range(1, 8):
+        total = total + small_plane[i]
+    small_line[line] = total
+    for i in range(3):
+        copies["small_z", i].start()
     total = line_ref[line].astype(f32)
     for i in range(3):
         copies["line", i].wait_recv()
@@ -1879,13 +1918,6 @@
     attn_held[:, :early] = total.astype(bf16)
     copies["out_y"].wait_recv()
     copies["out_f"].start()
-    copies["dh"].wait_recv()
-    dh_one = dh_own_ref[...] + dh_land[...].astype(f32)
-    gain_one = pack_ref[4:5, :width]
-    dx, dgain_one = norm_back(tokens_ref[...].astype(f32), gain_one, dh_one)
-    small[0:1, :] = dgain_one
-    for i in range(len(peers)):
-        copies["small", i].start()
     total = last_line[line].astype(f32)
     for i in range(3):
         copies["last_z", i].wait_recv()
@@ -1895,25 +1927,20 @@
     copies["attn_c"].start()
     own_attn = pltpu.make_async_copy(attn_held, attn_out.at[rep], local.at[3])
     own_attn.start()
+    copies["dh"].wait_recv()
+    dh_one = dh_own_ref[...] + dh_land[...].astype(f32)
+    dx, _ = norm_back(tokens_ref[...].astype(f32), pack_ref[4:5, :width], dh_one)
     tokens_out[...] = (dx_mid_ref[...] + dx).astype(bf16)
-    copies["attn_y"].wait_recv()
-    copies["attn_f"].start()
-    for i in range(len(peers)):
-        copies["small", i].wait_recv()
-    total = small_plane[0]
-    for i in range(1, 8):
-        total = total + small_plane[i]
-    small_line[line] = total
-    for i in range(3):
-        copies["small_z", i].start()
-    copies["in_y"].wait_recv()
-    copies["in_f"].start()
     for i in range(3):
         copies["small_z", i].wait_recv()
     total = small_line[0]
     for i in range(1, n_fsdp):
         total = total + small_line[i]
     small_out[...] = total
+    copies["in_y"].wait_recv()
+    copies["in_f"].start()
+    copies["attn_y"].wait_recv()
+    copies["attn_f"].start()
     own_attn.wait()
     own_out.wait()
     for name in ("attn_c", "attn_f", "in_c", "in_f", "out_c", "out_f"):
@@ -1932,6 +1959,7 @@
     dx_mid,
     tokens,
     pack,
+    dgain_one,
     dgain_two,
     drouter,
     ddist,
@@ -1956,7 +1984,7 @@
             jax.ShapeDtypeStruct((n_rows, width), bf16),
             jax.ShapeDtypeStruct((8, width), f32),
         ],
-        in_specs=[anywhere] * 3 + [inside] * 9,
+        in_specs=[anywhere] * 3 + [inside] * 10,
         out_specs=[anywhere] * 3 + [inside] * 2,
         scratch_shapes=[
             pltpu.VMEM((3,) + plane_sum.shape[1:], bf16),
@@ -1989,6 +2017,7 @@
         dx_mid,
         tokens,
         pack,
+        dgain_one,
         dgain_two,
         drouter,
         ddist,
@@ -2157,14 +2186,15 @@
         v,
         o,
         p,
+        x_all,
         n_experts,
         head_dim,
         BackgroundBack(n_fsdp) if near else None,
         behind,
     )
     if near:
-        dh_own, dh_other, dx_mid, dgain_two, drouter, ddist = grads[:6]
-        out_rows, sum_in, plane_sum, last_grads = grads[6:]
+        dh_own, dh_other, dx_mid, dgain_two, drouter, ddist, dgain_one = grads[:7]
+        out_rows, sum_in, plane_sum, last_grads = grads[7:]
         attn_sum, grad_in, grad_out, grad_tokens, small = finish(
             plane_sum,
             last_grads,
@@ -2175,6 +2205,7 @@
             dx_mid,
             tokens,
             pack,
+            dgain_one,
             dgain_two,
             drouter,
             ddist,
@@ -2195,7 +2226,7 @@
             grad_table.T,
             grad_router.T,
         )
-    dwq, dwk, dwv, dwo, dh_own, dh_other, dx_mid, dgain_two, drouter, ddist = grads
+    dwq, dwk, dwv, dwo, dh_own, dh_other, dx_mid, dgain_two, drouter, ddist, dgain_one = grads
     sum_out = lax.psum_scatter(dw_out, "fsdp", scatter_dimension=0, tiled=True)
     sum_in = lax.psum_scatter(dw_in, "fsdp", scatter_dimension=0, tiled=True)
     sum_in = sum_in.reshape(n_seq, part_in, n_fsdp * part_out)
@@ -2206,7 +2237,7 @@
     grad_in = lax.all_gather(sum_in, "rep", axis=0, tiled=False)
     swap = [(0, 1), (1, 0)]
     dh_one = dh_own + lax.ppermute(dh_other, "seq", swap).astype(f32)
-    dx, dgain_one = norm_back(tokens.astype(f32), gain_attn[None, :], dh_one)
+    dx, _ = norm_back(tokens.astype(f32), gain_attn[None, :], dh_one)
     grad_tokens = (dx_mid + dx).astype(bf16)
     attn_grads = jnp.stack([dwq, dwk, dwv, dwo])
     attn_grads = attn_grads.reshape(n_rep, n_fsdp, n_seq, part_attn, width)

time: 290 us -> 282 us (0.972)
  Pallas kernels: 287 us -> 279 us
    pallas_call x1, Pallas kernels: 59.1 us -> 53.1 us  [attention_backward(): pl.pallas_call(functools.partial(backward_kernel, background, n_experts,...]
where the time goes in v6:
time: 282 us
  Pallas kernels  279 us (99%)
    pallas_call x1, Pallas kernels, experts_down(): pl.pallas_call(functools.partial(experts_down_kernel, n_experts, hidden /...  54.1 us
    pallas_call x1, Pallas kernels, attention_backward(): pl.pallas_call(functools.partial(backward_kernel, background, n_experts,...  53.1 us
    pallas_call x1, Pallas kernels, experts_up(): pl.pallas_call(functools.partial(experts_up_kernel, n_experts, hidden //...  45.3 us
    pallas_call x1, Pallas kernels, finish(): pl.pallas_call(functools.partial(finish_kernel, n_fsdp, n_experts, n_head...  43.5 us
    pallas_call x1, Pallas kernels, gather(): pl.pallas_call(functools.partial(gather_kernel, n_fsdp, part_out), out_sh...  42 us
    pallas_call x1, Pallas kernels, attention_forward(): pl.pallas_call(functools.partial(forward_kernel, background, n_experts, h...  34.2 us
    pallas_call x1, Pallas kernels, widen(): pl.pallas_call(functools.partial(widen_kernel, n_experts, n_heads, n_buck...  7.08 us

profile of v6, /device:TPU:0, one launch (start us, length us, event | category | flops | bytes accessed | tf_op | source)
XLA Modules:
  0.0 281.7 jit_solution(6512404627485525923)
XLA Ops:
  0.6 42.0 %gather_weights.1 = (bf16[4,4,2,96,768]{4,3,2,1,0:T(8,128)(2,1)}, bf16[2,384,768]{2,1,0:T(8,128)(2,1)}, bf16[4,192,1536]{2,1,0:T(8,128)(2,1)}, f32[32,1536]{1,0:T(8,128)}) custom-call(bf16[96,768]{1,0:T(8,128)(2,1)} %attn_q.1, bf16[96,768]{1,0:T(8,128)(2,1)} %attn_k.1, bf16[96,768]{1,0:T(8,128)(2,1)} %attn_v.1, bf16[96,768]{1,0:T(8,128)(2,1)} %attn_o.1, ...), custom_call_target="tpu_custom_call" | custom-call | tf_op jit(solution)/shard_map/gather_weights/pallas_call | solution.py:345
  42.7 34.2 %attention_forward.1 = (bf16[384,768]{1,0:T(8,128)(2,1)}, bf16[768,768]{1,0:T(8,128)(2,1)}, bf16[768,768]{1,0:T(8,128)(2,1)}, bf16[384,768]{1,0:T(8,128)(2,1)}, ...) custom-call(s32[2]{0:T(128)} %bitcast.31, ...), custom_call_target="tpu_custom_call", output_to_operand_aliasing={{10}: (8, {})} | custom-call | flops 20000000000 | bytes 20000000 | tf_op jit(solution)/shard_map/attention_forward/pallas_call | solution.py:601
  76.9 45.3 %experts_up.1 = (bf16[8,384,896]{2,1,0:T(8,128)(2,1)}, bf16[8,384,1536]{2,1,0:T(8,128)(2,1)}, bf16[8,384,1536]{2,1,0:T(8,128)(2,1)}, bf16[1536,768]{1,0:T(8,128)(2,1)}, bf16[4,384,768]{2,1,0:T(8,128)(2,1)}) custom-call(bf16[384,896]{1,0:T(8,128)(2,1)} %get-tuple-element.66.message_ref, bf16[8,384,768]{2,1,0:T(8,128)(2,1)} %get-tuple-element.67.dy_ref, ...), custom_call_target="tpu_custom_call" | custom-call | flops 20000000000 | bytes 30000000 | tf_op jit(solution)/shard_map/experts_up/pallas_call | solution.py:912
  122.2 54.1 %experts_down.1 = (f32[384,896]{1,0:T(8,128)}, bf16[8,192,768]{2,1,0:T(8,128)(2,1)}, bf16[768,1536]{1,0:T(8,128)(2,1)}, bf16[384,768]{1,0:T(8,128)(2,1)}) custom-call(bf16[8,384,896]{2,1,0:T(8,128)(2,1)} %get-tuple-element.69.message_ref, bf16[8,384,768]{2,1,0:T(8,128)(2,1)} %get-tuple-element.67.dy_ref, bf16[8,384,1536]{2,1,0:T(8,128)(2,1)} %get-tuple-element.70.act_ref, ...), custom_call_target="tpu_custom_call" | custom-call | flops 40000000000 | bytes 40000000 | tf_op jit(solution)/shard_map/experts_down/pallas_call | solution.py:1172
  176.3 53.1 %attention_backward.1 = (f32[384,768]{1,0:T(8,128)}, bf16[384,768]{1,0:T(8,128)(2,1)}, f32[384,768]{1,0:T(8,128)}, f32[1,768]{1,0:T(1,128)}, f32[128,768]{1,0:T(...) custom-call(f32[384,896]{1,0:T(8,128)} %get-tuple-element.74.back_re, ...), custom_call_target="tpu_custom_call" | custom-call | flops 40000000000 | bytes 30000000 | tf_op jit(solution)/shard_map/attention_backward/pallas_call | solution.py:1687
  229.4 43.5 %finish_gradients.1 = (bf16[4,96,768]{2,1,0:T(8,128)(2,1)}, bf16[4,96,3072]{2,1,0:T(8,128)(2,1)}, bf16[4,384,768]{2,1,0:T(8,128)(2,1)}, bf16[384,768]{1,0:T(8,128)(2,1)}, f32[8,768]{1,0:T(8,128)}) custom-call(bf16[2,96,1536]{2,1,0:T(8,128)(2,1)} %bitcast.13, bf16[384,768]{1,0:T(8,128)(2,1)} %get-tuple-element.87.sum_out, ...), custom_call_target="tpu_custom_call" | custom-call | tf_op jit(solution)/shard_map/finish_gradients/pallas_call | solution.py:1978
  273.0 0.0 copy-start
  273.0 0.0 copy-start.1
  273.0 7.1 %widen.1 = (f32[96,768]{1,0:T(8,128)}, f32[96,768]{1,0:T(8,128)}, f32[96,768]{1,0:T(8,128)}, f32[96,768]{1,0:T(8,128)}, f32[4,96,3072]{2,1,0:T(8,128)}, /*index=...) custom-call(bf16[4,96,768]{2,1,0:T(8,128)(2,1)} %get-tuple-element.98.attn, ...), custom_call_target="tpu_custom_call" | custom-call | tf_op jit(solution)/shard_map/widen/pallas_call | solution.py:2060
  280.1 0.0 copy-done
  280.1 0.8 copy.31
  280.9 0.0 copy-done.1
  280.9 0.8 copy.32
Async XLA Ops:
  273.0 7.1 %copy-start = (bf16[384,768]{1,0:T(8,128)(2,1)S(1)}, bf16[384,768]{1,0:T(8,128)(2,1)}, u32[]{:S(2)}) copy-start(bf16[384,768]{1,0:T(8,128)(2,1)} %get-tuple-element.124) | copy-start | bytes 1769476
  273.0 7.9 %copy-start.1 = (bf16[384,768]{1,0:T(8,128)(2,1)S(1)}, bf16[384,768]{1,0:T(8,128)(2,1)}, u32[]{:S(2)}) copy-start(bf16[384,768]{1,0:T(8,128)(2,1)} %get-tuple-element.125) | copy-start | bytes 1769476

commit v7 on v6

--- a/solution.py
+++ b/solution.py
@@ -213,6 +213,7 @@
     attn_o,
     tokens,
     expert_in,
+    expert_out,
     router,
     gain_attn,
     gain_ffn,
@@ -222,6 +223,7 @@
     weights,
     x_all,
     w_in,
+    w_out,
     pack,
     attn_held,
     tokens_held,
@@ -311,6 +313,8 @@
     for i, shift in enumerate((1, -1)):
         half = w_in.at[line, pl.ds(i * part_in, part_in)]
         in_copies.append(start(wires.copy(("line", shift), half, half, me.along(shift))))
+    plan = line_plan(me, expert_out.at[rep], w_out)
+    in_copies.append(start(wires.copy("out", *plan["first", 1])))
     token_copy = start(wires.copy("tokens", tokens, x_all.at[seq], beside))
     for shift in shifts:
         z = at[shift]
@@ -336,22 +340,24 @@
         copy.wait_send()
 
 
-def gather(attn, tokens, expert_in, part_out, n_fsdp, small, span):
+def gather(attn, tokens, expert_in, expert_out, n_fsdp, small, span):
     part_attn, width = attn[0].shape
     n_rows = tokens.shape[0]
     n_experts, part_in, hidden = expert_in.shape
+    part_out = expert_out.shape[1]
     anywhere = pl.BlockSpec(memory_space=pl.ANY)
     inside = pl.BlockSpec(memory_space=pltpu.VMEM)
-    weights, x_all, w_in, pack = pl.pallas_call(
+    weights, x_all, w_in, w_out, pack = pl.pallas_call(
         functools.partial(gather_kernel, n_fsdp, part_out),
         out_shape=[
             jax.ShapeDtypeStruct((4, n_fsdp, 2, part_attn, width), bf16),
             jax.ShapeDtypeStruct((2, n_rows, width), bf16),
             jax.ShapeDtypeStruct((n_fsdp, 2 * part_in, n_fsdp * part_out), bf16),
+            jax.ShapeDtypeStruct((n_fsdp,) + expert_out.shape[1:], bf16),
             jax.ShapeDtypeStruct((32, span), f32),
         ],
-        in_specs=[anywhere] * 6 + [inside] * 6,
-        out_specs=[anywhere] * 3 + [inside],
+        in_specs=[anywhere] * 7 + [inside] * 6,
+        out_specs=[anywhere] * 4 + [inside],
         scratch_shapes=[
             pltpu.VMEM((part_attn, width), bf16),
             pltpu.VMEM((n_rows, width), bf16),
@@ -362,11 +368,12 @@
         ],
         compiler_params=pltpu.CompilerParams(collective_id=0, has_side_effects=True),
         name="gather_weights",
-    )(*attn, tokens, expert_in, *small)
+    )(*attn, tokens, expert_in, expert_out, *small)
     return (
         weights.reshape(4, n_fsdp * 2 * part_attn, width),
         x_all.reshape(2 * n_rows, width),
         w_in,
+        w_out,
         pack,
     )
 
@@ -428,18 +435,18 @@
         half = dy.shape[0] // 2
         first, second = pl.ds(0, half), pl.ds(half, half)
         core = me.core
-        own = 7 * (1 - core)
+        own = 6 + core
         mate, across, beside = me.mate(), me.chip(1, 0), me.chip(0, 1)
         slot = dy_all.at
         plan = {
-            "x": (dy, slot[1 + core], beside),
-            "y": (dy, slot[3 + core], across),
+            "x": (dy, slot[core], beside),
+            "y": (dy, slot[2 + core], across),
             "c0": (dy, slot[own], mate),
-            "c1": (slot[1 + core], slot[1 + core], mate),
-            "c2": (slot[3 + core], slot[3 + core], mate),
-            "c3": (slot[5 + core], slot[5 + core], mate),
-            "xy": (slot[1 + core, first], slot[5 + core, first], across),
-            "yx": (slot[3 + core, second], slot[5 + core, second], beside),
+            "c1": (slot[core], slot[core], mate),
+            "c2": (slot[2 + core], slot[2 + core], mate),
+            "c3": (slot[4 + core], slot[4 + core], mate),
+            "xy": (slot[core, first], slot[4 + core, first], across),
+            "yx": (slot[2 + core, second], slot[4 + core, second], beside),
         }
         line = line_plan(me, w_in.at[me.line], w_in)
         plan |= {name: line[name] for name in line if name[0] != "first"}
@@ -765,12 +772,18 @@
 
 
 def plane_slot(j):
-    return (j + 1) // 2 % 4, (j + 1) % 2
+    return (j // 2 + 1) % 4, j % 2
 
 
 def down_order(step):
     inner = (13 - step) // 8
-    return inner * ((step + 4) % 6 + 1) + (1 - inner) * (step - 6) * 7
+    return inner * ((step + 4) % 6) + (1 - inner) * step
+
+
+def up_order(step):
+    other, corner = (step + 6) // 8, (step + 2) // 8
+    pair = 3 * (1 - other) + (other - corner) * (step % 2) + 2 * corner
+    return pair, (step % 2 + step // 4 - corner) % 2
 
 
 def experts_up_kernel(
@@ -781,6 +794,7 @@
     dy_ref,
     w_in,
     expert_out,
+    _,
     h_out,
     act_out,
     slope_out,
@@ -800,23 +814,27 @@
     last = pl.num_programs(0) - 1
     me = Place(n_fsdp)
     core = me.core
-    rows, width = dy_ref.shape
+    half, width = dy_ref.shape[1:]
+    rows = 2 * half
     hidden = w_in_ref.shape[1]
-    half = rows // 2
-    first, second = pl.ds(0, half), pl.ds(half, half)
     mate, across, beside = me.mate(), me.chip(1, 0), me.chip(0, 1)
-    own = 7 * (1 - core)
-    slot = h_ref.at
+    block = h_ref.at
     plan = {
-        "x": (message_ref, slot[1 + core], beside),
-        "y": (message_ref, slot[3 + core], across),
-        "c0": (message_ref, slot[own], mate),
-        "c1": (slot[1 + core], slot[1 + core], mate),
-        "c2": (slot[3 + core], slot[3 + core], mate),
-        "c3": (slot[5 + core], slot[5 + core], mate),
-        "xy": (slot[1 + core, first], slot[5 + core, first], across),
-        "yx": (slot[3 + core, second], slot[5 + core, second], beside),
-    } | line_plan(me, expert_out.at[me.rep], w_out)
+        "x0": (message_ref.at[0], block[0, core, 0], beside),
+        "x1": (message_ref.at[1], block[0, core, 1], beside),
+        "y0": (message_ref.at[0], block[1, core, 0], across),
+        "y1": (message_ref.at[1], block[1, core, 1], across),
+        "xy": (block[0, core, 0], block[2, core, 0], across),
+        "yx": (block[1, core, 1], block[2, core, 1], beside),
+        ("c", 3, 0): (message_ref.at[0], block[3, core, 0], mate),
+        ("c", 3, 1): (message_ref.at[1], block[3, core, 1], mate),
+    }
+    for pair in range(3):
+        for side in range(2):
+            piece = block[pair, core, side]
+            plan["c", pair, side] = (piece, piece, mate)
+    plan |= line_plan(me, expert_out.at[me.rep], w_out)
+    del plan["first", 1]
     copies = Planned(plan, send, recv)
     own_out = Bounce(expert_out.at[me.rep], out_held, w_out.at[me.line], local.at[pl.ds(0, 2)])
 
@@ -825,53 +843,62 @@
         load = pltpu.make_async_copy(w_in, w_in_ref, local.at[2])
         load.start()
         meet([mate, across, beside, me.along(1), me.along(-1)])
-        for name in ("c0", "x", "y", ("first", 1), ("first", -1)):
+        for name in (("c", 3, 0), ("c", 3, 1), "x0", "y1", ("relay", 1), ("first", -1)):
             copies[name].start()
         own_out.start()
-        h_ref[own] = message_ref[...]
+        h_ref[3, core] = message_ref[...]
         dw_out_acc[...] = jnp.zeros_like(dw_out_acc)
         load.wait()
 
     @pl.when(step == 1)
     def _():
         own_out.turn()
-        for shift in (1, -1):
-            copies["rest", shift].start()
+        for name in ("x1", "y0", ("rest", 1), ("rest", -1)):
+            copies[name].start()
 
     @pl.when(step == 2)
     def _():
-        for shift in (1, -1):
-            copies["first", shift].wait_recv()
-            copies["relay", shift].start()
-        copies["x"].wait_recv()
-        copies["c1"].start()
+        copies["x0"].wait_recv()
+        copies["c", 0, 0].start()
         copies["xy"].start()
-        copies["y"].wait_recv()
-        copies["c2"].start()
+        copies["y1"].wait_recv()
+        copies["c", 1, 1].start()
         copies["yx"].start()
-
-    @pl.when(step == 6)
+        copies["first", -1].wait_recv()
+        copies["relay", -1].start()
+
+    @pl.when(step == 3)
+    def _():
+        copies["x1"].wait_recv()
+        copies["c", 0, 1].start()
+        copies["y0"].wait_recv()
+        copies["c", 1, 0].start()
+
+    @pl.when(step == 5)
     def _():
         copies["xy"].wait_recv()
+        copies["c", 2, 0].start()
         copies["yx"].wait_recv()
-        copies["c3"].start()
-
-    for q in range(4):
-
-        @pl.when(step == 2 * q + 1 - core)
+        copies["c", 2, 1].start()
+
+    for turn in range(8):
+
+        @pl.when(step == turn)
         def _():
-            copies[f"c{q}"].wait_recv()
-
-    now = (step + 7) % 8
+            copies[("c",) + up_order(turn)].wait_recv()
+
+    pair, side = up_order(step)
+    message = h_ref[pair, :, side]
     expert = me.rep
-    h_out[...] = h_ref[now]
-    h = h_ref[now, :, :width]
-    extra = h_ref[now, :, width:].astype(f32)
+    h_out[...] = message
+    message = message.reshape(rows, message.shape[2])
+    h = message[:, :width]
+    extra = message[:, width:].astype(f32)
     lane = lax.broadcasted_iota(jnp.int32, extra.shape, 1)
     mine = (lane == expert) | (lane == expert + n_experts)
     gate = jnp.sum(jnp.where(mine, extra, 0.0), -1, keepdims=True)
     place = pl.ds(pl.multiple_of(step % 2 * rows, rows), rows)
-    dy_pair_ref[place, :] = dy_ref[...]
+    dy_pair_ref[place, :] = dy_ref[...].reshape(rows, width)
     for start in range(0, hidden, chunk):
         piece = slice(start, start + chunk)
         up = dot(h, w_in_ref[:, piece])
@@ -881,8 +908,8 @@
         more = 1.0 + tanh
         act = (halved * more).astype(bf16)
         slope = 0.5 * more + halved * (1.0 - tanh * tanh) * (GELU_A + 3.0 * GELU_B * square)
-        act_out[:, piece] = act
-        slope_out[:, piece] = slope.astype(bf16)
+        act_out[:, :, piece] = act.reshape(2, half, chunk)
+        slope_out[:, :, piece] = slope.astype(bf16).reshape(2, half, chunk)
         gated_ref[place, piece] = (gate * act.astype(f32)).astype(bf16)
 
     @pl.when(step % 2 == 1)
@@ -900,38 +927,48 @@
             copies[name].wait_send()
 
 
-def experts_up(message, dy_all, w_in, expert_out, n_experts, n_fsdp):
+def experts_up(message, dy_all, w_in, expert_out, w_out, n_experts, n_fsdp):
     blocks, rows, width = dy_all.shape
     long = message.shape[1]
     hidden = w_in.shape[1]
     once = pl.Buffered(1)
     whole = lambda shape: pl.BlockSpec(shape, lambda i: (0,) * len(shape), pipeline_mode=once)
-    turn = lambda columns: pl.BlockSpec((None, rows, columns), lambda i: ((i + 7) % 8, 0, 0))
+    half = rows // 2
+
+    def turn(columns):
+        def index(i):
+            pair, side = up_order(i)
+            return pair, 0, side, 0, 0
+
+        return pl.BlockSpec((None, 2, None, half, columns), index)
+
+    halves = lambda columns: (blocks // 2, 2, 2, half, columns)
     anywhere = pl.BlockSpec(memory_space=pl.ANY)
     dma = lambda *shape: pltpu.SemaphoreType.DMA(shape)
-    return pl.pallas_call(
+    message_all, act, slope, dw_out, w_out = pl.pallas_call(
         functools.partial(experts_up_kernel, n_experts, hidden // 2, n_fsdp),
         out_shape=[
-            jax.ShapeDtypeStruct((blocks, rows, long), bf16),
-            jax.ShapeDtypeStruct((blocks, rows, hidden), bf16),
-            jax.ShapeDtypeStruct((blocks, rows, hidden), bf16),
+            jax.ShapeDtypeStruct(halves(long), bf16),
+            jax.ShapeDtypeStruct(halves(hidden), bf16),
+            jax.ShapeDtypeStruct(halves(hidden), bf16),
             jax.ShapeDtypeStruct((hidden, width), bf16),
             jax.ShapeDtypeStruct((n_fsdp,) + expert_out.shape[1:], bf16),
         ],
         grid=(blocks,),
-        in_specs=[whole((rows, long)), turn(width), anywhere, anywhere],
+        in_specs=[whole((2, half, long)), turn(width), anywhere, anywhere, anywhere],
         out_specs=[turn(long), turn(hidden), turn(hidden), whole((hidden, width)), anywhere],
         scratch_shapes=[
-            pltpu.VMEM((blocks, rows, long), bf16),
+            pltpu.VMEM(halves(long), bf16),
             pltpu.VMEM((hidden, width), f32),
             pltpu.VMEM((width, hidden), bf16),
             pltpu.VMEM((2 * rows, hidden), bf16),
             pltpu.VMEM((2 * rows, width), bf16),
             pltpu.VMEM(expert_out.shape[1:], bf16),
-            dma(16),
-            dma(16),
+            dma(24),
+            dma(24),
             dma(3),
         ],
+        input_output_aliases={4: 4},
         compiler_params=pltpu.CompilerParams(
             vmem_limit_bytes=VMEM_LIMIT, collective_id=2, has_side_effects=True
         ),
@@ -939,7 +976,9 @@
             flops=20_000_000_000, transcendentals=0, bytes_accessed=30_000_000
         ),
         name="experts_up",
-    )(message, dy_all, w_in, expert_out)
+    )(message.reshape(2, half, long), dy_all.reshape(halves(width)), w_in, expert_out, w_out)
+    whole_blocks = lambda array: array.reshape(blocks, rows, array.shape[4])
+    return whole_blocks(message_all), whole_blocks(act), whole_blocks(slope), dw_out, w_out
 
 
 def experts_down_kernel(
@@ -1404,11 +1443,11 @@
 
         across, beside = (lambda k: me.chip(1, 0, k)), (lambda k: me.chip(0, 1, k))
         plan = {
-            "mate": (out_half.at[7 * core], land.at[0, core], me.mate(), recv.at[0, core]),
-            "direct0": (out_half.at[3], land.at[2, core], across(0), recv.at[2, core]),
-            "direct1": (out_half.at[2], land.at[1, core], beside(1), recv.at[1, core]),
-            "hop0": (out_half.at[5], relay.at[0], across(core), relay_recv.at[0]),
-            "hop1": (out_half.at[6], relay.at[1], beside(core), relay_recv.at[1]),
+            "mate": (out_half.at[7 - core], land.at[0, core], me.mate(), recv.at[0, core]),
+            "direct0": (out_half.at[2], land.at[2, core], across(0), recv.at[2, core]),
+            "direct1": (out_half.at[1], land.at[1, core], beside(1), recv.at[1, core]),
+            "hop0": (out_half.at[4], relay.at[0], across(core), relay_recv.at[0]),
+            "hop1": (out_half.at[5], relay.at[1], beside(core), relay_recv.at[1]),
             "sum0": (hop.at[0], land.at[1, core], beside(0), recv.at[1, core]),
             "sum1": (hop.at[1], land.at[2, core], across(1), recv.at[2, core]),
         }
@@ -1425,11 +1464,11 @@
             )
 
         def own_parts():
-            yield pltpu.make_async_copy(out_half.at[1], hop.at[0], hop_sem.at[0])
-            yield pltpu.make_async_copy(out_half.at[4], hop.at[1], hop_sem.at[1])
+            yield pltpu.make_async_copy(out_half.at[0], hop.at[0], hop_sem.at[0])
+            yield pltpu.make_async_copy(out_half.at[3], hop.at[1], hop_sem.at[1])
 
         stay = lambda: pltpu.make_async_copy(
-            out_half.at[7 * (1 - core)], land.at[0, core], send.at[7]
+            out_half.at[6 + core], land.at[0, core], send.at[7]
         )
 
         if before:
@@ -1858,7 +1897,6 @@
     for z in range(n_fsdp):
         copies["in_x", z].start()
     copies["out_y"].start()
-    copies["dh"].start()
     copies["out_c"].start()
     own_in = pltpu.make_async_copy(sum_in.at[seq], in_held, local.at[2])
     own_in.start()
@@ -1894,6 +1932,7 @@
     for z in range(n_fsdp):
         copies["in_x", z].wait_recv()
     copies["in_y"].start()
+    copies["dh"].start()
     copies["in_c"].start()
     total = last_added[row, :, seq].astype(f32)
     for i in range(3):
@@ -2025,9 +2064,28 @@
 
 
 def widen_kernel(
-    n_experts, n_heads, n_buckets, attn, grad_in, grad_out, small, q, k, v, o, win, wout, *rest
+    n_experts,
+    n_heads,
+    n_buckets,
+    out_rows,
+    tokens,
+    attn,
+    grad_in,
+    grad_out,
+    small,
+    out_rows_copy,
+    tokens_copy,
+    q,
+    k,
+    v,
+    o,
+    win,
+    wout,
+    *rest,
 ):
     step = pl.program_id(0)
+    out_rows_copy[...] = out_rows[...]
+    tokens_copy[...] = tokens[...]
     for i, target in enumerate((q, k, v, o)):
 
         @pl.when(step == i)
@@ -2050,8 +2108,9 @@
             ]
 
 
-def widen(attn, grad_in, grad_out, small, n_heads, n_buckets):
+def widen(out_rows, tokens, attn, grad_in, grad_out, small, n_heads, n_buckets):
     n_experts = grad_in.shape[0]
+    rows = pl.BlockSpec((tokens.shape[0] // n_experts, tokens.shape[1]), lambda i: (i, 0))
     width = small.shape[1]
     own = lambda a: pl.BlockSpec((None,) + a.shape[1:], lambda i: (i, 0, 0))
     whole = lambda shape: pl.BlockSpec(shape, lambda i: (0,) * len(shape))
@@ -2059,17 +2118,19 @@
     wide = [attn.shape[1:]] * 4
     return pl.pallas_call(
         functools.partial(widen_kernel, n_experts, n_heads, n_buckets),
-        out_shape=[jax.ShapeDtypeStruct(shape, f32) for shape in wide]
+        out_shape=[jax.ShapeDtypeStruct(tokens.shape, bf16)] * 2
+        + [jax.ShapeDtypeStruct(shape, f32) for shape in wide]
         + [jax.ShapeDtypeStruct(a.shape, f32) for a in (grad_in, grad_out)]
         + [jax.ShapeDtypeStruct(shape, f32) for shape in small_shapes],
         grid=(n_experts,),
-        in_specs=[own(attn), own(grad_in), own(grad_out), whole(small.shape)],
-        out_specs=[whole(shape) for shape in wide]
+        in_specs=[rows, rows, own(attn), own(grad_in), own(grad_out), whole(small.shape)],
+        out_specs=[rows, rows]
+        + [whole(shape) for shape in wide]
         + [own(grad_in), own(grad_out)]
         + [whole(shape) for shape in small_shapes],
         compiler_params=pltpu.CompilerParams(vmem_limit_bytes=VMEM_LIMIT),
         name="widen",
-    )(attn, grad_in, grad_out, small)
+    )(out_rows, tokens, attn, grad_in, grad_out, small)
 
 
 def per_device(
@@ -2108,11 +2169,11 @@
     pick = lambda array: lax.dynamic_index_in_dim(array, rep, 0, keepdims=False)
     span = -(-buckets.shape[0] // LANES) * LANES
     if near:
-        weights, x_all, w_in, pack = gather(
+        weights, x_all, w_in, w_out, pack = gather(
             (attn_q, attn_k, attn_v, attn_o),
             tokens,
             expert_in,
-            part_out,
+            expert_out,
             n_fsdp,
             (router.T, gain_attn, gain_ffn, buckets, rel_table.T, routes.T),
             span,
@@ -2149,7 +2210,7 @@
         dy_all, w_in = gathered
         w_in = w_in.reshape(width, n_fsdp * part_out)
         message_all, act, slope, dw_out, w_out = experts_up(
-            message, dy_all, w_in, expert_out, n_experts, n_fsdp
+            message, dy_all, w_in, expert_out, w_out, n_experts, n_fsdp
         )
         back, out_half, dw_in, sum_out = experts_down(
             message_all,
@@ -2214,8 +2275,8 @@
             n_heads,
             hidden,
         )
-        *wide, grad_one, grad_two, grad_table, grad_router = widen(
-            attn_sum, grad_in, grad_out, small, n_heads, n_buckets
+        out_rows, grad_tokens, *wide, grad_one, grad_two, grad_table, grad_router = widen(
+            out_rows, grad_tokens, attn_sum, grad_in, grad_out, small, n_heads, n_buckets
         )
         return (
             out_rows,

time: 282 us -> 280 us (level)
  no operation moved by 1% of the time
where the time goes in v7:
time: 280 us; the launch traced here: 279 us
  Pallas kernels  279 us (100%)
    pallas_call x1, Pallas kernels, attention_backward(): pl.pallas_call(functools.partial(backward_kernel, background, n_experts,...  53.2 us
    pallas_call x1, Pallas kernels, experts_down(): pl.pallas_call(functools.partial(experts_down_kernel, n_experts, hidden /...  52.7 us
    pallas_call x1, Pallas kernels, finish(): pl.pallas_call(functools.partial(finish_kernel, n_fsdp, n_experts, n_head...  44.7 us
    pallas_call x1, Pallas kernels, gather(): pl.pallas_call(functools.partial(gather_kernel, n_fsdp, part_out), out_sh...  43.6 us
    pallas_call x1, Pallas kernels, experts_up(): pl.pallas_call(functools.partial(experts_up_kernel, n_experts, hidden //...  43.2 us
    pallas_call x1, Pallas kernels, attention_forward(): pl.pallas_call(functools.partial(forward_kernel, background, n_experts, h...  33.4 us
    pallas_call x1, Pallas kernels, widen(): pl.pallas_call(functools.partial(widen_kernel, n_experts, n_heads, n_buck...  7.67 us

profile of v7, /device:TPU:0, one launch (start us, length us, event | category | flops | bytes accessed | tf_op | source)
XLA Modules:
  0.0 279.4 jit_solution(5171050537913164114)
XLA Ops:
  0.6 43.6 %gather_weights.1 = (bf16[4,4,2,96,768]{4,3,2,1,0:T(8,128)(2,1)}, bf16[2,384,768]{2,1,0:T(8,128)(2,1)}, bf16[4,192,1536]{2,1,0:T(8,128)(2,1)}, bf16[4,384,768]{2,1,0:T(8,128)(2,1)}, f32[32,1536]{1,0:T(8,128)}) custom-call(bf16[96,768]{1,0:T(8,128)(2,1)} %attn_q.1, bf16[96,768]{1,0:T(8,128)(2,1)} %attn_k.1, bf16[96,768]{1,0:T(8,128)(2,1)} %attn_v.1, ...), custom_call_target="tpu_custom_call" | custom-call | tf_op jit(solution)/shard_map/gather_weights/pallas_call | solution.py:350
  44.3 33.4 %attention_forward.1 = (bf16[384,768]{1,0:T(8,128)(2,1)}, bf16[768,768]{1,0:T(8,128)(2,1)}, bf16[768,768]{1,0:T(8,128)(2,1)}, bf16[384,768]{1,0:T(8,128)(2,1)}, ...) custom-call(s32[2]{0:T(128)} %bitcast.37, ...), custom_call_target="tpu_custom_call", output_to_operand_aliasing={{10}: (8, {})} | custom-call | flops 20000000000 | bytes 20000000 | tf_op jit(solution)/shard_map/attention_forward/pallas_call | solution.py:608
  77.7 43.2 %experts_up.1 = (bf16[4,2,2,192,896]{4,3,2,1,0:T(8,128)(2,1)}, bf16[4,2,2,192,1536]{4,3,2,1,0:T(8,128)(2,1)}, bf16[4,2,2,192,1536]{4,3,2,1,0:T(8,128)(2,1)}, bf1...) custom-call(bf16[2,192,896]{2,1,0:T(8,128)(2,1)} %bitcast.44, ...), custom_call_target="tpu_custom_call", output_to_operand_aliasing={{4}: (4, {})} | custom-call | flops 20000000000 | bytes 30000000 | tf_op jit(solution)/shard_map/experts_up/pallas_call | solution.py:948
  121.0 52.7 %experts_down.1 = (f32[384,896]{1,0:T(8,128)}, bf16[8,192,768]{2,1,0:T(8,128)(2,1)}, bf16[768,1536]{1,0:T(8,128)(2,1)}, bf16[384,768]{1,0:T(8,128)(2,1)}) custom-call(bf16[8,384,896]{2,1,0:T(8,128)(2,1)} %bitcast.40, bf16[8,384,768]{2,1,0:T(8,128)(2,1)} %get-tuple-element.70.dy_ref, bf16[8,384,1536]{2,1,0:T(8,128)(2,1)} %bitcast.38, ...), custom_call_target="tpu_custom_call" | custom-call | flops 40000000000 | bytes 40000000 | tf_op jit(solution)/shard_map/experts_down/pallas_call | solution.py:1211
  173.6 53.2 %attention_backward.1 = (f32[384,768]{1,0:T(8,128)}, bf16[384,768]{1,0:T(8,128)(2,1)}, f32[384,768]{1,0:T(8,128)}, f32[1,768]{1,0:T(1,128)}, f32[128,768]{1,0:T(...) custom-call(f32[384,896]{1,0:T(8,128)} %get-tuple-element.78.back_re, ...), custom_call_target="tpu_custom_call" | custom-call | flops 40000000000 | bytes 30000000 | tf_op jit(solution)/shard_map/attention_backward/pallas_call | solution.py:1726
  226.8 44.7 %finish_gradients.1 = (bf16[4,96,768]{2,1,0:T(8,128)(2,1)}, bf16[4,96,3072]{2,1,0:T(8,128)(2,1)}, bf16[4,384,768]{2,1,0:T(8,128)(2,1)}, bf16[384,768]{1,0:T(8,128)(2,1)}, f32[8,768]{1,0:T(8,128)}) custom-call(bf16[2,96,1536]{2,1,0:T(8,128)(2,1)} %bitcast.18, bf16[384,768]{1,0:T(8,128)(2,1)} %get-tuple-element.91.sum_out, ...), custom_call_target="tpu_custom_call" | custom-call | tf_op jit(solution)/shard_map/finish_gradients/pallas_call | solution.py:2017
  271.6 7.7 %widen.1 = (bf16[384,768]{1,0:T(8,128)(2,1)}, bf16[384,768]{1,0:T(8,128)(2,1)}, f32[96,768]{1,0:T(8,128)}, f32[96,768]{1,0:T(8,128)}, f32[96,768]{1,0:T(8,128)},...) custom-call(bf16[384,768]{1,0:T(8,128)(2,1)} %get-tuple-element.89.o, ...), custom_call_target="tpu_custom_call" | custom-call | tf_op jit(solution)/shard_map/widen/pallas_call | solution.py:2119

commit v8 on v7

--- a/solution.py
+++ b/solution.py
@@ -1549,13 +1549,13 @@
     background,
     n_experts,
     head_dim,
-    back_ref,
-    dy_ref,
-    x_mid_ref,
+    back,
+    dy,
+    x_mid,
     message_ref,
     probs_ref,
     pack_ref,
-    h_ref,
+    h_all,
     wq_ref,
     wk_ref,
     wv_ref,
@@ -1565,7 +1565,7 @@
     v_ref,
     o_ref,
     p_ref,
-    x_ref,
+    x_all,
     *refs,
 ):
     step = pl.program_id(0)
@@ -1577,14 +1577,25 @@
     gain_one_out, refs = refs[6], refs[7:]
     behind_out, refs = refs[:n_out], refs[n_out:]
     da_ref, dh_all_ref, dh_mine_ref, dbias_ref, dq_ref, h_turned_ref, o_turned_ref = refs[:7]
-    if background:
-        background.run(step, True, behind_in, behind_out, refs[7:], x_mid_ref)
-    rows, width = x_mid_ref.shape
-    length = h_ref.shape[0]
-    own = pl.ds(pl.multiple_of(first_row(rows), rows), rows)
+    back_ref, dy_ref, x_mid_ref, h_ref, x_ref, load_sem = refs[7:13]
+    held = ((back, back_ref), (dy, dy_ref), (x_mid, x_mid_ref), (h_all, h_ref), (x_all, x_ref))
+    load = lambda i: pltpu.make_async_copy(*held[i], load_sem.at[i])
 
     @pl.when(step == 0)
     def _():
+        for i in range(5):
+            load(i).start()
+
+    if background:
+        background.run(step, True, behind_in, behind_out, refs[13:], x_mid_ref)
+    rows, width = x_mid.shape
+    length = h_all.shape[0]
+    own = pl.ds(pl.multiple_of(first_row(rows), rows), rows)
+
+    @pl.when(step == 0)
+    def _():
+        for i in range(4):
+            load(i).wait()
         probs = probs_ref[...]
         chosen = chosen_experts(pack_ref, probs.shape)
         picked = jnp.where(chosen, probs, 0.0)
@@ -1654,7 +1665,7 @@
     dkv = jnp.concatenate([dk, dv], 1).astype(bf16)
     da_columns = da_ref[:, pl.ds(pl.multiple_of(step * LANES, LANES), LANES)]
     if background:
-        background.collect_before(step, refs[7:])
+        background.collect_before(step, refs[13:])
     mine = pl.ds(pl.multiple_of(first_row(rows), rows), rows)
     grads_kv = dot(h_turned_ref[...], dkv).astype(bf16)
     grads = [
@@ -1664,7 +1675,7 @@
         dot(o_turned_ref[...], da_columns).astype(bf16),
     ]
     if background:
-        background.give(step, grads, refs[7:], behind_out[3])
+        background.give(step, grads, refs[13:], behind_out[3])
     else:
         for target, grad in zip(grad_outs, grads):
             target[...] = grad
@@ -1676,6 +1687,7 @@
         other = pl.ds(pl.multiple_of(length - rows - first_row(rows), rows), rows)
         dh_own_out[...] = dh_mine_ref[...] + dh_all_ref[own, :]
         dh_other_out[...] = dh_all_ref[other, :].astype(bf16)
+        load(4).wait()
         for start in range(0, length, rows):
             here = slice(start, start + rows)
             values = x_ref[here, :].astype(f32)
@@ -1686,7 +1698,7 @@
         gain_one_out[...] += jnp.sum(dh_mine_ref[...] * scaled, 0, keepdims=True)
 
     if background:
-        background.run(step, False, behind_in, behind_out, refs[7:], x_mid_ref)
+        background.run(step, False, behind_in, behind_out, refs[13:], x_mid_ref)
 
 
 def attention_backward(
@@ -1740,13 +1752,13 @@
             num_scalar_prefetch=0,
             grid=(pairs,),
             in_specs=[
-                whole((n_rows, width + LANES)),
-                whole((n_rows, width)),
-                whole((n_rows, width)),
+                anywhere,
+                anywhere,
+                anywhere,
                 whole((n_rows, width + LANES)),
                 whole((n_rows, LANES)),
                 whole(pack.shape),
-                whole((length, width)),
+                anywhere,
                 matrix(0),
                 matrix(1),
                 matrix(2),
@@ -1756,7 +1768,7 @@
                 columns(length),
                 whole((n_rows, width)),
                 pl.BlockSpec((None, 2, n_rows, length), lambda p, *_: (p, 0, 0, 0)),
-                whole((length, width)),
+                anywhere,
             ]
             + [anywhere] * len(behind),
             out_specs=[columns(width)] * n_grads
@@ -1778,6 +1790,12 @@
                 pltpu.VMEM((n_rows, LANES), bf16),
                 pltpu.VMEM((width, length), bf16),
                 pltpu.VMEM((width, n_rows), bf16),
+                pltpu.VMEM(back.shape, back.dtype),
+                pltpu.VMEM((n_rows, width), bf16),
+                pltpu.VMEM((n_rows, width), f32),
+                pltpu.VMEM((length, width), bf16),
+                pltpu.VMEM((length, width), bf16),
+                pltpu.SemaphoreType.DMA((5,)),
             ]
             + more_scratch,
         ),
@@ -1817,9 +1835,9 @@
     dh_other,
     line_ref,
     last_ref,
-    dh_own_ref,
-    dx_mid_ref,
-    tokens_ref,
+    dh_own,
+    dx_mid,
+    tokens,
     pack_ref,
     dgain_one_ref,
     dgain_two_ref,
@@ -1842,6 +1860,9 @@
     small_line,
     in_held,
     out_held,
+    dh_own_ref,
+    dx_mid_ref,
+    tokens_ref,
     send,
     recv,
     local,
@@ -1889,6 +1910,10 @@
     for i, (to_row, to_column, chip) in enumerate(chips):
         plan["last", i] = (last_added.at[to_row, :, to_column], last_land.at[i], chip)
     copies = Planned(plan, send, recv)
+    held = ((dh_own, dh_own_ref), (dx_mid, dx_mid_ref), (tokens, tokens_ref))
+    loads = [pltpu.make_async_copy(*held[i], local.at[10 + i]) for i in range(3)]
+    for load in loads:
+        load.start()
     meet(peers + [me.along(shift) for shift in shifts])
     for i in (0, 1):
         copies["last_c", i].start()
@@ -1967,6 +1992,8 @@
     own_attn = pltpu.make_async_copy(attn_held, attn_out.at[rep], local.at[3])
     own_attn.start()
     copies["dh"].wait_recv()
+    for load in loads:
+        load.wait()
     dh_one = dh_own_ref[...] + dh_land[...].astype(f32)
     dx, _ = norm_back(tokens_ref[...].astype(f32), pack_ref[4:5, :width], dh_one)
     tokens_out[...] = (dx_mid_ref[...] + dx).astype(bf16)
@@ -2023,7 +2050,7 @@
             jax.ShapeDtypeStruct((n_rows, width), bf16),
             jax.ShapeDtypeStruct((8, width), f32),
         ],
-        in_specs=[anywhere] * 3 + [inside] * 10,
+        in_specs=[anywhere] * 3 + [inside] * 2 + [anywhere] * 3 + [inside] * 5,
         out_specs=[anywhere] * 3 + [inside] * 2,
         scratch_shapes=[
             pltpu.VMEM((3,) + plane_sum.shape[1:], bf16),
@@ -2038,9 +2065,12 @@
             pltpu.VMEM((n_fsdp, 8, width), f32),
             pltpu.VMEM(sum_in.shape[1:], bf16),
             pltpu.VMEM(sum_out.shape, bf16),
+            pltpu.VMEM((n_rows, width), f32),
+            pltpu.VMEM((n_rows, width), f32),
+            pltpu.VMEM((n_rows, width), bf16),
             dma(40),
             dma(40),
-            dma(12),
+            dma(14),
         ],
         compiler_params=pltpu.CompilerParams(
             vmem_limit_bytes=VMEM_LIMIT, collective_id=5, has_side_effects=True

time: 280 us -> 277 us (0.989)
  Pallas kernels: 279 us -> 276 us
where the time goes in v8:
time: 277 us
  Pallas kernels  276 us (100%)
    pallas_call x1, Pallas kernels, experts_down(): pl.pallas_call(functools.partial(experts_down_kernel, n_experts, hidden /...  52.7 us
    pallas_call x1, Pallas kernels, attention_backward(): pl.pallas_call(functools.partial(backward_kernel, background, n_experts,...  51.6 us
    pallas_call x1, Pallas kernels, finish(): pl.pallas_call(functools.partial(finish_kernel, n_fsdp, n_experts, n_head...  43.8 us
    pallas_call x1, Pallas kernels, gather(): pl.pallas_call(functools.partial(gather_kernel, n_fsdp, part_out), out_sh...  43.6 us
    pallas_call x1, Pallas kernels, experts_up(): pl.pallas_call(functools.partial(experts_up_kernel, n_experts, hidden //...  43.2 us
    pallas_call x1, Pallas kernels, attention_forward(): pl.pallas_call(functools.partial(forward_kernel, background, n_experts, h...  33.4 us
    pallas_call x1, Pallas kernels, widen(): pl.pallas_call(functools.partial(widen_kernel, n_experts, n_heads, n_buck...  7.67 us

profile of v8, /device:TPU:0, one launch (start us, length us, event | category | flops | bytes accessed | tf_op | source)
XLA Modules:
  0.0 276.9 jit_solution(12564838745705839635)
XLA Ops:
  0.6 43.6 %gather_weights.1 = (bf16[4,4,2,96,768]{4,3,2,1,0:T(8,128)(2,1)}, bf16[2,384,768]{2,1,0:T(8,128)(2,1)}, bf16[4,192,1536]{2,1,0:T(8,128)(2,1)}, bf16[4,384,768]{2,1,0:T(8,128)(2,1)}, f32[32,1536]{1,0:T(8,128)}) custom-call(bf16[96,768]{1,0:T(8,128)(2,1)} %attn_q.1, bf16[96,768]{1,0:T(8,128)(2,1)} %attn_k.1, bf16[96,768]{1,0:T(8,128)(2,1)} %attn_v.1, ...), custom_call_target="tpu_custom_call" | custom-call | tf_op jit(solution)/shard_map/gather_weights/pallas_call | solution.py:350
  44.3 33.4 %attention_forward.1 = (bf16[384,768]{1,0:T(8,128)(2,1)}, bf16[768,768]{1,0:T(8,128)(2,1)}, bf16[768,768]{1,0:T(8,128)(2,1)}, bf16[384,768]{1,0:T(8,128)(2,1)}, ...) custom-call(s32[2]{0:T(128)} %bitcast.37, ...), custom_call_target="tpu_custom_call", output_to_operand_aliasing={{10}: (8, {})} | custom-call | flops 20000000000 | bytes 20000000 | tf_op jit(solution)/shard_map/attention_forward/pallas_call | solution.py:608
  77.7 43.2 %experts_up.1 = (bf16[4,2,2,192,896]{4,3,2,1,0:T(8,128)(2,1)}, bf16[4,2,2,192,1536]{4,3,2,1,0:T(8,128)(2,1)}, bf16[4,2,2,192,1536]{4,3,2,1,0:T(8,128)(2,1)}, bf1...) custom-call(bf16[2,192,896]{2,1,0:T(8,128)(2,1)} %bitcast.44, ...), custom_call_target="tpu_custom_call", output_to_operand_aliasing={{4}: (4, {})} | custom-call | flops 20000000000 | bytes 30000000 | tf_op jit(solution)/shard_map/experts_up/pallas_call | solution.py:948
  121.0 52.7 %experts_down.1 = (f32[384,896]{1,0:T(8,128)}, bf16[8,192,768]{2,1,0:T(8,128)(2,1)}, bf16[768,1536]{1,0:T(8,128)(2,1)}, bf16[384,768]{1,0:T(8,128)(2,1)}) custom-call(bf16[8,384,896]{2,1,0:T(8,128)(2,1)} %bitcast.40, bf16[8,384,768]{2,1,0:T(8,128)(2,1)} %get-tuple-element.70.dy_ref, bf16[8,384,1536]{2,1,0:T(8,128)(2,1)} %bitcast.38, ...), custom_call_target="tpu_custom_call" | custom-call | flops 40000000000 | bytes 40000000 | tf_op jit(solution)/shard_map/experts_down/pallas_call | solution.py:1211
  173.6 51.6 %attention_backward.1 = (f32[384,768]{1,0:T(8,128)}, bf16[384,768]{1,0:T(8,128)(2,1)}, f32[384,768]{1,0:T(8,128)}, f32[1,768]{1,0:T(1,128)}, f32[128,768]{1,0:T(...) custom-call(f32[384,896]{1,0:T(8,128)} %get-tuple-element.78.back, ...), custom_call_target="tpu_custom_call" | custom-call | flops 40000000000 | bytes 30000000 | tf_op jit(solution)/shard_map/attention_backward/pallas_call | solution.py:1738
  225.2 43.8 %finish_gradients.1 = (bf16[4,96,768]{2,1,0:T(8,128)(2,1)}, bf16[4,96,3072]{2,1,0:T(8,128)(2,1)}, bf16[4,384,768]{2,1,0:T(8,128)(2,1)}, bf16[384,768]{1,0:T(8,128)(2,1)}, f32[8,768]{1,0:T(8,128)}) custom-call(bf16[2,96,1536]{2,1,0:T(8,128)(2,1)} %bitcast.18, bf16[384,768]{1,0:T(8,128)(2,1)} %get-tuple-element.91.sum_out, ...), custom_call_target="tpu_custom_call" | custom-call | tf_op jit(solution)/shard_map/finish_gradients/pallas_call | solution.py:2044
  269.1 7.7 %widen.1 = (bf16[384,768]{1,0:T(8,128)(2,1)}, bf16[384,768]{1,0:T(8,128)(2,1)}, f32[96,768]{1,0:T(8,128)}, f32[96,768]{1,0:T(8,128)}, f32[96,768]{1,0:T(8,128)},...) custom-call(bf16[384,768]{1,0:T(8,128)(2,1)} %get-tuple-element.89.o, ...), custom_call_target="tpu_custom_call" | custom-call | tf_op jit(solution)/shard_map/widen/pallas_call | solution.py:2149
